TPU v7x, 32 devices: a whole 2x2x4 slice. The times are simulated.
32 devices in a mesh: space: 16 (over z, x, core), tensor: 2 (over y).
Axes of the slice: x: 2, y: 2, z: 4, core: 2. Of those that a mesh axis runs over, the one named last changes fastest.
Arguments:
- tokens: float32 [2, 128, 128, 2048], P(None, 'space', None, 'tensor'), may hold values from -6 to 6
- in_gain: float32 [2048], replicated, may hold values from 0.25 to 1.75
- w_inner: bfloat16 [2048, 3072], P(None, 'tensor'), may hold values from -0.125 to 0.125
- w_bc: bfloat16 [2048, 256], replicated, may hold values from -0.03125 to 0.03125
- w_step: bfloat16 [2048, 48], P(None, 'tensor'), may hold values from -0.125 to 0.125
- step_bias: float32 [48], P('tensor'), may hold values from -3 to 0
- decay_rate: float32 [48], P('tensor'), may hold values from 0.02 to 2
- skip: float32 [48], P('tensor'), may hold values from 0.5 to 2
- norm_gain: float32 [3072], P('tensor'), may hold values from 0.25 to 1.75
- w_out: bfloat16 [3072, 2048], P('tensor'), may hold values from -0.109375 to 0.109375
Outputs:
- mixed: bfloat16 [2, 128, 128, 2048], P(None, 'space', None, 'tensor')
All inputs are finite; a program needn't handle non-finite values.
Results may differ from a plain program's by a relative error of at most 0.011.
Values may be sent and summed in bfloat16 or wider, within the bound.
A program may use at most 128 MiB of HBM per device.

v0:
```python
import jax
import jax.numpy as jnp
from jax import lax
from jax.sharding import PartitionSpec as P

HEAD_DIM = 64
STATE = 128
NORM_HEADS = 6


EPS = 1e-05


def kernel(logdecay):
    running = jnp.cumsum(logdecay, axis=-1)
    length = logdecay.shape[-1]
    place = jnp.arange(length)
    lower = place[:, None] >= place[None, :]
    upper = place[:, None] <= place[None, :]
    later = running[..., :, None] - running[..., None, :]
    shifted = running - logdecay
    earlier = shifted[..., None, :] - shifted[..., :, None]
    forward = jnp.exp(jnp.where(lower, later, -jnp.inf))
    backward = jnp.exp(jnp.where(upper, earlier, -jnp.inf))
    return forward + backward


def scan_grid(values, maps, logdecay, along_rows):
    heads = logdecay.shape[-1]
    in_map = maps[..., :STATE]
    out_map = maps[..., STATE:]
    split_values = values.reshape(values.shape[:3] + (heads, HEAD_DIM))
    if along_rows:
        scores = jnp.einsum("ialn,iamn->ialm", out_map, in_map, preferred_element_type=jnp.float32)
        decays = jnp.moveaxis(logdecay.astype(jnp.float32), 3, 2)
    else:
        scores = jnp.einsum("ilan,iman->ialm", out_map, in_map, preferred_element_type=jnp.float32)
        decays = jnp.transpose(logdecay.astype(jnp.float32), (0, 2, 3, 1))
    weights = (scores[:, :, None] * kernel(decays)).astype(jnp.bfloat16)
    if along_rows:
        result = jnp.einsum(
            "iahlm,iamhp->ialhp", weights, split_values, preferred_element_type=jnp.float32
        )
    else:
        result = jnp.einsum(
            "iahlm,imahp->ilahp", weights, split_values, preferred_element_type=jnp.float32
        )
    return result.reshape(values.shape)


def on_device(
    tokens, in_gain, w_inner, w_bc, w_step, step_bias, decay_rate, skip, norm_gain, w_out
):
    whole = lax.all_gather(tokens.astype(jnp.bfloat16), "tensor", axis=3, tiled=True)
    rounded = whole.astype(jnp.float32)
    scale = lax.rsqrt(jnp.mean(rounded * rounded, axis=-1, keepdims=True) + EPS)
    normed = (rounded * scale * in_gain).astype(jnp.bfloat16)
    inner = jnp.einsum("irwd,dc->irwc", normed, w_inner, preferred_element_type=jnp.float32).astype(
        jnp.bfloat16
    )
    maps = jnp.einsum("irwd,dc->irwc", normed, w_bc, preferred_element_type=jnp.float32).astype(
        jnp.bfloat16
    )
    step = jax.nn.softplus(
        jnp.einsum("irwd,dc->irwc", normed, w_step, preferred_element_type=jnp.float32) + step_bias
    )
    logdecay = (-decay_rate * step).astype(jnp.bfloat16)
    heads_local = w_step.shape[1]
    lead = inner.shape[:3]
    value = (
        (inner.reshape(lead + (heads_local, HEAD_DIM)).astype(jnp.float32) * step[..., None])
        .reshape(inner.shape)
        .astype(jnp.bfloat16)
    )
    share = maps.shape[3] // lax.axis_size("tensor")
    maps_sent = lax.dynamic_slice_in_dim(maps, lax.axis_index("tensor") * share, share, 3)
    col_value = lax.all_to_all(value, "space", split_axis=2, concat_axis=1, tiled=True)
    col_maps = lax.all_to_all(maps_sent, "space", split_axis=2, concat_axis=1, tiled=True)
    col_decay = lax.all_to_all(logdecay, "space", split_axis=2, concat_axis=1, tiled=True)
    col_maps = lax.all_gather(col_maps, "tensor", axis=3, tiled=True)
    column_out = scan_grid(col_value, col_maps, col_decay, False).astype(jnp.bfloat16)
    column_back = lax.all_to_all(column_out, "space", split_axis=1, concat_axis=2, tiled=True)
    row_out = scan_grid(value, maps, logdecay, True)
    skip_wide = jnp.repeat(skip, HEAD_DIM)
    total = row_out + column_back.astype(jnp.float32) + skip_wide * inner.astype(jnp.float32)
    group = NORM_HEADS * HEAD_DIM
    grouped = total.reshape(lead + (inner.shape[3] // group, group))
    norm_scale = lax.rsqrt(jnp.mean(grouped * grouped, axis=-1, keepdims=True) + EPS)
    gated = ((grouped * norm_scale).reshape(inner.shape) * norm_gain).astype(jnp.bfloat16)
    partial_out = jnp.einsum("irwc,cd->irwd", gated, w_out, preferred_element_type=jnp.float32)
    mixer = lax.psum_scatter(partial_out, "tensor", scatter_dimension=3, tiled=True)
    return (tokens + mixer).astype(jnp.bfloat16)


def solution(mesh):
    return jax.shard_map(
        on_device,
        mesh=mesh,
        in_specs=(
            P(None, "space", None, "tensor"),
            P(),
            P(None, "tensor"),
            P(),
            P(None, "tensor"),
            P("tensor"),
            P("tensor"),
            P("tensor"),
            P("tensor"),
            P("tensor", None),
        ),
        out_specs=P(None, "space", None, "tensor"),
        check_vma=False,
    )
```

profile of v0, /device:TPU:0, one launch (start us, length us, event | category | flops | bytes accessed | tf_op | source)
XLA Modules:
  0.0 838.0 jit_solution(12779345311613857947)
XLA Ops:
  6.5 0.0 copy-start
  6.5 0.0 all-gather.3.cloned.1.call-start
  6.6 6.1 convert_element_type.76
  12.7 0.0 all-gather.3.cloned.1.call-update
  12.8 106.8 %all-gather.3.cloned.1.call-done = bf16[2,8,128,2048]{3,2,1,0:T(8,128)(2,1)} async-done(((bf16[2,8,128,1024]{3,2,1,0:T(8,128)(2,1)}), bf16[2,8,128,2048]{3,2,1,0:T(8,128)(2,1)}) %all-gather.3.cloned.1.call-update) | async-done | bytes 8388624 | tf_op jit(solution)/shard_map/all_gather | solution.py:54
  119.6 5.1 fusion
  124.8 4.9 multiply_convert_fusion.8
  129.6 0.4 copy.85
  130.1 1.3 reshape.70
  131.4 5.6 all-to-all-start.2
  137.0 0.0 copy-done
  137.0 6.0 fusion.40
  143.1 0.1 constant_dynamic-slice_fusion
  143.2 1.1 copy.81
  144.3 5.3 mul.102
  149.6 12.6 %copy.77 = f32[2,8,128,1536]{3,2,1,0:T(8,128)} copy(f32[2,8,128,1536]{2,3,1,0:T(8,128)} %bitcast.94) | data formatting | bytes 25165824 | tf_op jit(solution)/shard_map/mul | solution.py:71
  162.1 0.0 all-to-all-done.2
  162.1 6.5 all-to-all-start.1
  168.6 23.2 %fusion.5 = (bf16[2,8,128,1536]{3,2,1,0:T(8,128)(2,1)}, bf16[2,8,128,1536]{3,2,1,0:T(8,128)(2,1)}) fusion(f32[2,8,128,1536]{3,2,1,0:T(8,128)} %copy.77, bf16[2048,1536]{1,0:T(8,128)(2,1)} %param.12, bf16[2,8,128,2048]{3,2,1,0:T(8,128)(2,1)} %all-gather.3.cloned.1.call-done, f32[2048]{0:T(1024)S(1)} %copy-done.5, f32[2,8,128]{2,1,0:T(8,128)S(1)} %add_rsqrt_fusion.1), kind=kOutput, calls=%fused_computation.11 | convolution fusion | flops 12914262016 | bytes 39862272 | tf_op jit(solution)/shard_map/irwd,dc->irwc/dot_general | solution.py:58
  191.8 8.9 %copy.79 = bf16[2,8,128,1536]{3,1,0,2:T(8,128)(2,1)} copy(bf16[2,8,128,1536]{3,2,1,0:T(8,128)(2,1)} %get-tuple-element.8) | data formatting | bytes 12582912 | tf_op jit(solution)/shard_map/convert_element_type | solution.py:73
  200.6 0.0 all-to-all-done.1
  200.6 6.2 all-to-all-start
  206.8 0.2 all-gather.5.cloned.1.call-start
  207.0 0.1 copy.83
  207.2 0.9 copy.84
  208.1 0.0 all-gather.5.cloned.1.call-update
  208.1 0.7 reshape.71
  208.8 0.1 convert_bitcast_fusion.1
  208.9 0.1 copy.87
  209.1 0.3 copy.88
  209.4 4.6 reduce_window_sum.18
  214.0 16.7 %all-gather.5.cloned.1.call-done = bf16[2,128,8,256]{3,1,2,0:T(8,128)(2,1)} async-done(((bf16[2,128,8,128]{3,1,2,0:T(8,128)(2,1)}), bf16[2,128,8,256]{3,1,2,0:T(8,128)(2,1)}) %all-gather.5.cloned.1.call-update) | async-done | bytes 1048592 | tf_op jit(solution)/shard_map/all_gather | solution.py:80
  230.8 1.7 fusion.47
  232.5 88.4 %all-to-all-done = bf16[2,8,128,1536]{3,1,0,2:T(8,128)(2,1)} async-done(((bf16[2,8,128,1536]{3,1,0,2:T(8,128)(2,1)}), bf16[2,8,128,1536]{3,1,0,2:T(8,128)(2,1)}, u32[]{:S(2)}, u32[]{:S(2)}) %all-to-all-start) | async-done | bytes 6291488 | tf_op jit(solution)/shard_map/all_to_all | solution.py:77
  320.9 10.6 %copy.114 = bf16[2,8,16,8,1536]{4,3,1,2,0:T(8,128)(2,1)} copy(bf16[2,8,16,8,1536]{4,1,0,3,2:T(8,128)(2,1)} %bitcast.11) | data formatting | bytes 12582912 | tf_op jit(solution)/shard_map/all_to_all | solution.py:77
  331.5 16.3 %reshape.61 = bf16[2,128,8,24,64]{4,3,2,1,0:T(8,128)(2,1)} reshape(bf16[2,16,8,8,1536]{4,3,2,1,0:T(8,128)(2,1)} %bitcast.97) | data formatting | bytes 12582912 | tf_op jit(solution)/shard_map/reshape | solution.py:32
  347.8 22.6 %fusion.37 = bf16[2,8,24,64,128]{4,3,2,1,0:T(8,128)(2,1)} fusion(f32[2,8,24,128]{3,2,1,0:T(8,128)S(1)} %bitcast_subtract_fusion, f32[2,8,24,128]{3,2,1,0:T(8,128)S(1)} %reduce_window_sum.18, f32[2,8,128,128]{3,2,1,0:T(8,128)S(1)} %fusion.47, pred[128,128]{1,0:T(8,128)(4,1)S(1)} %get-tuple-element.10, pred[128,128]{1,0:T(8,128)(4,1)S(1)} %get-tuple-element.11, ...), kind=kOutput, calls=%fused_computation.43 | convolution fusion | flops 852492288 | bytes 14057472 | tf_op jit(solution)/shard_map/iahlm,imahp->ilahp/dot_general | solution.py:45
  370.4 9.1 %copy.90 = bf16[2,128,8,1536]{3,2,0,1:T(8,128)(2,1)} copy(bf16[2,128,8,1536]{1,3,2,0:T(8,128)(2,1)} %bitcast.100) | data formatting | bytes 12582912 | tf_op jit(solution)/shard_map/convert_element_type | solution.py:81
  379.5 28.1 %all-to-all-start.3 = ((bf16[2,128,8,1536]{3,2,0,1:T(8,128)(2,1)}), bf16[2,128,8,1536]{3,2,0,1:T(8,128)(2,1)}, u32[]{:S(2)}, u32[]{:S(2)}) async-start(bf16[2,128,8,1536]{3,2,0,1:T(8,128)(2,1)} %copy.90), calls=%async_computation.3 | async-start | bytes 12582912 | tf_op jit(solution)/shard_map/all_to_all | solution.py:82
  407.6 0.3 reduce-scatter.2.cloned.1.call-start
  407.9 0.1 broadcast_in_dim.25
  407.9 0.1 mul.114
  408.0 8.6 %copy.78 = bf16[2,8,128,1536]{2,3,1,0:T(8,128)(2,1)} copy(bf16[2,8,128,1536]{3,2,1,0:T(8,128)(2,1)} %get-tuple-element.8) | data formatting | bytes 12582912 | tf_op jit(solution)/shard_map/convert_element_type | solution.py:73
  416.6 0.1 fusion.61
  416.7 4.6 reduce_window_sum.17
  421.3 0.1 fusion.66
  421.4 0.5 fusion.50
  421.9 18.8 %fusion.4 = f32[2,8,24,64,128]{4,3,2,1,0:T(8,128)} fusion(bf16[2,8,128,24,64]{2,4,3,1,0:T(8,128)(2,1)} %bitcast.99, f32[2,8,24,128]{3,2,1,0:T(8,128)S(1)} %fusion.66, f32[2,8,24,128]{3,2,1,0:T(8,128)S(1)} %reduce_window_sum.17, f32[2,8,128,128]{3,2,1,0:T(8,128)S(1)} %fusion.50, pred[128,128]{1,0:T(8,128)(4,1)S(1)} %get-tuple-element.10, ...), kind=kOutput, calls=%fused_computation.10 | convolution fusion | flops 849346560 | bytes 20348928 | tf_op jit(solution)/shard_map/iahlm,iamhp->ialhp/dot_general | solution.py:41
  440.7 12.6 %copy.93 = f32[2,8,128,1536]{3,2,1,0:T(8,128)} copy(f32[2,8,128,1536]{2,3,1,0:T(8,128)} %bitcast.98) | data formatting | bytes 25165824 | tf_op jit(solution)/shard_map/reshape | solution.py:48
  453.3 68.4 %all-to-all-done.3 = bf16[2,128,8,1536]{3,2,0,1:T(8,128)(2,1)} async-done(((bf16[2,128,8,1536]{3,2,0,1:T(8,128)(2,1)}), bf16[2,128,8,1536]{3,2,0,1:T(8,128)(2,1)}, u32[]{:S(2)}, u32[]{:S(2)}) %all-to-all-start.3) | async-done | bytes 6291488 | tf_op jit(solution)/shard_map/all_to_all | solution.py:82
  521.7 6.6 copy.91
  528.3 2.0 copy-done.2
  530.3 11.3 %fusion.60 = f32[2,8,128,1536]{3,2,1,0:T(8,128)} fusion(bf16[2,8,128,1536]{3,2,1,0:T(8,128)(2,1)} %get-tuple-element.9, f32[1536]{0:T(1024)S(1)} %mul.114, f32[2,8,128,1536]{3,2,1,0:T(8,128)S(1)} %copy-done.2, bf16[2,16,8,8,1536]{4,3,2,1,0:T(8,128)(2,1)} %bitcast.95), kind=kLoop, calls=%fused_computation.65 | loop fusion | flops 18874368 | bytes 37754880 | tf_op jit(solution)/shard_map/mul | solution.py:88
  541.7 14.7 %mul.118 = f32[2,8,128,4,384]{4,3,2,1,0:T(4,128)} reshape(f32[2,8,128,1536]{3,2,1,0:T(8,128)} %fusion.60) | data formatting | bytes 25165824 | tf_op jit(solution)/shard_map/mul | solution.py:88
  556.4 6.9 reduce_sum.19
  563.3 0.3 copy.94
  563.7 0.4 copy.95
  564.0 6.1 mul.119
  570.1 15.3 %mul.120 = f32[2,8,128,1536]{3,2,1,0:T(8,128)} reshape(f32[2,8,128,4,384]{4,3,2,1,0:T(4,128)} %mul.119) | data formatting | bytes 25165824 | tf_op jit(solution)/shard_map/mul | solution.py:89
  585.4 24.6 %fusion.24 = f32[2,8,128,2048]{3,2,1,0:T(8,128)} fusion(f32[2,8,128,1536]{3,2,1,0:T(8,128)} %mul.120, bf16[1536,2048]{1,0:T(8,128)(2,1)} %param.19, f32[1536]{0:T(1024)S(1)} %copy-done.6, bf16[2,8,128,1536]{3,2,1,0:T(8,128)(2,1)} %get-tuple-element.9, f32[2,8,128,1536]{3,2,1,0:T(8,128)} %copy.93, f32[1536]{0:T(1024)S(1)} %mul.114, ...), kind=kOutput, calls=%fused_computation.34 | convolution fusion | flops 12910067712 | bytes 60829696 | tf_op jit(solution)/shard_map/irwc,cd->irwd/dot_general | solution.py:90
  610.1 0.0 reduce-scatter.2.cloned.1.call-update
  610.1 0.0 copy-start.1
  610.1 211.8 %reduce-scatter.2.cloned.1.call-done = f32[2,8,128,1024]{3,2,1,0:T(8,128)} async-done(((f32[2,8,128,2048]{3,2,1,0:T(8,128)}), f32[2,8,128,1024]{3,2,1,0:T(8,128)}) %reduce-scatter.2.cloned.1.call-update) | async-done | bytes 8388624 | tf_op jit(solution)/shard_map/reduce_scatter | solution.py:91
  821.9 9.3 %add_convert_fusion = bf16[2,8,128,1024]{3,2,1,0:T(8,128)(2,1)} fusion(f32[2,8,128,1024]{3,2,1,0:T(8,128)} %param.10, f32[2,8,128,1024]{3,2,1,0:T(8,128)} %reduce-scatter.2.cloned.1.call-done), kind=kLoop, calls=%fused_computation.33 | loop fusion | flops 4194304 | bytes 20971520 | tf_op jit(solution)/shard_map/convert_element_type | solution.py:92
  (19 shorter events, 0.1 us)
Async XLA Ops:
  6.5 130.5 %copy-start = (bf16[2048,256]{1,0:T(8,128)(2,1)S(1)}, bf16[2048,256]{1,0:T(8,128)(2,1)}, u32[]{:S(2)}) copy-start(bf16[2048,256]{1,0:T(8,128)(2,1)} %param.13) | copy-start | bytes 3145732
  6.5 6.2 copy-start.7
  6.5 118.2 %copy-start.5 = (f32[2048]{0:T(1024)S(1)}, f32[2048]{0:T(1024)}, u32[]{:S(2)}) copy-start(f32[2048]{0:T(1024)} %param.11) | copy-start | bytes 24580
  6.5 118.2 %copy-start.8 = (f32[24]{0:T(128)S(1)}, f32[24]{0:T(128)}, u32[]{:S(2)}) copy-start(f32[24]{0:T(128)} %param.15) | copy-start | bytes 292
  6.5 118.2 %copy-start.4 = (bf16[2048,24]{0,1:T(8,128)(2,1)S(1)}, bf16[2048,24]{0,1:T(8,128)(2,1)}, u32[]{:S(2)}) copy-start(bf16[2048,24]{0,1:T(8,128)(2,1)} %param.14) | copy-start | bytes 294916
  6.5 113.1 %all-gather.3.cloned.1.call-start = ((), (), s32[]{:S(2)}) async-start(), calls=%async_computation.5 | async-start | bytes 12582912 | tf_op jit(solution)/shard_map/all_gather | solution.py:54
  131.4 30.8 %all-to-all-start.2 = ((bf16[16,2,1536]{2,1,0:T(2,128)(2,1)}), bf16[16,2,1536]{2,1,0:T(2,128)(2,1)S(1)}, u32[]{:S(2)}, u32[]{:S(2)}) async-start(bf16[16,2,1536]{2,1,0:T(2,128)(2,1)} %reshape.70), calls=%async_computation.2 | async-start | bytes 196608 | tf_op jit(solution)/shard_map/all_to_all | solution.py:79
  162.1 38.5 %all-to-all-start.1 = ((bf16[2,8,128,128]{3,1,0,2:T(8,128)(2,1)}), bf16[2,8,128,128]{3,1,0,2:T(8,128)(2,1)S(1)}, u32[]{:S(2)}, u32[]{:S(2)}) async-start(bf16[2,8,128,128]{3,1,0,2:T(8,128)(2,1)} %copy.81), calls=%async_computation.1 | async-start | bytes 1048576 | tf_op jit(solution)/shard_map/all_to_all | solution.py:78
  200.6 120.2 %all-to-all-start = ((bf16[2,8,128,1536]{3,1,0,2:T(8,128)(2,1)}), bf16[2,8,128,1536]{3,1,0,2:T(8,128)(2,1)}, u32[]{:S(2)}, u32[]{:S(2)}) async-start(bf16[2,8,128,1536]{3,1,0,2:T(8,128)(2,1)} %copy.79), calls=%async_computation | async-start | bytes 12582912 | tf_op jit(solution)/shard_map/all_to_all | solution.py:77
  206.8 24.0 %all-gather.5.cloned.1.call-start = ((), (), s32[]{:S(2)}) async-start(), calls=%async_computation.6 | async-start | bytes 1572864 | tf_op jit(solution)/shard_map/all_gather | solution.py:80
  370.4 37.5 %copy-start.3 = (f32[24]{0:T(128)S(1)}, f32[24]{0:T(128)}, u32[]{:S(2)}) copy-start(f32[24]{0:T(128)} %param.17) | copy-start | bytes 292
  379.5 142.2 %all-to-all-start.3 = ((bf16[2,128,8,1536]{3,2,0,1:T(8,128)(2,1)}), bf16[2,128,8,1536]{3,2,0,1:T(8,128)(2,1)}, u32[]{:S(2)}, u32[]{:S(2)}) async-start(bf16[2,128,8,1536]{3,2,0,1:T(8,128)(2,1)} %copy.90), calls=%async_computation.3 | async-start | bytes 12582912 | tf_op jit(solution)/shard_map/all_to_all | solution.py:82
  407.6 414.3 %reduce-scatter.2.cloned.1.call-start = ((), (), s32[]{:S(2)}) async-start(), calls=%async_computation.7 | async-start | bytes 25165824 | tf_op jit(solution)/shard_map/reduce_scatter | solution.py:91
  521.7 8.7 %copy-start.2 = (f32[2,8,128,1536]{3,2,1,0:T(8,128)S(1)}, f32[2,8,128,1536]{3,2,1,0:T(8,128)}, u32[]{:S(2)}) copy-start(f32[2,8,128,1536]{3,2,1,0:T(8,128)} %copy.93) | copy-start | bytes 37748740
  570.1 15.3 %copy-start.6 = (f32[1536]{0:T(1024)S(1)}, f32[1536]{0:T(1024)}, u32[]{:S(2)}) copy-start(f32[1536]{0:T(1024)} %param.18) | copy-start | bytes 18436
  610.1 221.1 %copy-start.1 = (bf16[2048,256]{1,0:T(8,128)(2,1)S(1)}, bf16[2048,256]{1,0:T(8,128)(2,1)}, u32[]{:S(2)}) copy-start(bf16[2048,256]{1,0:T(8,128)(2,1)} %param.13) | copy-start | bytes 3145732
Sparse Core Ops, SparseCore 0:
  12.9 106.6 all-gather.2
  209.1 21.5 all-gather.4
  610.2 211.6 reduce-scatter.1
where the time goes:
time: 847 us; the launch traced here: 838 us
  waiting for transfers between devices  492 us (58%)
  local copies, waits for them, and re-layouts  135 us (16%)
  matrix products  102 us (12%)
  other arithmetic  48.4 us (6%)
  starting transfers between devices  46.9 us (6%)
  between operations  13.6 us (2%)
    reduce_scatter x1, waiting for transfers between devices, on_device(): lax.psum_scatter(partial_out, 'tensor', scatter_dimension=3, tiled=True)  212 us
    all_gather x1, waiting for transfers between devices, on_device(): lax.all_gather(tokens.astype(jnp.bfloat16), 'tensor', axis=3, tiled=True)  107 us
    all_to_all x1, waiting for transfers between devices, on_device(): lax.all_to_all(value, 'space', split_axis=2, concat_axis=1, tiled=True)  88.4 us
    all_to_all x1, waiting for transfers between devices, on_device(): lax.all_to_all(column_out, 'space', split_axis=1, concat_axis=2, tiled=True)  68.4 us
    all_to_all x1, starting transfers between devices, on_device(): lax.all_to_all(column_out, 'space', split_axis=1, concat_axis=2, tiled=True)  28.1 us
    dot_general x1, matrix products, on_device(): jnp.einsum('irwc,cd->irwd', gated, w_out, preferred_element_type=jnp.floa...  24.6 us
    dot_general x1, matrix products, on_device(): jnp.einsum('irwd,dc->irwc', normed, w_inner, preferred_element_type=jnp.f...  23.2 us
    dot_general x1, matrix products, scan_grid(): jnp.einsum('iahlm,imahp->ilahp', weights, split_values, preferred_element...  22.6 us
  transfers between devices with their start and end apart: 7, of which 5 were waited for; matrix products, arithmetic and copies ran while one was open for 13% of the time, Pallas kernels for 0%

commit v1 on v0

--- a/solution.py
+++ b/solution.py
@@ -1,6 +1,10 @@
+import functools
+
 import jax
 import jax.numpy as jnp
 from jax import lax
+from jax.experimental import pallas as pl
+from jax.experimental.pallas import tpu as pltpu
 from jax.sharding import PartitionSpec as P
 
 HEAD_DIM = 64
@@ -92,9 +96,425 @@
     return (tokens + mixer).astype(jnp.bfloat16)
 
 
+LANES = 128
+SUBLANES = 8
+LOG2E = 1.4426950408889634
+HALVES = 2
+VMEM_LIMIT = 60 * 1024 * 1024
+
+
+def params(**extra):
+    return pltpu.CompilerParams(vmem_limit_bytes=VMEM_LIMIT, **extra)
+
+
+def resident(shape, index_map):
+    return pl.BlockSpec(shape, index_map, pipeline_mode=pl.Buffered(1))
+
+
+def turn_kernel(rows, tok_ref, out_ref, held):
+    width = tok_ref.shape[2]
+    for lane in range(tok_ref.shape[3] // LANES):
+        part = slice(lane * LANES, (lane + 1) * LANES)
+        for row in range(rows):
+            held[lane, pl.ds(row, width, stride=rows), :] = tok_ref[0, row, :, part]
+        out_ref[:, part] = held[lane].astype(jnp.bfloat16)
+
+
+def turn(tokens, image, part, width):
+    _, rows, _, feats = tokens.shape
+    step = width // 2
+    return pl.pallas_call(
+        functools.partial(turn_kernel, rows),
+        grid=(2,),
+        in_specs=[
+            pl.BlockSpec((1, rows, step, feats), lambda k: (image, 0, 2 * part + k, 0)),
+        ],
+        out_specs=pl.BlockSpec((step * rows, feats), lambda k: (k, 0)),
+        out_shape=jax.ShapeDtypeStruct((width * rows, feats), jnp.bfloat16),
+        scratch_shapes=[pltpu.VMEM((feats // LANES, step * rows, LANES), jnp.float32)],
+        compiler_params=params(),
+        cost_estimate=pl.CostEstimate(
+            flops=0, transcendentals=0, bytes_accessed=6 * width * rows * feats
+        ),
+        name="turn",
+    )(tokens)
+
+
+def project_kernel(
+    depth, heads, t_ref, own_ref, other_ref, g_own, g_other, w_own, w_other, m_own, m_other,
+    bias_ref, rate_ref, inner_ref, pack_ref,
+):
+    own = own_ref[...].astype(jnp.float32)
+    other = other_ref[...].astype(jnp.float32)
+    squares = jnp.sum(own * own, axis=-1, keepdims=True) + jnp.sum(
+        other * other, axis=-1, keepdims=True
+    )
+    scale = lax.rsqrt(squares / depth + EPS)
+    n_own = (own * scale * g_own[0]).astype(jnp.bfloat16)
+    n_other = (other * scale * g_other[0]).astype(jnp.bfloat16)
+
+    def project(a, b):
+        return jnp.dot(n_own, a, preferred_element_type=jnp.float32) + jnp.dot(
+            n_other, b, preferred_element_type=jnp.float32
+        )
+
+    small = project(m_own[0], m_other[0])
+    wide = inner_ref.shape[1]
+    step = jax.nn.softplus(small[:, 2 * STATE :] + bias_ref[...])
+    pack_ref[:, wide : wide + 2 * STATE] = small[:, : 2 * STATE].astype(jnp.bfloat16)
+    pack_ref[:, wide + 2 * STATE :] = (-rate_ref[...] * step).astype(jnp.bfloat16)
+    inner = project(w_own[0], w_other[0]).astype(jnp.bfloat16)
+    inner_ref[...] = inner
+    rows = inner.shape[0]
+    low = lax.broadcasted_iota(jnp.int32, (rows, LANES), 1) < HEAD_DIM
+    for pair in range(heads // 2):
+        part = slice(pair * LANES, (pair + 1) * LANES)
+        spread = jnp.where(
+            low, step[:, 2 * pair : 2 * pair + 1], step[:, 2 * pair + 1 : 2 * pair + 2]
+        )
+        pack_ref[:, part] = (inner[:, part].astype(jnp.float32) * spread).astype(jnp.bfloat16)
+
+
+def project(own, other, in_gain, w_inner, w_small, bias, rate, place, heads):
+    rows, feats = own.shape
+    wide = w_inner.shape[1]
+    small = w_small.shape[1]
+    tile = min(rows, 256)
+    gains = in_gain.reshape(2, 1, feats)
+    w_inner = w_inner.reshape(2, feats, wide)
+    w_small = w_small.reshape(2, feats, small)
+    row_spec = pl.BlockSpec((tile, feats), lambda i, t: (i, 0))
+
+    def pair(shape):
+        return [
+            resident((1,) + shape, lambda i, t: (t[0], 0, 0)),
+            resident((1,) + shape, lambda i, t: (1 - t[0], 0, 0)),
+        ]
+
+    packed = wide + small
+    return pl.pallas_call(
+        functools.partial(project_kernel, 2 * feats, heads),
+        grid_spec=pltpu.PrefetchScalarGridSpec(
+            num_scalar_prefetch=1,
+            grid=(rows // tile,),
+            in_specs=[row_spec, row_spec]
+            + pair((1, feats))
+            + pair((feats, wide))
+            + pair((feats, small))
+            + [resident((1, LANES), lambda i, t: (0, 0))] * 2,
+            out_specs=[
+                pl.BlockSpec((tile, wide), lambda i, t: (i, 0)),
+                pl.BlockSpec((tile, packed), lambda i, t: (i, 0)),
+            ],
+        ),
+        out_shape=[
+            jax.ShapeDtypeStruct((rows, wide), jnp.bfloat16),
+            jax.ShapeDtypeStruct((rows, packed), jnp.bfloat16),
+        ],
+        compiler_params=params(),
+        cost_estimate=pl.CostEstimate(
+            flops=4 * rows * feats * packed, transcendentals=0, bytes_accessed=20 * 2**20
+        ),
+        name="project",
+    )(place, own, other, gains, gains, w_inner, w_inner, w_small, w_small, bias, rate)
+
+
+def scan_sequence(length, heads, in_map, out_map, decay, value_of, store):
+    row = lax.broadcasted_iota(jnp.int32, (length, length), 0)
+    col = lax.broadcasted_iota(jnp.int32, (length, length), 1)
+    lower = row >= col
+    ones = jnp.where(lower, 1.0, 0.0).astype(jnp.bfloat16)
+    eye = jnp.where(row == col, 1.0, 0.0).astype(jnp.bfloat16)
+    scores = lax.dot_general(
+        out_map, in_map, (((1,), (1,)), ((), ())), preferred_element_type=jnp.float32
+    )
+    scores = jnp.where(row == col, scores + scores, scores)
+    running = jnp.dot(ones, decay, preferred_element_type=jnp.float32) * LOG2E
+    shifted = running - decay.astype(jnp.float32) * LOG2E
+    turned = lax.dot_general(
+        decay, ones, (((0,), (1,)), ((), ())), preferred_element_type=jnp.float32
+    )
+    turned_decay = lax.dot_general(
+        decay, eye, (((0,), (1,)), ((), ())), preferred_element_type=jnp.float32
+    )
+    running_row = turned * LOG2E
+    shifted_row = running_row - turned_decay * LOG2E
+    low = lax.broadcasted_iota(jnp.int32, (length, LANES), 1) < HEAD_DIM
+    for pair in range(heads // 2):
+        weights = []
+        for head in (2 * pair, 2 * pair + 1):
+            later = running[:, head : head + 1] - running_row[head : head + 1, :]
+            earlier = shifted_row[head : head + 1, :] - shifted[:, head : head + 1]
+            decayed = jnp.exp2(jnp.where(lower, later, earlier))
+            weights.append((scores * decayed).astype(jnp.bfloat16))
+        value = value_of(pair)
+        zero = jnp.zeros_like(value)
+        stacked = jnp.concatenate(
+            [jnp.where(low, value, zero), jnp.where(low, zero, value)], axis=0
+        ).astype(jnp.bfloat16)
+        store(
+            pair,
+            jnp.dot(
+                jnp.concatenate(weights, axis=1), stacked, preferred_element_type=jnp.float32
+            ),
+        )
+
+
+def column_kernel(heads, pack_ref, out_ref):
+    owners, _, rows, packed = pack_ref.shape
+    length = owners * rows
+    wide = out_ref.shape[3]
+
+    def take(start):
+        block = pack_ref[:, 0, :, start : start + LANES].astype(jnp.float32)
+        return block.reshape(length, LANES)
+
+    def store(pair, result):
+        out_ref[:, 0, :, pair * LANES : (pair + 1) * LANES] = result.reshape(
+            owners, rows, LANES
+        ).astype(jnp.bfloat16)
+
+    scan_sequence(
+        length,
+        heads,
+        take(wide).astype(jnp.bfloat16),
+        take(wide + STATE).astype(jnp.bfloat16),
+        take(wide + 2 * STATE).astype(jnp.bfloat16),
+        lambda pair: take(pair * LANES),
+        store,
+    )
+
+
+def scan_cost(sequences, length, heads):
+    return pl.CostEstimate(
+        flops=8 * sequences * heads * length * length * LANES,
+        transcendentals=sequences * heads * length * length,
+        bytes_accessed=sequences * length * heads * HEAD_DIM * 6,
+    )
+
+
+def column_scan(pack, heads):
+    owners, columns, rows, packed = pack.shape
+    wide = heads * HEAD_DIM
+    return pl.pallas_call(
+        functools.partial(column_kernel, heads),
+        grid=(columns,),
+        in_specs=[pl.BlockSpec((owners, 1, rows, packed), lambda c: (0, c, 0, 0))],
+        out_specs=pl.BlockSpec((owners, 1, rows, wide), lambda c: (0, c, 0, 0)),
+        out_shape=jax.ShapeDtypeStruct((owners, columns, rows, wide), jnp.bfloat16),
+        compiler_params=params(),
+        cost_estimate=scan_cost(columns, owners * rows, heads),
+        name="column_scan",
+    )(pack)
+
+
+def row_kernel(rows, heads, *refs):
+    packs, out_ref, held = refs[:-2], refs[-2], refs[-1]
+    row = pl.program_id(0)
+    wide = heads * HEAD_DIM
+    tall = packs[0].shape[0]
+    length = tall * len(packs) // rows
+
+    @pl.when(row == 0)
+    def _():
+        for k, pack in enumerate(packs):
+            for lane in range(pack.shape[1] // LANES):
+                part = slice(lane * LANES, (lane + 1) * LANES)
+                held[lane, k * tall : (k + 1) * tall, :] = pack[:, part].astype(jnp.float32)
+
+    def take(lane):
+        return held[lane, pl.ds(row, length, stride=rows), :]
+
+    def store(pair, result):
+        out_ref[pair, pl.ds(row, length, stride=rows), :] = result
+
+    first = wide // LANES
+    scan_sequence(
+        length,
+        heads,
+        take(first).astype(jnp.bfloat16),
+        take(first + 1).astype(jnp.bfloat16),
+        take(first + 2).astype(jnp.bfloat16),
+        take,
+        store,
+    )
+
+
+def row_scan(packs, rows, heads):
+    tall, packed = packs[0].shape
+    total = tall * len(packs)
+    wide = heads * HEAD_DIM
+    return pl.pallas_call(
+        functools.partial(row_kernel, rows, heads),
+        grid=(rows,),
+        in_specs=[resident((tall, packed), lambda r: (0, 0))] * len(packs),
+        out_specs=resident((wide // LANES, total, LANES), lambda r: (0, 0, 0)),
+        out_shape=jax.ShapeDtypeStruct((wide // LANES, total, LANES), jnp.float32),
+        scratch_shapes=[pltpu.VMEM((packed // LANES, total, LANES), jnp.float32)],
+        compiler_params=params(),
+        cost_estimate=scan_cost(rows, total // rows, heads),
+        name="row_scan",
+    )(*packs)
+
+
+def output_kernel(t_ref, row_ref, col_ref, inner_ref, skip_ref, gain_ref, w_own, w_other, own_ref, send_ref):
+    wide = inner_ref.shape[1]
+    group = NORM_HEADS * HEAD_DIM
+    gated = []
+    for start in range(0, wide, group):
+        parts = []
+        squares = 0.0
+        for lane in range(start, start + group, LANES):
+            part = slice(lane, lane + LANES)
+            total = (
+                row_ref[lane // LANES]
+                + col_ref[:, part].astype(jnp.float32)
+                + skip_ref[:, part] * inner_ref[:, part].astype(jnp.float32)
+            )
+            parts.append(total)
+            squares = squares + total * total
+        scale = lax.rsqrt(jnp.sum(squares, axis=-1, keepdims=True) / group + EPS)
+        for k, total in enumerate(parts):
+            lane = start + k * LANES
+            gated.append((total * scale * gain_ref[:, lane : lane + LANES]).astype(jnp.bfloat16))
+    gated = jnp.concatenate(gated, axis=1)
+    send_ref[...] = jnp.dot(gated, w_other[...], preferred_element_type=jnp.float32).astype(
+        jnp.bfloat16
+    )
+    own_ref[...] = jnp.dot(gated, w_own[...], preferred_element_type=jnp.float32)
+
+
+def output(row_out, part, col, inner, skip, gain, w_out, place):
+    rows, wide = inner.shape
+    feats = w_out.shape[1] // 2
+    tile = min(rows, 256)
+    steps = rows // tile
+    row_spec = pl.BlockSpec((tile, wide), lambda i, t: (i, 0))
+    out_spec = pl.BlockSpec((tile, feats), lambda i, t: (i, 0))
+    return pl.pallas_call(
+        output_kernel,
+        grid_spec=pltpu.PrefetchScalarGridSpec(
+            num_scalar_prefetch=1,
+            grid=(steps,),
+            in_specs=[
+                pl.BlockSpec((wide // LANES, tile, LANES), lambda i, t: (0, part * steps + i, 0)),
+                row_spec,
+                row_spec,
+                resident((1, wide), lambda i, t: (0, 0)),
+                resident((1, wide), lambda i, t: (0, 0)),
+                resident((wide, feats), lambda i, t: (0, t[0])),
+                resident((wide, feats), lambda i, t: (0, 1 - t[0])),
+            ],
+            out_specs=[out_spec, out_spec],
+        ),
+        out_shape=[
+            jax.ShapeDtypeStruct((rows, feats), jnp.float32),
+            jax.ShapeDtypeStruct((rows, feats), jnp.bfloat16),
+        ],
+        compiler_params=params(),
+        cost_estimate=pl.CostEstimate(
+            flops=4 * rows * feats * wide, transcendentals=0, bytes_accessed=16 * 2**20
+        ),
+        name="output",
+    )(place, row_out, col, inner, skip, gain, w_out, w_out)
+
+
+def finish_kernel(rows, own_ref, got_ref, tok_ref, *rest):
+    out_ref, held = rest[-2:]
+    width = tok_ref.shape[2]
+    for lane in range(tok_ref.shape[3] // LANES):
+        part = slice(lane * LANES, (lane + 1) * LANES)
+        held[lane] = own_ref[:, part] + got_ref[:, part].astype(jnp.float32)
+        for row in range(rows):
+            out_ref[0, row, :, part] = (
+                tok_ref[0, row, :, part] + held[lane, pl.ds(row, width, stride=rows), :]
+            ).astype(jnp.bfloat16)
+
+
+def finish(own, got, tokens, image, part, width, earlier):
+    _, rows, _, feats = tokens.shape
+    step = width // 2
+    flat = pl.BlockSpec((step * rows, feats), lambda k: (k, 0))
+    grid_block = pl.BlockSpec((1, rows, step, feats), lambda k: (image, 0, 2 * part + k, 0))
+    chained = [] if earlier is None else [earlier]
+    return pl.pallas_call(
+        functools.partial(finish_kernel, rows),
+        grid=(2,),
+        in_specs=[flat, flat, grid_block] + [pl.BlockSpec(memory_space=pl.ANY)] * len(chained),
+        out_specs=grid_block,
+        out_shape=jax.ShapeDtypeStruct(tokens.shape, jnp.bfloat16),
+        scratch_shapes=[pltpu.VMEM((feats // LANES, step * rows, LANES), jnp.float32)],
+        input_output_aliases={3: 0} if chained else {},
+        compiler_params=params(),
+        cost_estimate=pl.CostEstimate(
+            flops=0, transcendentals=0, bytes_accessed=12 * width * rows * feats
+        ),
+        name="finish",
+    )(own, got, tokens, *chained)
+
+
+def pipelined(
+    owners, tokens, in_gain, w_inner, w_bc, w_step, step_bias, decay_rate, skip, norm_gain, w_out
+):
+    images, rows, columns, feats = tokens.shape
+    heads = w_step.shape[1]
+    wide = w_inner.shape[1]
+    width = columns // HALVES
+    swap = [(0, 1), (1, 0)]
+    place = lax.axis_index("tensor").astype(jnp.int32).reshape(1)
+    pad = LANES - heads
+    w_small = jnp.concatenate([w_bc, jnp.pad(w_step, ((0, 0), (0, pad)))], axis=1)
+    bias = jnp.pad(step_bias, (0, pad)).reshape(1, LANES)
+    rate = jnp.pad(decay_rate, (0, pad)).reshape(1, LANES)
+    skip_wide = jnp.repeat(skip, HEAD_DIM).reshape(1, wide)
+    gain = norm_gain.reshape(1, wide)
+    chunks = [(image, part) for image in range(images) for part in range(HALVES)]
+    own = [turn(tokens, image, part, width) for image, part in chunks]
+    other = [lax.ppermute(block, "tensor", swap) for block in own]
+    inner, packs, arrived = [], [], []
+    for k in range(len(chunks)):
+        a, b = project(own[k], other[k], in_gain, w_inner, w_small, bias, rate, place, heads)
+        inner.append(a)
+        packs.append(b)
+        sent = b.reshape(owners, width // owners, rows, b.shape[1])
+        arrived.append(lax.all_to_all(sent, "space", split_axis=0, concat_axis=0, tiled=True))
+    row_out = [
+        row_scan(packs[image * HALVES : (image + 1) * HALVES], rows, heads)
+        for image in range(images)
+    ]
+    result = None
+    for k, (image, part) in enumerate(chunks):
+        back = lax.all_to_all(
+            column_scan(arrived[k], heads), "space", split_axis=0, concat_axis=0, tiled=True
+        ).reshape(width * rows, wide)
+        kept, send = output(row_out[image], part, back, inner[k], skip_wide, gain, w_out, place)
+        got = lax.ppermute(send, "tensor", swap)
+        result = finish(kept, got, tokens, image, part, width, result)
+    return result
+
+
+def dispatch(owners, tensor, tokens, *rest):
+    heads = rest[3].shape[1]
+    rows, columns = tokens.shape[1:3]
+    fits = (
+        tensor == 2
+        and rows == SUBLANES
+        and columns % (HALVES * owners) == 0
+        and owners * rows == columns == LANES
+        and heads % NORM_HEADS == 0
+        and heads % 2 == 0
+        and heads <= LANES
+        and STATE == LANES == 2 * HEAD_DIM
+    )
+    if fits:
+        return pipelined(owners, tokens, *rest)
+    return on_device(tokens, *rest)
+
+
 def solution(mesh):
+    body = functools.partial(dispatch, mesh.shape["space"], mesh.shape["tensor"])
     return jax.shard_map(
-        on_device,
+        body,
         mesh=mesh,
         in_specs=(
             P(None, "space", None, "tensor"),

time: 847 us -> 511 us (0.60)
  waiting for transfers between devices: 492 us -> 248 us
  Pallas kernels: 0 us -> 163 us
  local copies, waits for them, and re-layouts: 135 us -> 11.9 us
  matrix products: 102 us -> 0 us
  other arithmetic: 48.4 us -> 1.38 us
  starting transfers between devices: 46.9 us -> 85.4 us
  between operations: 13.6 us -> 0.16 us
    reduce_scatter x1 -> x0, waiting for transfers between devices: 212 us -> none  [on_device(): lax.psum_scatter(partial_out, 'tensor', scatter_dimension=3, tiled=True)]
    pallas_call x0 -> x22, Pallas kernels: none -> 163 us  [the longest x4 40.9 us: project(): pl.pallas_call(functools.partial(project_kernel, 2 * feats, heads), grid_...]
    ppermute x0 -> x8, waiting for transfers between devices: none -> 142 us  [the longest x4 93.5 us: pipelined(): other = [lax.ppermute(block, 'tensor', swap) for block in own]]
    all_gather x2 -> x0, waiting for transfers between devices: 124 us -> none  [the longest x1 107 us: on_device(): lax.all_gather(tokens.astype(jnp.bfloat16), 'tensor', axis=3, tiled=True)]
    dot_general x8 -> x0, matrix products: 102 us -> none  [the longest x1 24.6 us: on_device(): jnp.einsum('irwc,cd->irwd', gated, w_out, preferred_element_type=jnp.floa...]
    mul x6 -> x0, local copies, waits for them, and re-layouts: 54 us -> none  [the longest x2 21.4 us: on_device(): grouped * norm_scale]
    all_to_all x4 -> x8, waiting for transfers between devices: 157 us -> 106 us  [the longest x4 74.3 us: pipelined(): lax.all_to_all(column_scan(arrived[k], heads), 'space', split_axis=0, con...]
    reshape x2, local copies, waits for them, and re-layouts: 28.9 us -> 1.19 us  [the longest x1 0.6 us: pipelined(): gain = norm_gain.reshape(1, wide)]
  transfers between devices with their start and end apart: 7 -> 16, of which waited for: 5 -> 11; matrix products, arithmetic and copies ran while one was open for 13% -> 1% of each run, Pallas kernels for 0% -> 29%
where the time goes in v1:
time: 511 us; the launch traced here: 510 us
  waiting for transfers between devices  248 us (49%)
  Pallas kernels  163 us (32%)
  starting transfers between devices  85.4 us (17%)
  local copies, waits for them, and re-layouts  11.9 us (2%)
    ppermute x4, waiting for transfers between devices, pipelined(): other = [lax.ppermute(block, 'tensor', swap) for block in own]  93.5 us
    all_to_all x4, waiting for transfers between devices, pipelined(): lax.all_to_all(column_scan(arrived[k], heads), 'space', split_axis=0, con...  74.3 us
    ppermute x4, waiting for transfers between devices, pipelined(): got = lax.ppermute(send, 'tensor', swap)  48.9 us
    pallas_call x4, Pallas kernels, project(): pl.pallas_call(functools.partial(project_kernel, 2 * feats, heads), grid_...  40.9 us
    all_to_all x4, starting transfers between devices, pipelined(): lax.all_to_all(column_scan(arrived[k], heads), 'space', split_axis=0, con...  38 us
    all_to_all x4, starting transfers between devices, pipelined(): lax.all_to_all(sent, 'space', split_axis=0, concat_axis=0, tiled=True)  35.7 us
    pallas_call x4, Pallas kernels, output(): pl.pallas_call(output_kernel, grid_spec=pltpu.PrefetchScalarGridSpec(num_...  35.7 us
    pallas_call x2, Pallas kernels, row_scan(): pl.pallas_call(functools.partial(row_kernel, rows, heads), grid=(rows,),...  32.3 us
  transfers between devices with their start and end apart: 16, of which 11 were waited for; matrix products, arithmetic and copies ran while one was open for 1% of the time, Pallas kernels for 29%

profile of v1, /device:TPU:0, one launch (start us, length us, event | category | flops | bytes accessed | tf_op | source)
XLA Modules:
  0.0 510.1 jit_solution(11163204106213099316)
XLA Ops:
  0.0 2.8 turn.6.own_ref
  2.8 3.0 collective-permute-start.4
  5.8 0.3 copy.15
  6.1 0.6 pad_bitcast_fusion
  6.7 1.4 fusion.1
  8.1 21.1 %collective-permute-done.4.other_ref = bf16[512,1024]{1,0:T(8,128)(2,1)S(1)} collective-permute-done((bf16[512,1024]{1,0:T(8,128)(2,1)}, bf16[512,1024]{1,0:T(8,128)(2,1)S(1)}, u32[]{:S(2)}, u32[]{:S(2)}) %collective-permute-start.4) | collective-permute-done | bytes 1048608 | tf_op jit(solution)/shard_map/ppermute | solution.py:473
  29.2 1.0 copy-done.9
  30.1 10.2 %project.6 = (bf16[512,1536]{1,0:T(8,128)(2,1)}, bf16[512,1920]{1,0:T(8,128)(2,1)}) custom-call(s32[1]{0:T(128)} %bitcast.t_ref, bf16[512,1024]{1,0:T(8,128)(2,1)} %turn.6.own_ref, bf16[512,1024]{1,0:T(8,128)(2,1)} %copy-done.9, f32[2,1,1024]{2,1,0:T(1,128)} %bitcast.40, f32[2,1,1024]{2,1,0:T(1,128)} %bitcast.41, bf16[2,1024,1536]{2,1,0:T(8,128)(2,1)} %bitcast.16, ...), custom_call_target="tpu_custom_call" | custom-call | flops 4026531840 | bytes 20971520 | tf_op jit(solution)/shard_map/project/pallas_call | solution.py:195
  40.4 6.1 %all-to-all-start.6 = ((bf16[16,4,8,1920]{3,2,1,0:T(8,128)(2,1)}), bf16[16,4,8,1920]{3,2,1,0:T(8,128)(2,1)S(1)}, u32[]{:S(2)}, u32[]{:S(2)}) async-start(bf16[16,4,8,1920]{3,2,1,0:T(8,128)(2,1)} %bitcast.36), calls=%async_computation.6 | async-start | bytes 3932160 | tf_op jit(solution)/shard_map/all_to_all | solution.py:480
  46.5 2.7 turn.7.own_ref
  49.2 1.5 collective-permute-start.5
  50.7 24.2 %collective-permute-done.5.other_ref = bf16[512,1024]{1,0:T(8,128)(2,1)S(1)} collective-permute-done((bf16[512,1024]{1,0:T(8,128)(2,1)}, bf16[512,1024]{1,0:T(8,128)(2,1)S(1)}, u32[]{:S(2)}, u32[]{:S(2)}) %collective-permute-start.5) | collective-permute-done | bytes 1048608 | tf_op jit(solution)/shard_map/ppermute | solution.py:473
  74.9 1.0 copy-done.11
  75.9 10.2 %project.7 = (bf16[512,1536]{1,0:T(8,128)(2,1)}, bf16[512,1920]{1,0:T(8,128)(2,1)}) custom-call(s32[1]{0:T(128)} %bitcast.t_ref, bf16[512,1024]{1,0:T(8,128)(2,1)} %turn.7.own_ref, bf16[512,1024]{1,0:T(8,128)(2,1)} %copy-done.11, f32[2,1,1024]{2,1,0:T(1,128)} %bitcast.42, f32[2,1,1024]{2,1,0:T(1,128)} %bitcast.43, bf16[2,1024,1536]{2,1,0:T(8,128)(2,1)} %bitcast.18, ...), custom_call_target="tpu_custom_call" | custom-call | flops 4026531840 | bytes 20971520 | tf_op jit(solution)/shard_map/project/pallas_call | solution.py:195
  86.1 1.3 copy-done.4
  87.4 9.8 %all-to-all-start.4 = ((bf16[16,4,8,1920]{3,2,1,0:T(8,128)(2,1)}), bf16[16,4,8,1920]{3,2,1,0:T(8,128)(2,1)}, u32[]{:S(2)}, u32[]{:S(2)}) async-start(bf16[16,4,8,1920]{3,2,1,0:T(8,128)(2,1)} %bitcast.37), calls=%async_computation.4 | async-start | bytes 3932160 | tf_op jit(solution)/shard_map/all_to_all | solution.py:480
  97.3 2.7 turn.4.own_ref
  100.0 1.5 collective-permute-start
  101.5 24.1 %collective-permute-done.other_ref = bf16[512,1024]{1,0:T(8,128)(2,1)S(1)} collective-permute-done((bf16[512,1024]{1,0:T(8,128)(2,1)}, bf16[512,1024]{1,0:T(8,128)(2,1)S(1)}, u32[]{:S(2)}, u32[]{:S(2)}) %collective-permute-start) | collective-permute-done | bytes 1048608 | tf_op jit(solution)/shard_map/ppermute | solution.py:473
  125.6 1.0 copy-done.12
  126.6 10.2 %project.4 = (bf16[512,1536]{1,0:T(8,128)(2,1)}, bf16[512,1920]{1,0:T(8,128)(2,1)}) custom-call(s32[1]{0:T(128)} %bitcast.t_ref, bf16[512,1024]{1,0:T(8,128)(2,1)} %turn.4.own_ref, bf16[512,1024]{1,0:T(8,128)(2,1)} %copy-done.12, f32[2,1,1024]{2,1,0:T(1,128)} %bitcast.44, f32[2,1,1024]{2,1,0:T(1,128)} %bitcast.45, bf16[2,1024,1536]{2,1,0:T(8,128)(2,1)} %bitcast.20, ...), custom_call_target="tpu_custom_call" | custom-call | flops 4026531840 | bytes 20971520 | tf_op jit(solution)/shard_map/project/pallas_call | solution.py:195
  136.8 9.9 %all-to-all-start.2 = ((bf16[16,4,8,1920]{3,2,1,0:T(8,128)(2,1)}), bf16[16,4,8,1920]{3,2,1,0:T(8,128)(2,1)S(1)}, u32[]{:S(2)}, u32[]{:S(2)}) async-start(bf16[16,4,8,1920]{3,2,1,0:T(8,128)(2,1)} %bitcast.38), calls=%async_computation.2 | async-start | bytes 3932160 | tf_op jit(solution)/shard_map/all_to_all | solution.py:480
  146.7 2.7 turn.5.own_ref
  149.4 1.5 collective-permute-start.1
  150.9 24.1 %collective-permute-done.1.other_ref = bf16[512,1024]{1,0:T(8,128)(2,1)S(1)} collective-permute-done((bf16[512,1024]{1,0:T(8,128)(2,1)}, bf16[512,1024]{1,0:T(8,128)(2,1)S(1)}, u32[]{:S(2)}, u32[]{:S(2)}) %collective-permute-start.1) | collective-permute-done | bytes 1048608 | tf_op jit(solution)/shard_map/ppermute | solution.py:473
  175.1 1.0 copy-done.10
  176.1 10.2 %project.5 = (bf16[512,1536]{1,0:T(8,128)(2,1)}, bf16[512,1920]{1,0:T(8,128)(2,1)}) custom-call(s32[1]{0:T(128)} %bitcast.t_ref, bf16[512,1024]{1,0:T(8,128)(2,1)} %turn.5.own_ref, bf16[512,1024]{1,0:T(8,128)(2,1)} %copy-done.10, f32[2,1,1024]{2,1,0:T(1,128)} %bitcast.46, f32[2,1,1024]{2,1,0:T(1,128)} %bitcast.47, bf16[2,1024,1536]{2,1,0:T(8,128)(2,1)} %bitcast.22, ...), custom_call_target="tpu_custom_call" | custom-call | flops 4026531840 | bytes 20971520 | tf_op jit(solution)/shard_map/project/pallas_call | solution.py:195
  186.3 1.3 copy-done.5
  187.6 9.8 %all-to-all-start = ((bf16[16,4,8,1920]{3,2,1,0:T(8,128)(2,1)}), bf16[16,4,8,1920]{3,2,1,0:T(8,128)(2,1)}, u32[]{:S(2)}, u32[]{:S(2)}) async-start(bf16[16,4,8,1920]{3,2,1,0:T(8,128)(2,1)} %bitcast.39), calls=%async_computation | async-start | bytes 3932160 | tf_op jit(solution)/shard_map/all_to_all | solution.py:480
  197.4 7.1 %column_scan.7 = bf16[16,4,8,1536]{3,2,1,0:T(8,128)(2,1)} custom-call(bf16[16,4,8,1920]{3,2,1,0:T(8,128)(2,1)} %copy-done.4), custom_call_target="tpu_custom_call" | custom-call | flops 1610612736 | bytes 4718592 | tf_op jit(solution)/shard_map/column_scan/pallas_call | solution.py:299
  204.5 31.6 %all-to-all-done.pack_ref = bf16[16,4,8,1920]{3,2,1,0:T(8,128)(2,1)} async-done(((bf16[16,4,8,1920]{3,2,1,0:T(8,128)(2,1)}), bf16[16,4,8,1920]{3,2,1,0:T(8,128)(2,1)}, u32[]{:S(2)}, u32[]{:S(2)}) %all-to-all-start) | async-done | bytes 1966112 | tf_op jit(solution)/shard_map/all_to_all | solution.py:480
  236.2 10.7 %all-to-all-start.7 = ((bf16[16,4,8,1536]{3,2,1,0:T(8,128)(2,1)}), bf16[16,4,8,1536]{3,2,1,0:T(8,128)(2,1)S(1)}, u32[]{:S(2)}, u32[]{:S(2)}) async-start(bf16[16,4,8,1536]{3,2,1,0:T(8,128)(2,1)} %column_scan.7), calls=%async_computation.7 | async-start | bytes 3145728 | tf_op jit(solution)/shard_map/all_to_all | solution.py:487
  246.9 7.1 %column_scan.6 = bf16[16,4,8,1536]{3,2,1,0:T(8,128)(2,1)} custom-call(bf16[16,4,8,1920]{3,2,1,0:T(8,128)(2,1)} %all-to-all-done.4.pack_ref), custom_call_target="tpu_custom_call" | custom-call | flops 1610612736 | bytes 4718592 | tf_op jit(solution)/shard_map/column_scan/pallas_call | solution.py:299
  253.9 24.8 %all-to-all-done.7 = bf16[16,4,8,1536]{3,2,1,0:T(8,128)(2,1)S(1)} async-done(((bf16[16,4,8,1536]{3,2,1,0:T(8,128)(2,1)}), bf16[16,4,8,1536]{3,2,1,0:T(8,128)(2,1)S(1)}, u32[]{:S(2)}, u32[]{:S(2)}) %all-to-all-start.7) | async-done | bytes 1572896 | tf_op jit(solution)/shard_map/all_to_all | solution.py:487
  278.7 9.1 %all-to-all-start.5 = ((bf16[16,4,8,1536]{3,2,1,0:T(8,128)(2,1)}), bf16[16,4,8,1536]{3,2,1,0:T(8,128)(2,1)S(1)}, u32[]{:S(2)}, u32[]{:S(2)}) async-start(bf16[16,4,8,1536]{3,2,1,0:T(8,128)(2,1)} %column_scan.6), calls=%async_computation.5 | async-start | bytes 3145728 | tf_op jit(solution)/shard_map/all_to_all | solution.py:487
  287.8 7.1 %column_scan.5 = bf16[16,4,8,1536]{3,2,1,0:T(8,128)(2,1)} custom-call(bf16[16,4,8,1920]{3,2,1,0:T(8,128)(2,1)} %copy-done.5), custom_call_target="tpu_custom_call" | custom-call | flops 1610612736 | bytes 4718592 | tf_op jit(solution)/shard_map/column_scan/pallas_call | solution.py:299
  294.9 24.7 %all-to-all-done.5 = bf16[16,4,8,1536]{3,2,1,0:T(8,128)(2,1)S(1)} async-done(((bf16[16,4,8,1536]{3,2,1,0:T(8,128)(2,1)}), bf16[16,4,8,1536]{3,2,1,0:T(8,128)(2,1)S(1)}, u32[]{:S(2)}, u32[]{:S(2)}) %all-to-all-start.5) | async-done | bytes 1572896 | tf_op jit(solution)/shard_map/all_to_all | solution.py:487
  319.7 9.1 %all-to-all-start.3 = ((bf16[16,4,8,1536]{3,2,1,0:T(8,128)(2,1)}), bf16[16,4,8,1536]{3,2,1,0:T(8,128)(2,1)S(1)}, u32[]{:S(2)}, u32[]{:S(2)}) async-start(bf16[16,4,8,1536]{3,2,1,0:T(8,128)(2,1)} %column_scan.5), calls=%async_computation.3 | async-start | bytes 3145728 | tf_op jit(solution)/shard_map/all_to_all | solution.py:487
  328.8 7.1 %column_scan.4 = bf16[16,4,8,1536]{3,2,1,0:T(8,128)(2,1)} custom-call(bf16[16,4,8,1920]{3,2,1,0:T(8,128)(2,1)} %all-to-all-done.pack_ref), custom_call_target="tpu_custom_call" | custom-call | flops 1610612736 | bytes 4718592 | tf_op jit(solution)/shard_map/column_scan/pallas_call | solution.py:299
  335.9 24.8 %all-to-all-done.3 = bf16[16,4,8,1536]{3,2,1,0:T(8,128)(2,1)S(1)} async-done(((bf16[16,4,8,1536]{3,2,1,0:T(8,128)(2,1)}), bf16[16,4,8,1536]{3,2,1,0:T(8,128)(2,1)S(1)}, u32[]{:S(2)}, u32[]{:S(2)}) %all-to-all-start.3) | async-done | bytes 1572896 | tf_op jit(solution)/shard_map/all_to_all | solution.py:487
  360.6 9.1 %all-to-all-start.1 = ((bf16[16,4,8,1536]{3,2,1,0:T(8,128)(2,1)}), bf16[16,4,8,1536]{3,2,1,0:T(8,128)(2,1)S(1)}, u32[]{:S(2)}, u32[]{:S(2)}) async-start(bf16[16,4,8,1536]{3,2,1,0:T(8,128)(2,1)} %column_scan.4), calls=%async_computation.1 | async-start | bytes 3145728 | tf_op jit(solution)/shard_map/all_to_all | solution.py:487
  369.8 0.1 broadcast_in_dim.3
  369.8 0.7 reshape_reshape.3.skip_ref
  370.5 0.6 reshape.62.gain_ref
  371.1 16.2 %row_scan.3.row_ref = f32[12,1024,128]{2,1,0:T(8,128)} custom-call(bf16[512,1920]{1,0:T(8,128)(2,1)} %get-tuple-element.29.refs_0_, bf16[512,1920]{1,0:T(8,128)(2,1)} %get-tuple-element.30.refs_1_), custom_call_target="tpu_custom_call" | custom-call | flops 3221225472 | bytes 9437184 | tf_op jit(solution)/shard_map/row_scan/pallas_call | solution.py:347
  387.3 16.2 %row_scan.2.row_ref = f32[12,1024,128]{2,1,0:T(8,128)} custom-call(bf16[512,1920]{1,0:T(8,128)(2,1)} %get-tuple-element.21.refs_0_, bf16[512,1920]{1,0:T(8,128)(2,1)} %get-tuple-element.22.refs_1_), custom_call_target="tpu_custom_call" | custom-call | flops 3221225472 | bytes 9437184 | tf_op jit(solution)/shard_map/row_scan/pallas_call | solution.py:347
  403.4 8.9 %output.7 = (f32[512,1024]{1,0:T(8,128)}, bf16[512,1024]{1,0:T(8,128)(2,1)}) custom-call(s32[1]{0:T(128)} %bitcast.t_ref, f32[12,1024,128]{2,1,0:T(8,128)} %row_scan.3.row_ref, bf16[512,1536]{1,0:T(8,128)(2,1)} %bitcast.33, bf16[512,1536]{1,0:T(8,128)(2,1)} %get-tuple-element.34.inner_ref, f32[1,1536]{1,0:T(1,128)} %reshape_reshape.3.skip_ref, ...), custom_call_target="tpu_custom_call" | custom-call | flops 3221225472 | bytes 16777216 | tf_op jit(solution)/shard_map/output/pallas_call | solution.py:394
  412.3 1.5 collective-permute-start.7
  413.9 8.9 %output.6 = (f32[512,1024]{1,0:T(8,128)}, bf16[512,1024]{1,0:T(8,128)(2,1)}) custom-call(s32[1]{0:T(128)} %bitcast.t_ref, f32[12,1024,128]{2,1,0:T(8,128)} %row_scan.3.row_ref, bf16[512,1536]{1,0:T(8,128)(2,1)} %bitcast.34, bf16[512,1536]{1,0:T(8,128)(2,1)} %get-tuple-element.31.inner_ref, f32[1,1536]{1,0:T(1,128)} %reshape_reshape.3.skip_ref, ...), custom_call_target="tpu_custom_call" | custom-call | flops 3221225472 | bytes 16777216 | tf_op jit(solution)/shard_map/output/pallas_call | solution.py:394
  422.8 0.5 collective-permute-start.6
  423.3 9.0 %output.5 = (f32[512,1024]{1,0:T(8,128)}, bf16[512,1024]{1,0:T(8,128)(2,1)}) custom-call(s32[1]{0:T(128)} %bitcast.t_ref, f32[12,1024,128]{2,1,0:T(8,128)} %row_scan.2.row_ref, bf16[512,1536]{1,0:T(8,128)(2,1)} %bitcast.35, bf16[512,1536]{1,0:T(8,128)(2,1)} %get-tuple-element.26.inner_ref, f32[1,1536]{1,0:T(1,128)} %reshape_reshape.3.skip_ref, ...), custom_call_target="tpu_custom_call" | custom-call | flops 3221225472 | bytes 16777216 | tf_op jit(solution)/shard_map/output/pallas_call | solution.py:394
  432.2 1.5 collective-permute-start.3
  433.8 1.1 copy-done
  434.9 8.9 %output.4 = (f32[512,1024]{1,0:T(8,128)}, bf16[512,1024]{1,0:T(8,128)(2,1)}) custom-call(s32[1]{0:T(128)} %bitcast.t_ref, f32[12,1024,128]{2,1,0:T(8,128)} %row_scan.2.row_ref, bf16[512,1536]{1,0:T(8,128)(2,1)} %bitcast.32, bf16[512,1536]{1,0:T(8,128)(2,1)} %get-tuple-element.23.inner_ref, f32[1,1536]{1,0:T(1,128)} %reshape_reshape.3.skip_ref, ...), custom_call_target="tpu_custom_call" | custom-call | flops 3221225472 | bytes 16777216 | tf_op jit(solution)/shard_map/output/pallas_call | solution.py:394
  443.8 0.5 collective-permute-start.2
  444.3 3.7 finish.4.rest_0_
  448.0 13.0 %collective-permute-done.6.got_ref = bf16[512,1024]{1,0:T(8,128)(2,1)S(1)} collective-permute-done((bf16[512,1024]{1,0:T(8,128)(2,1)}, bf16[512,1024]{1,0:T(8,128)(2,1)S(1)}, u32[]{:S(2)}, u32[]{:S(2)}) %collective-permute-start.6) | collective-permute-done | bytes 1048608 | tf_op jit(solution)/shard_map/ppermute | solution.py:491
  461.1 1.0 copy-done.7
  462.0 3.7 finish.5.rest_0_
  465.8 17.9 %collective-permute-done.3.got_ref = bf16[512,1024]{1,0:T(8,128)(2,1)} collective-permute-done((bf16[512,1024]{1,0:T(8,128)(2,1)}, bf16[512,1024]{1,0:T(8,128)(2,1)}, u32[]{:S(2)}, u32[]{:S(2)}) %collective-permute-start.3) | collective-permute-done | bytes 1048608 | tf_op jit(solution)/shard_map/ppermute | solution.py:491
  483.6 3.7 finish.6.rest_0_
  487.4 18.1 %collective-permute-done.2.got_ref = bf16[512,1024]{1,0:T(8,128)(2,1)S(1)} collective-permute-done((bf16[512,1024]{1,0:T(8,128)(2,1)}, bf16[512,1024]{1,0:T(8,128)(2,1)S(1)}, u32[]{:S(2)}, u32[]{:S(2)}) %collective-permute-start.2) | collective-permute-done | bytes 1048608 | tf_op jit(solution)/shard_map/ppermute | solution.py:491
  505.4 1.0 copy-done.8
  506.4 3.7 finish.7
  (32 shorter events, 0.1 us)
Async XLA Ops:
  0.0 5.8 %copy-start.13 = (bf16[2048,24]{0,1:T(8,128)(2,1)S(1)}, bf16[2048,24]{0,1:T(8,128)(2,1)}, u32[]{:S(2)}) copy-start(bf16[2048,24]{0,1:T(8,128)(2,1)} %param.14) | copy-start | bytes 294916
  0.0 6.1 %copy-start.17 = (f32[24]{0:T(128)S(1)}, f32[24]{0:T(128)}, u32[]{:S(2)}) copy-start(f32[24]{0:T(128)} %param.15) | copy-start | bytes 292
  0.0 6.1 %copy-start.16 = (f32[24]{0:T(128)S(1)}, f32[24]{0:T(128)}, u32[]{:S(2)}) copy-start(f32[24]{0:T(128)} %param.16) | copy-start | bytes 292
  0.0 6.7 %copy-start.6 = (bf16[2048,256]{1,0:T(8,128)(2,1)S(1)}, bf16[2048,256]{1,0:T(8,128)(2,1)}, u32[]{:S(2)}) copy-start(bf16[2048,256]{1,0:T(8,128)(2,1)} %param.13) | copy-start | bytes 3145732
  2.8 26.4 %collective-permute-start.4 = (bf16[512,1024]{1,0:T(8,128)(2,1)}, bf16[512,1024]{1,0:T(8,128)(2,1)S(1)}, u32[]{:S(2)}, u32[]{:S(2)}) collective-permute-start(bf16[512,1024]{1,0:T(8,128)(2,1)} %turn.6.own_ref), channel_id=1, source_target_pairs={{0,1},{1,0},{2,3},{3,2},{4,5},{5,4},{6,7},{7,6},{8,9},{9,8},{10,11... | collective-permute-start | bytes 3145736 | tf_op jit(solution)/shard_map/ppermute | solution.py:473
  29.2 1.0 copy-start.9
  40.4 45.7 %all-to-all-start.6 = ((bf16[16,4,8,1920]{3,2,1,0:T(8,128)(2,1)}), bf16[16,4,8,1920]{3,2,1,0:T(8,128)(2,1)S(1)}, u32[]{:S(2)}, u32[]{:S(2)}) async-start(bf16[16,4,8,1920]{3,2,1,0:T(8,128)(2,1)} %bitcast.36), calls=%async_computation.6 | async-start | bytes 3932160 | tf_op jit(solution)/shard_map/all_to_all | solution.py:480
  49.2 25.7 %collective-permute-start.5 = (bf16[512,1024]{1,0:T(8,128)(2,1)}, bf16[512,1024]{1,0:T(8,128)(2,1)S(1)}, u32[]{:S(2)}, u32[]{:S(2)}) collective-permute-start(bf16[512,1024]{1,0:T(8,128)(2,1)} %turn.7.own_ref), channel_id=1, source_target_pairs={{0,1},{1,0},{2,3},{3,2},{4,5},{5,4},{6,7},{7,6},{8,9},{9,8},{10,11... | collective-permute-start | bytes 3145736 | tf_op jit(solution)/shard_map/ppermute | solution.py:473
  74.9 1.0 copy-start.11
  86.1 1.3 copy-start.4
  87.4 49.4 %all-to-all-start.4 = ((bf16[16,4,8,1920]{3,2,1,0:T(8,128)(2,1)}), bf16[16,4,8,1920]{3,2,1,0:T(8,128)(2,1)}, u32[]{:S(2)}, u32[]{:S(2)}) async-start(bf16[16,4,8,1920]{3,2,1,0:T(8,128)(2,1)} %bitcast.37), calls=%async_computation.4 | async-start | bytes 3932160 | tf_op jit(solution)/shard_map/all_to_all | solution.py:480
  100.0 25.6 %collective-permute-start = (bf16[512,1024]{1,0:T(8,128)(2,1)}, bf16[512,1024]{1,0:T(8,128)(2,1)S(1)}, u32[]{:S(2)}, u32[]{:S(2)}) collective-permute-start(bf16[512,1024]{1,0:T(8,128)(2,1)} %turn.4.own_ref), channel_id=1, source_target_pairs={{0,1},{1,0},{2,3},{3,2},{4,5},{5,4},{6,7},{7,6},{8,9},{9,8},{10,11... | collective-permute-start | bytes 3145736 | tf_op jit(solution)/shard_map/ppermute | solution.py:473
  125.6 1.0 copy-start.12
  136.8 49.5 %all-to-all-start.2 = ((bf16[16,4,8,1920]{3,2,1,0:T(8,128)(2,1)}), bf16[16,4,8,1920]{3,2,1,0:T(8,128)(2,1)S(1)}, u32[]{:S(2)}, u32[]{:S(2)}) async-start(bf16[16,4,8,1920]{3,2,1,0:T(8,128)(2,1)} %bitcast.38), calls=%async_computation.2 | async-start | bytes 3932160 | tf_op jit(solution)/shard_map/all_to_all | solution.py:480
  149.4 25.7 %collective-permute-start.1 = (bf16[512,1024]{1,0:T(8,128)(2,1)}, bf16[512,1024]{1,0:T(8,128)(2,1)S(1)}, u32[]{:S(2)}, u32[]{:S(2)}) collective-permute-start(bf16[512,1024]{1,0:T(8,128)(2,1)} %turn.5.own_ref), channel_id=1, source_target_pairs={{0,1},{1,0},{2,3},{3,2},{4,5},{5,4},{6,7},{7,6},{8,9},{9,8},{10,11... | collective-permute-start | bytes 3145736 | tf_op jit(solution)/shard_map/ppermute | solution.py:473
  175.1 1.0 copy-start.10
  186.3 1.3 copy-start.5
  187.6 48.6 %all-to-all-start = ((bf16[16,4,8,1920]{3,2,1,0:T(8,128)(2,1)}), bf16[16,4,8,1920]{3,2,1,0:T(8,128)(2,1)}, u32[]{:S(2)}, u32[]{:S(2)}) async-start(bf16[16,4,8,1920]{3,2,1,0:T(8,128)(2,1)} %bitcast.39), calls=%async_computation | async-start | bytes 3932160 | tf_op jit(solution)/shard_map/all_to_all | solution.py:480
  236.2 42.5 %all-to-all-start.7 = ((bf16[16,4,8,1536]{3,2,1,0:T(8,128)(2,1)}), bf16[16,4,8,1536]{3,2,1,0:T(8,128)(2,1)S(1)}, u32[]{:S(2)}, u32[]{:S(2)}) async-start(bf16[16,4,8,1536]{3,2,1,0:T(8,128)(2,1)} %column_scan.7), calls=%async_computation.7 | async-start | bytes 3145728 | tf_op jit(solution)/shard_map/all_to_all | solution.py:487
  278.7 16.2 %copy-start.1 = (bf16[16,4,8,1536]{3,2,1,0:T(8,128)(2,1)}, bf16[16,4,8,1536]{3,2,1,0:T(8,128)(2,1)S(1)}, u32[]{:S(2)}) copy-start(bf16[16,4,8,1536]{3,2,1,0:T(8,128)(2,1)S(1)} %all-to-all-done.7) | copy-start | bytes 4718596
  278.7 41.0 %all-to-all-start.5 = ((bf16[16,4,8,1536]{3,2,1,0:T(8,128)(2,1)}), bf16[16,4,8,1536]{3,2,1,0:T(8,128)(2,1)S(1)}, u32[]{:S(2)}, u32[]{:S(2)}) async-start(bf16[16,4,8,1536]{3,2,1,0:T(8,128)(2,1)} %column_scan.6), calls=%async_computation.5 | async-start | bytes 3145728 | tf_op jit(solution)/shard_map/all_to_all | solution.py:487
  319.7 16.2 %copy-start.2 = (bf16[16,4,8,1536]{3,2,1,0:T(8,128)(2,1)}, bf16[16,4,8,1536]{3,2,1,0:T(8,128)(2,1)S(1)}, u32[]{:S(2)}) copy-start(bf16[16,4,8,1536]{3,2,1,0:T(8,128)(2,1)S(1)} %all-to-all-done.5) | copy-start | bytes 4718596
  319.7 41.0 %all-to-all-start.3 = ((bf16[16,4,8,1536]{3,2,1,0:T(8,128)(2,1)}), bf16[16,4,8,1536]{3,2,1,0:T(8,128)(2,1)S(1)}, u32[]{:S(2)}, u32[]{:S(2)}) async-start(bf16[16,4,8,1536]{3,2,1,0:T(8,128)(2,1)} %column_scan.5), calls=%async_computation.3 | async-start | bytes 3145728 | tf_op jit(solution)/shard_map/all_to_all | solution.py:487
  335.9 33.9 %copy-start.15 = (f32[24]{0:T(128)S(1)}, f32[24]{0:T(128)}, u32[]{:S(2)}) copy-start(f32[24]{0:T(128)} %param.17) | copy-start | bytes 292
  335.9 34.6 %copy-start.14 = (f32[1536]{0:T(1024)S(1)}, f32[1536]{0:T(1024)}, u32[]{:S(2)}) copy-start(f32[1536]{0:T(1024)} %param.18) | copy-start | bytes 18436
  360.6 26.6 %copy-start.3 = (bf16[16,4,8,1536]{3,2,1,0:T(8,128)(2,1)}, bf16[16,4,8,1536]{3,2,1,0:T(8,128)(2,1)S(1)}, u32[]{:S(2)}) copy-start(bf16[16,4,8,1536]{3,2,1,0:T(8,128)(2,1)S(1)} %all-to-all-done.3) | copy-start | bytes 4718596
  360.6 73.1 %all-to-all-start.1 = ((bf16[16,4,8,1536]{3,2,1,0:T(8,128)(2,1)}), bf16[16,4,8,1536]{3,2,1,0:T(8,128)(2,1)S(1)}, u32[]{:S(2)}, u32[]{:S(2)}) async-start(bf16[16,4,8,1536]{3,2,1,0:T(8,128)(2,1)} %column_scan.4), calls=%async_computation.1 | async-start | bytes 3145728 | tf_op jit(solution)/shard_map/all_to_all | solution.py:487
  412.3 32.0 %collective-permute-start.7 = (bf16[512,1024]{1,0:T(8,128)(2,1)}, bf16[512,1024]{1,0:T(8,128)(2,1)}, u32[]{:S(2)}, u32[]{:S(2)}) collective-permute-start(bf16[512,1024]{1,0:T(8,128)(2,1)} %get-tuple-element.36), channel_id=1, source_target_pairs={{0,1},{1,0},{2,3},{3,2},{4,5},{5,4},{6,7},{7,6},{8,9},{9,8},{10,11... | collective-permute-start | bytes 3145736 | tf_op jit(solution)/shard_map/ppermute | solution.py:491
  422.8 38.3 %collective-permute-start.6 = (bf16[512,1024]{1,0:T(8,128)(2,1)}, bf16[512,1024]{1,0:T(8,128)(2,1)S(1)}, u32[]{:S(2)}, u32[]{:S(2)}) collective-permute-start(bf16[512,1024]{1,0:T(8,128)(2,1)} %get-tuple-element.33), channel_id=1, source_target_pairs={{0,1},{1,0},{2,3},{3,2},{4,5},{5,4},{6,7},{7,6},{8,9},{9,8},{10,11... | collective-permute-start | bytes 3145736 | tf_op jit(solution)/shard_map/ppermute | solution.py:491
  432.2 51.4 %collective-permute-start.3 = (bf16[512,1024]{1,0:T(8,128)(2,1)}, bf16[512,1024]{1,0:T(8,128)(2,1)}, u32[]{:S(2)}, u32[]{:S(2)}) collective-permute-start(bf16[512,1024]{1,0:T(8,128)(2,1)} %get-tuple-element.28), channel_id=1, source_target_pairs={{0,1},{1,0},{2,3},{3,2},{4,5},{5,4},{6,7},{7,6},{8,9},{9,8},{10,11... | collective-permute-start | bytes 3145736 | tf_op jit(solution)/shard_map/ppermute | solution.py:491
  433.8 1.1 copy-start
  443.8 61.6 %collective-permute-start.2 = (bf16[512,1024]{1,0:T(8,128)(2,1)}, bf16[512,1024]{1,0:T(8,128)(2,1)S(1)}, u32[]{:S(2)}, u32[]{:S(2)}) collective-permute-start(bf16[512,1024]{1,0:T(8,128)(2,1)} %get-tuple-element.25), channel_id=1, source_target_pairs={{0,1},{1,0},{2,3},{3,2},{4,5},{5,4},{6,7},{7,6},{8,9},{9,8},{10,11... | collective-permute-start | bytes 3145736 | tf_op jit(solution)/shard_map/ppermute | solution.py:491
  461.1 1.0 copy-start.7
  505.4 1.0 copy-start.8

commit v2 on v1

--- a/solution.py
+++ b/solution.py
@@ -120,24 +120,33 @@
         out_ref[:, part] = held[lane].astype(jnp.bfloat16)
 
 
-def turn(tokens, image, part, width):
-    _, rows, _, feats = tokens.shape
-    step = width // 2
+def turn(tokens, start, count):
+    _, rows, columns, feats = tokens.shape
+    step = columns // HALVES // 2
     return pl.pallas_call(
         functools.partial(turn_kernel, rows),
-        grid=(2,),
-        in_specs=[
-            pl.BlockSpec((1, rows, step, feats), lambda k: (image, 0, 2 * part + k, 0)),
-        ],
+        grid=(2 * count,),
+        in_specs=[grid_block(tokens, start)],
         out_specs=pl.BlockSpec((step * rows, feats), lambda k: (k, 0)),
-        out_shape=jax.ShapeDtypeStruct((width * rows, feats), jnp.bfloat16),
+        out_shape=jax.ShapeDtypeStruct((2 * count * step * rows, feats), jnp.bfloat16),
         scratch_shapes=[pltpu.VMEM((feats // LANES, step * rows, LANES), jnp.float32)],
         compiler_params=params(),
         cost_estimate=pl.CostEstimate(
-            flops=0, transcendentals=0, bytes_accessed=6 * width * rows * feats
+            flops=0, transcendentals=0, bytes_accessed=12 * count * step * rows * feats
         ),
         name="turn",
     )(tokens)
+
+
+def grid_block(tokens, start):
+    _, rows, columns, feats = tokens.shape
+    per_image = 2 * HALVES
+
+    def place(k):
+        at = 2 * start + k
+        return at // per_image, 0, at % per_image, 0
+
+    return pl.BlockSpec((1, rows, columns // per_image, feats), place)
 
 
 def project_kernel(
@@ -161,8 +170,14 @@
     small = project(m_own[0], m_other[0])
     wide = inner_ref.shape[1]
     step = jax.nn.softplus(small[:, 2 * STATE :] + bias_ref[...])
-    pack_ref[:, wide : wide + 2 * STATE] = small[:, : 2 * STATE].astype(jnp.bfloat16)
-    pack_ref[:, wide + 2 * STATE :] = (-rate_ref[...] * step).astype(jnp.bfloat16)
+    blocks = pack_ref.shape[:2]
+
+    def put(start, block):
+        lanes = block.shape[1]
+        pack_ref[:, :, start : start + lanes] = block.astype(jnp.bfloat16).reshape(blocks + (lanes,))
+
+    put(wide, small[:, : 2 * STATE])
+    put(wide + 2 * STATE, -rate_ref[...] * step)
     inner = project(w_own[0], w_other[0]).astype(jnp.bfloat16)
     inner_ref[...] = inner
     rows = inner.shape[0]
@@ -172,14 +187,15 @@
         spread = jnp.where(
             low, step[:, 2 * pair : 2 * pair + 1], step[:, 2 * pair + 1 : 2 * pair + 2]
         )
-        pack_ref[:, part] = (inner[:, part].astype(jnp.float32) * spread).astype(jnp.bfloat16)
-
-
-def project(own, other, in_gain, w_inner, w_small, bias, rate, place, heads):
+        put(pair * LANES, inner[:, part].astype(jnp.float32) * spread)
+
+
+def project(own, other, in_gain, w_inner, w_small, bias, rate, place, heads, owners, count):
     rows, feats = own.shape
     wide = w_inner.shape[1]
     small = w_small.shape[1]
-    tile = min(rows, 256)
+    tile = rows // (2 * count)
+    depth = 2 * tile // owners
     gains = in_gain.reshape(2, 1, feats)
     w_inner = w_inner.reshape(2, feats, wide)
     w_small = w_small.reshape(2, feats, small)
@@ -204,12 +220,12 @@
             + [resident((1, LANES), lambda i, t: (0, 0))] * 2,
             out_specs=[
                 pl.BlockSpec((tile, wide), lambda i, t: (i, 0)),
-                pl.BlockSpec((tile, packed), lambda i, t: (i, 0)),
+                pl.BlockSpec((owners // 2, depth, packed), lambda i, t: (i % 2, i // 2, 0)),
             ],
         ),
         out_shape=[
             jax.ShapeDtypeStruct((rows, wide), jnp.bfloat16),
-            jax.ShapeDtypeStruct((rows, packed), jnp.bfloat16),
+            jax.ShapeDtypeStruct((owners, count * depth, packed), jnp.bfloat16),
         ],
         compiler_params=params(),
         cost_estimate=pl.CostEstimate(
@@ -261,7 +277,7 @@
 
 
 def column_kernel(heads, pack_ref, out_ref):
-    owners, _, rows, packed = pack_ref.shape
+    owners, _, rows, _ = pack_ref.shape
     length = owners * rows
     wide = out_ref.shape[3]
 
@@ -308,19 +324,24 @@
     )(pack)
 
 
-def row_kernel(rows, heads, *refs):
+def row_kernel(rows, heads, counts, *refs):
     packs, out_ref, held = refs[:-2], refs[-2], refs[-1]
-    row = pl.program_id(0)
+    image, row = pl.program_id(0), pl.program_id(1)
     wide = heads * HEAD_DIM
-    tall = packs[0].shape[0]
-    length = tall * len(packs) // rows
-
-    @pl.when(row == 0)
-    def _():
-        for k, pack in enumerate(packs):
-            for lane in range(pack.shape[1] // LANES):
-                part = slice(lane * LANES, (lane + 1) * LANES)
-                held[lane, k * tall : (k + 1) * tall, :] = pack[:, part].astype(jnp.float32)
+    tall = held.shape[1] // HALVES
+    length = held.shape[1] // rows
+    units = [(pack, k) for pack, count in zip(packs, counts) for k in range(count)]
+
+    for u, (pack, k) in enumerate(units):
+
+        @pl.when((row == 0) & (image == u // HALVES))
+        def _(pack=pack, k=k, half=u % HALVES):
+            depth = tall // pack.shape[0]
+            for lane in range(pack.shape[2] // LANES):
+                block = pack[:, k * depth : (k + 1) * depth, lane * LANES : (lane + 1) * LANES]
+                held[lane, half * tall : (half + 1) * tall, :] = block.reshape(
+                    tall, LANES
+                ).astype(jnp.float32)
 
     def take(lane):
         return held[lane, pl.ds(row, length, stride=rows), :]
@@ -340,25 +361,25 @@
     )
 
 
-def row_scan(packs, rows, heads):
-    tall, packed = packs[0].shape
-    total = tall * len(packs)
+def row_scan(packs, counts, images, rows, columns, heads):
+    packed = packs[0].shape[2]
+    total = rows * columns
     wide = heads * HEAD_DIM
     return pl.pallas_call(
-        functools.partial(row_kernel, rows, heads),
-        grid=(rows,),
-        in_specs=[resident((tall, packed), lambda r: (0, 0))] * len(packs),
-        out_specs=resident((wide // LANES, total, LANES), lambda r: (0, 0, 0)),
-        out_shape=jax.ShapeDtypeStruct((wide // LANES, total, LANES), jnp.float32),
+        functools.partial(row_kernel, rows, heads, counts),
+        grid=(images, rows),
+        in_specs=[resident(pack.shape, lambda i, r: (0, 0, 0)) for pack in packs],
+        out_specs=pl.BlockSpec((wide // LANES, total, LANES), lambda i, r: (0, i, 0)),
+        out_shape=jax.ShapeDtypeStruct((wide // LANES, images * total, LANES), jnp.float32),
         scratch_shapes=[pltpu.VMEM((packed // LANES, total, LANES), jnp.float32)],
         compiler_params=params(),
-        cost_estimate=scan_cost(rows, total // rows, heads),
+        cost_estimate=scan_cost(images * rows, columns, heads),
         name="row_scan",
     )(*packs)
 
 
 def output_kernel(t_ref, row_ref, col_ref, inner_ref, skip_ref, gain_ref, w_own, w_other, own_ref, send_ref):
-    wide = inner_ref.shape[1]
+    tall, wide = inner_ref.shape
     group = NORM_HEADS * HEAD_DIM
     gated = []
     for start in range(0, wide, group):
@@ -368,7 +389,7 @@
             part = slice(lane, lane + LANES)
             total = (
                 row_ref[lane // LANES]
-                + col_ref[:, part].astype(jnp.float32)
+                + col_ref[:, :, part].astype(jnp.float32).reshape(tall, LANES)
                 + skip_ref[:, part] * inner_ref[:, part].astype(jnp.float32)
             )
             parts.append(total)
@@ -384,10 +405,12 @@
     own_ref[...] = jnp.dot(gated, w_own[...], preferred_element_type=jnp.float32)
 
 
-def output(row_out, part, col, inner, skip, gain, w_out, place):
+def output(row_out, start, count, col, inner, skip, gain, w_out, place):
     rows, wide = inner.shape
     feats = w_out.shape[1] // 2
-    tile = min(rows, 256)
+    depth = col.shape[1] // count
+    owners = col.shape[0]
+    tile = owners * depth // 2
     steps = rows // tile
     row_spec = pl.BlockSpec((tile, wide), lambda i, t: (i, 0))
     out_spec = pl.BlockSpec((tile, feats), lambda i, t: (i, 0))
@@ -397,8 +420,8 @@
             num_scalar_prefetch=1,
             grid=(steps,),
             in_specs=[
-                pl.BlockSpec((wide // LANES, tile, LANES), lambda i, t: (0, part * steps + i, 0)),
-                row_spec,
+                pl.BlockSpec((wide // LANES, tile, LANES), lambda i, t: (0, 2 * start + i, 0)),
+                pl.BlockSpec((owners // 2, depth, wide), lambda i, t: (i % 2, i // 2, 0)),
                 row_spec,
                 resident((1, wide), lambda i, t: (0, 0)),
                 resident((1, wide), lambda i, t: (0, 0)),
@@ -431,23 +454,23 @@
             ).astype(jnp.bfloat16)
 
 
-def finish(own, got, tokens, image, part, width, earlier):
-    _, rows, _, feats = tokens.shape
-    step = width // 2
+def finish(own, got, tokens, start, count, earlier):
+    _, rows, columns, feats = tokens.shape
+    step = columns // HALVES // 2
     flat = pl.BlockSpec((step * rows, feats), lambda k: (k, 0))
-    grid_block = pl.BlockSpec((1, rows, step, feats), lambda k: (image, 0, 2 * part + k, 0))
     chained = [] if earlier is None else [earlier]
     return pl.pallas_call(
         functools.partial(finish_kernel, rows),
-        grid=(2,),
-        in_specs=[flat, flat, grid_block] + [pl.BlockSpec(memory_space=pl.ANY)] * len(chained),
-        out_specs=grid_block,
+        grid=(2 * count,),
+        in_specs=[flat, flat, grid_block(tokens, start)]
+        + [pl.BlockSpec(memory_space=pl.ANY)] * len(chained),
+        out_specs=grid_block(tokens, start),
         out_shape=jax.ShapeDtypeStruct(tokens.shape, jnp.bfloat16),
         scratch_shapes=[pltpu.VMEM((feats // LANES, step * rows, LANES), jnp.float32)],
         input_output_aliases={3: 0} if chained else {},
         compiler_params=params(),
         cost_estimate=pl.CostEstimate(
-            flops=0, transcendentals=0, bytes_accessed=12 * width * rows * feats
+            flops=0, transcendentals=0, bytes_accessed=24 * count * step * rows * feats
         ),
         name="finish",
     )(own, got, tokens, *chained)
@@ -456,10 +479,9 @@
 def pipelined(
     owners, tokens, in_gain, w_inner, w_bc, w_step, step_bias, decay_rate, skip, norm_gain, w_out
 ):
-    images, rows, columns, feats = tokens.shape
+    images, rows, columns, _ = tokens.shape
     heads = w_step.shape[1]
     wide = w_inner.shape[1]
-    width = columns // HALVES
     swap = [(0, 1), (1, 0)]
     place = lax.axis_index("tensor").astype(jnp.int32).reshape(1)
     pad = LANES - heads
@@ -468,36 +490,47 @@
     rate = jnp.pad(decay_rate, (0, pad)).reshape(1, LANES)
     skip_wide = jnp.repeat(skip, HEAD_DIM).reshape(1, wide)
     gain = norm_gain.reshape(1, wide)
-    chunks = [(image, part) for image in range(images) for part in range(HALVES)]
-    own = [turn(tokens, image, part, width) for image, part in chunks]
-    other = [lax.ppermute(block, "tensor", swap) for block in own]
-    inner, packs, arrived = [], [], []
-    for k in range(len(chunks)):
-        a, b = project(own[k], other[k], in_gain, w_inner, w_small, bias, rate, place, heads)
+    counts = (1, images * HALVES - 2, 1)
+    starts = (0, 1, images * HALVES - 1)
+    groups = range(len(counts))
+    own, other, inner, packs, arrived, columns_out = [], [], [], [], [], []
+    for g in groups:
+        own.append(turn(tokens, starts[g], counts[g]))
+    for g in groups:
+        other.append(lax.ppermute(own[g], "tensor", swap))
+    for g in groups:
+        a, b = project(
+            own[g], other[g], in_gain, w_inner, w_small, bias, rate, place, heads, owners, counts[g]
+        )
         inner.append(a)
         packs.append(b)
-        sent = b.reshape(owners, width // owners, rows, b.shape[1])
-        arrived.append(lax.all_to_all(sent, "space", split_axis=0, concat_axis=0, tiled=True))
-    row_out = [
-        row_scan(packs[image * HALVES : (image + 1) * HALVES], rows, heads)
-        for image in range(images)
-    ]
+        arrived.append(lax.all_to_all(b, "space", split_axis=0, concat_axis=0, tiled=True))
+    for g in groups:
+        block = arrived[g]
+        shape = (owners, block.shape[1] // rows, rows, block.shape[2])
+        columns_out.append(
+            column_scan(block.reshape(shape), heads).reshape(owners, block.shape[1], wide)
+        )
+    row_out = row_scan(packs, counts, images, rows, columns, heads)
     result = None
-    for k, (image, part) in enumerate(chunks):
-        back = lax.all_to_all(
-            column_scan(arrived[k], heads), "space", split_axis=0, concat_axis=0, tiled=True
-        ).reshape(width * rows, wide)
-        kept, send = output(row_out[image], part, back, inner[k], skip_wide, gain, w_out, place)
+    for g in ORDER:
+        back = lax.all_to_all(columns_out[g], "space", split_axis=0, concat_axis=0, tiled=True)
+        kept, send = output(
+            row_out, starts[g], counts[g], back, inner[g], skip_wide, gain, w_out, place
+        )
         got = lax.ppermute(send, "tensor", swap)
-        result = finish(kept, got, tokens, image, part, width, result)
+        result = finish(kept, got, tokens, starts[g], counts[g], result)
     return result
 
 
-def dispatch(owners, tensor, tokens, *rest):
-    heads = rest[3].shape[1]
-    rows, columns = tokens.shape[1:3]
-    fits = (
+ORDER = (1, 0, 2)
+
+
+def fits(owners, tensor, tokens, heads):
+    images, rows, columns, _ = tokens
+    return (
         tensor == 2
+        and images * HALVES > 2
         and rows == SUBLANES
         and columns % (HALVES * owners) == 0
         and owners * rows == columns == LANES
@@ -506,7 +539,10 @@
         and heads <= LANES
         and STATE == LANES == 2 * HEAD_DIM
     )
-    if fits:
+
+
+def dispatch(owners, tensor, tokens, *rest):
+    if fits(owners, tensor, tokens.shape, rest[3].shape[1]):
         return pipelined(owners, tokens, *rest)
     return on_device(tokens, *rest)
 

time: 511 us -> 521 us (1.020)
  waiting for transfers between devices: 248 us -> 289 us
  Pallas kernels: 163 us -> 148 us
  starting transfers between devices: 85.4 us -> 74.5 us
    all_to_all x8 -> x6, waiting for transfers between devices: 106 us -> 138 us  [the longest x3 71.7 us: pipelined(): lax.all_to_all(columns_out[g], 'space', split_axis=0, concat_axis=0, tile...]
    ppermute x4 -> x3, waiting for transfers between devices: 48.9 us -> 59.2 us  [pipelined(): got = lax.ppermute(send, 'tensor', swap)]
    all_to_all x8 -> x6, starting transfers between devices: 73.7 us -> 64.8 us  [the longest x3 43.2 us: pipelined(): lax.all_to_all(columns_out[g], 'space', split_axis=0, concat_axis=0, tile...]
    pallas_call x4 -> x3, Pallas kernels: 40.9 us -> 36.3 us  [project(): pl.pallas_call(functools.partial(project_kernel, 2 * feats, heads), grid_...]
    pallas_call x4 -> x3, Pallas kernels: 35.7 us -> 31.2 us  [output(): pl.pallas_call(output_kernel, grid_spec=pltpu.PrefetchScalarGridSpec(num_...]
    pallas_call x10 -> x7, Pallas kernels: 58.1 us -> 53.8 us  [the longest x1 29.6 us: row_scan(): pl.pallas_call(functools.partial(row_kernel, rows, heads, counts), grid=(...]
    pallas_call x4 -> x3, Pallas kernels: 28.4 us -> 26.4 us  [column_scan(): pl.pallas_call(functools.partial(column_kernel, heads), grid=(columns,),...]
    ppermute x4 -> x3, waiting for transfers between devices: 93.5 us -> 92 us  [pipelined(): other.append(lax.ppermute(own[g], 'tensor', swap))]
  transfers between devices with their start and end apart: 16 -> 12, of which waited for: 11 -> 9; matrix products, arithmetic and copies ran while one was open for 1% -> 1% of each run, Pallas kernels for 29% -> 25%
where the time goes in v2:
time: 521 us; the launch traced here: 520 us
  waiting for transfers between devices  289 us (55%)
  Pallas kernels  148 us (28%)
  starting transfers between devices  74.5 us (14%)
  local copies, waits for them, and re-layouts  7.74 us (1%)
    ppermute x3, waiting for transfers between devices, pipelined(): other.append(lax.ppermute(own[g], 'tensor', swap))  92 us
    all_to_all x3, waiting for transfers between devices, pipelined(): lax.all_to_all(columns_out[g], 'space', split_axis=0, concat_axis=0, tile...  71.7 us
    all_to_all x3, waiting for transfers between devices, pipelined(): lax.all_to_all(b, 'space', split_axis=0, concat_axis=0, tiled=True)  65.9 us
    ppermute x3, waiting for transfers between devices, pipelined(): got = lax.ppermute(send, 'tensor', swap)  59.2 us
    all_to_all x3, starting transfers between devices, pipelined(): lax.all_to_all(columns_out[g], 'space', split_axis=0, concat_axis=0, tile...  43.2 us
    pallas_call x3, Pallas kernels, project(): pl.pallas_call(functools.partial(project_kernel, 2 * feats, heads), grid_...  36.3 us
    pallas_call x3, Pallas kernels, output(): pl.pallas_call(output_kernel, grid_spec=pltpu.PrefetchScalarGridSpec(num_...  31.2 us
    pallas_call x1, Pallas kernels, row_scan(): pl.pallas_call(functools.partial(row_kernel, rows, heads, counts), grid=(...  29.6 us
  transfers between devices with their start and end apart: 12, of which 9 were waited for; matrix products, arithmetic and copies ran while one was open for 1% of the time, Pallas kernels for 25%

profile of v2, /device:TPU:0, one launch (start us, length us, event | category | flops | bytes accessed | tf_op | source)
XLA Modules:
  0.0 520.2 jit_solution(2484107347028908491)
XLA Ops:
  0.0 0.0 copy-start.8
  0.0 0.0 copy-start.11
  0.0 0.0 copy-start.12
  0.0 0.0 copy-start.4
  0.0 2.8 turn.5.own_ref
  2.8 3.1 collective-permute-start.2
  5.9 0.0 copy-done.8
  5.9 0.3 copy.14
  6.2 0.0 copy-done.11
  6.2 0.0 copy-done.12
  6.2 0.6 pad_bitcast_fusion
  6.7 0.0 copy-done.4
  6.8 1.3 fusion.1
  8.1 21.2 %collective-permute-done.2.other_ref = bf16[512,1024]{1,0:T(8,128)(2,1)S(1)} collective-permute-done((bf16[512,1024]{1,0:T(8,128)(2,1)}, bf16[512,1024]{1,0:T(8,128)(2,1)S(1)}, u32[]{:S(2)}, u32[]{:S(2)}) %collective-permute-start.2) | collective-permute-done | bytes 1048608 | tf_op jit(solution)/shard_map/ppermute | solution.py:500
  29.2 1.0 copy-done.6
  30.2 10.2 %project.5 = (bf16[512,1536]{1,0:T(8,128)(2,1)}, bf16[16,32,1920]{2,1,0:T(8,128)(2,1)}) custom-call(s32[1]{0:T(128)} %bitcast.t_ref, bf16[512,1024]{1,0:T(8,128)(2,1)} %turn.5.own_ref, bf16[512,1024]{1,0:T(8,128)(2,1)} %copy-done.6, f32[2,1,1024]{2,1,0:T(1,128)} %bitcast.30, f32[2,1,1024]{2,1,0:T(1,128)} %bitcast.31, bf16[2,1024,1536]{2,1,0:T(8,128)(2,1)} %bitcast.14, ...), custom_call_target="tpu_custom_call" | custom-call | flops 4026531840 | bytes 20971520 | tf_op jit(solution)/shard_map/project/pallas_call | solution.py:211
  40.5 6.1 %all-to-all-start = ((bf16[16,32,1920]{2,1,0:T(8,128)(2,1)}), bf16[16,32,1920]{2,1,0:T(8,128)(2,1)S(1)}, u32[]{:S(2)}, u32[]{:S(2)}) async-start(bf16[16,32,1920]{2,1,0:T(8,128)(2,1)} %get-tuple-element.19.refs_2_), calls=%async_computation | async-start | bytes 3932160 | tf_op jit(solution)/shard_map/all_to_all | solution.py:507
  46.6 2.7 turn.3.own_ref
  49.3 1.5 collective-permute-start
  50.9 24.2 %collective-permute-done.other_ref = bf16[512,1024]{1,0:T(8,128)(2,1)S(1)} collective-permute-done((bf16[512,1024]{1,0:T(8,128)(2,1)}, bf16[512,1024]{1,0:T(8,128)(2,1)S(1)}, u32[]{:S(2)}, u32[]{:S(2)}) %collective-permute-start) | collective-permute-done | bytes 1048608 | tf_op jit(solution)/shard_map/ppermute | solution.py:500
  75.0 1.0 copy-done.7
  76.0 10.2 %project.3 = (bf16[512,1536]{1,0:T(8,128)(2,1)}, bf16[16,32,1920]{2,1,0:T(8,128)(2,1)}) custom-call(s32[1]{0:T(128)} %bitcast.t_ref, bf16[512,1024]{1,0:T(8,128)(2,1)} %turn.3.own_ref, bf16[512,1024]{1,0:T(8,128)(2,1)} %copy-done.7, f32[2,1,1024]{2,1,0:T(1,128)} %bitcast.32, f32[2,1,1024]{2,1,0:T(1,128)} %bitcast.33, bf16[2,1024,1536]{2,1,0:T(8,128)(2,1)} %bitcast.16, ...), custom_call_target="tpu_custom_call" | custom-call | flops 4026531840 | bytes 20971520 | tf_op jit(solution)/shard_map/project/pallas_call | solution.py:211
  86.3 0.0 all-to-all-done
  86.3 0.0 copy-start.3
  86.3 9.8 %all-to-all-start.2 = ((bf16[16,32,1920]{2,1,0:T(8,128)(2,1)}), bf16[16,32,1920]{2,1,0:T(8,128)(2,1)}, u32[]{:S(2)}, u32[]{:S(2)}) async-start(bf16[16,32,1920]{2,1,0:T(8,128)(2,1)} %get-tuple-element.17.refs_0_), calls=%async_computation.2 | async-start | bytes 3932160 | tf_op jit(solution)/shard_map/all_to_all | solution.py:507
  96.1 4.8 turn.4.own_ref
  100.8 0.0 copy-done.3
  100.8 1.5 collective-permute-start.1
  102.4 46.7 %collective-permute-done.1.other_ref = bf16[1024,1024]{1,0:T(8,128)(2,1)} collective-permute-done((bf16[1024,1024]{1,0:T(8,128)(2,1)}, bf16[1024,1024]{1,0:T(8,128)(2,1)}, u32[]{:S(2)}, u32[]{:S(2)}) %collective-permute-start.1) | collective-permute-done | bytes 2097184 | tf_op jit(solution)/shard_map/ppermute | solution.py:500
  149.1 15.8 %project.4 = (bf16[1024,1536]{1,0:T(8,128)(2,1)}, bf16[16,64,1920]{2,1,0:T(8,128)(2,1)}) custom-call(s32[1]{0:T(128)} %bitcast.t_ref, bf16[1024,1024]{1,0:T(8,128)(2,1)} %turn.4.own_ref, bf16[1024,1024]{1,0:T(8,128)(2,1)} %collective-permute-done.1.other_ref, f32[2,1,1024]{2,1,0:T(1,128)} %bitcast.34, f32[2,1,1024]{2,1,0:T(1,128)} %bitcast.35, ...), custom_call_target="tpu_custom_call" | custom-call | flops 8053063680 | bytes 20971520 | tf_op jit(solution)/shard_map/project/pallas_call | solution.py:211
  164.9 0.0 all-to-all-done.2
  164.9 5.8 %all-to-all-start.4 = ((bf16[16,64,1920]{2,1,0:T(8,128)(2,1)}), bf16[16,64,1920]{2,1,0:T(8,128)(2,1)}, u32[]{:S(2)}, u32[]{:S(2)}) async-start(bf16[16,64,1920]{2,1,0:T(8,128)(2,1)} %get-tuple-element.18.refs_1_), calls=%async_computation.4 | async-start | bytes 7864320 | tf_op jit(solution)/shard_map/all_to_all | solution.py:507
  170.7 7.1 %column_scan.4 = bf16[16,4,8,1536]{3,2,1,0:T(8,128)(2,1)} custom-call(bf16[16,4,8,1920]{3,2,1,0:T(8,128)(2,1)} %bitcast.8.pack_ref), custom_call_target="tpu_custom_call" | custom-call | flops 1610612736 | bytes 4718592 | tf_op jit(solution)/shard_map/column_scan/pallas_call | solution.py:315
  177.7 65.9 %all-to-all-done.4 = bf16[16,64,1920]{2,1,0:T(8,128)(2,1)} async-done(((bf16[16,64,1920]{2,1,0:T(8,128)(2,1)}), bf16[16,64,1920]{2,1,0:T(8,128)(2,1)}, u32[]{:S(2)}, u32[]{:S(2)}) %all-to-all-start.4) | async-done | bytes 3932192 | tf_op jit(solution)/shard_map/all_to_all | solution.py:507
  243.7 18.6 %all-to-all-start.3 = ((bf16[16,32,1536]{2,1,0:T(8,128)(2,1)}), bf16[16,32,1536]{2,1,0:T(8,128)(2,1)S(1)}, u32[]{:S(2)}, u32[]{:S(2)}) async-start(bf16[16,32,1536]{2,1,0:T(8,128)(2,1)} %bitcast.29), calls=%async_computation.3 | async-start | bytes 3145728 | tf_op jit(solution)/shard_map/all_to_all | solution.py:517
  262.3 12.3 %column_scan.5 = bf16[16,8,8,1536]{3,2,1,0:T(8,128)(2,1)} custom-call(bf16[16,8,8,1920]{3,2,1,0:T(8,128)(2,1)} %bitcast.10.pack_ref), custom_call_target="tpu_custom_call" | custom-call | flops 3221225472 | bytes 9437184 | tf_op jit(solution)/shard_map/column_scan/pallas_call | solution.py:315
  274.6 19.5 %all-to-all-done.3.col_ref = bf16[16,32,1536]{2,1,0:T(8,128)(2,1)S(1)} async-done(((bf16[16,32,1536]{2,1,0:T(8,128)(2,1)}), bf16[16,32,1536]{2,1,0:T(8,128)(2,1)S(1)}, u32[]{:S(2)}, u32[]{:S(2)}) %all-to-all-start.3) | async-done | bytes 1572896 | tf_op jit(solution)/shard_map/all_to_all | solution.py:517
  294.1 1.1 copy-done.1
  295.2 9.1 %all-to-all-start.5 = ((bf16[16,64,1536]{2,1,0:T(8,128)(2,1)}), bf16[16,64,1536]{2,1,0:T(8,128)(2,1)S(1)}, u32[]{:S(2)}, u32[]{:S(2)}) async-start(bf16[16,64,1536]{2,1,0:T(8,128)(2,1)} %bitcast.26), calls=%async_computation.5 | async-start | bytes 6291456 | tf_op jit(solution)/shard_map/all_to_all | solution.py:517
  304.4 7.1 %column_scan.3 = bf16[16,4,8,1536]{3,2,1,0:T(8,128)(2,1)} custom-call(bf16[16,4,8,1920]{3,2,1,0:T(8,128)(2,1)} %bitcast.27), custom_call_target="tpu_custom_call" | custom-call | flops 1610612736 | bytes 4718592 | tf_op jit(solution)/shard_map/column_scan/pallas_call | solution.py:315
  311.4 52.2 %all-to-all-done.5.col_ref = bf16[16,64,1536]{2,1,0:T(8,128)(2,1)S(1)} async-done(((bf16[16,64,1536]{2,1,0:T(8,128)(2,1)}), bf16[16,64,1536]{2,1,0:T(8,128)(2,1)S(1)}, u32[]{:S(2)}, u32[]{:S(2)}) %all-to-all-start.5) | async-done | bytes 3145760 | tf_op jit(solution)/shard_map/all_to_all | solution.py:517
  363.6 15.5 %all-to-all-start.1 = ((bf16[16,32,1536]{2,1,0:T(8,128)(2,1)}), bf16[16,32,1536]{2,1,0:T(8,128)(2,1)}, u32[]{:S(2)}, u32[]{:S(2)}) async-start(bf16[16,32,1536]{2,1,0:T(8,128)(2,1)} %bitcast.28), calls=%async_computation.1 | async-start | bytes 3145728 | tf_op jit(solution)/shard_map/all_to_all | solution.py:517
  379.1 0.0 copy-done.10
  379.1 0.1 broadcast_in_dim.3
  379.2 0.7 reshape_reshape.3.skip_ref
  379.8 0.0 copy-done.9
  379.8 0.6 reshape.53.gain_ref
  380.4 29.6 %row_scan.1.row_ref = f32[12,2048,128]{2,1,0:T(8,128)} custom-call(bf16[16,32,1920]{2,1,0:T(8,128)(2,1)} %get-tuple-element.17.refs_0_, bf16[16,64,1920]{2,1,0:T(8,128)(2,1)} %get-tuple-element.18.refs_1_, bf16[16,32,1920]{2,1,0:T(8,128)(2,1)} %get-tuple-element.19.refs_2_), custom_call_target="tpu_custom_call" | custom-call | flops 6442450944 | bytes 18874368 | tf_op jit(solution)/shard_map/row_scan/pallas_call | solution.py:368
  410.0 0.0 copy-done
  410.0 13.3 %output.5 = (f32[1024,1024]{1,0:T(8,128)}, bf16[1024,1024]{1,0:T(8,128)(2,1)}) custom-call(s32[1]{0:T(128)} %bitcast.t_ref, f32[12,2048,128]{2,1,0:T(8,128)} %row_scan.1.row_ref, bf16[16,64,1536]{2,1,0:T(8,128)(2,1)} %copy-done, bf16[1024,1536]{1,0:T(8,128)(2,1)} %get-tuple-element.26.inner_ref, f32[1,1536]{1,0:T(1,128)} %reshape_reshape.3.skip_ref, ...), custom_call_target="tpu_custom_call" | custom-call | flops 6442450944 | bytes 16777216 | tf_op jit(solution)/shard_map/output/pallas_call | solution.py:417
  423.3 1.5 collective-permute-start.5
  424.8 8.9 %output.4 = (f32[512,1024]{1,0:T(8,128)}, bf16[512,1024]{1,0:T(8,128)(2,1)}) custom-call(s32[1]{0:T(128)} %bitcast.t_ref, f32[12,2048,128]{2,1,0:T(8,128)} %row_scan.1.row_ref, bf16[16,32,1536]{2,1,0:T(8,128)(2,1)} %copy-done.1, bf16[512,1536]{1,0:T(8,128)(2,1)} %get-tuple-element.23.inner_ref, f32[1,1536]{1,0:T(1,128)} %reshape_reshape.3.skip_ref, ...), custom_call_target="tpu_custom_call" | custom-call | flops 3221225472 | bytes 16777216 | tf_op jit(solution)/shard_map/output/pallas_call | solution.py:417
  433.7 0.5 collective-permute-start.4
  434.3 0.0 all-to-all-done.1.col_ref
  434.3 9.0 %output.3 = (f32[512,1024]{1,0:T(8,128)}, bf16[512,1024]{1,0:T(8,128)(2,1)}) custom-call(s32[1]{0:T(128)} %bitcast.t_ref, f32[12,2048,128]{2,1,0:T(8,128)} %row_scan.1.row_ref, bf16[16,32,1536]{2,1,0:T(8,128)(2,1)} %all-to-all-done.1.col_ref, bf16[512,1536]{1,0:T(8,128)(2,1)} %get-tuple-element.20.inner_ref, f32[1,1536]{1,0:T(1,128)} %reshape_reshape.3.skip_ref, ...), custom_call_target="tpu_custom_call" | custom-call | flops 3221225472 | bytes 16777216 | tf_op jit(solution)/shard_map/output/pallas_call | solution.py:417
  443.3 1.5 collective-permute-start.3
  444.8 27.3 %collective-permute-done.5.got_ref = bf16[1024,1024]{1,0:T(8,128)(2,1)S(1)} collective-permute-done((bf16[1024,1024]{1,0:T(8,128)(2,1)}, bf16[1024,1024]{1,0:T(8,128)(2,1)S(1)}, u32[]{:S(2)}, u32[]{:S(2)}) %collective-permute-start.5) | collective-permute-done | bytes 2097184 | tf_op jit(solution)/shard_map/ppermute | solution.py:521
  472.0 1.4 copy-done.2
  473.4 6.4 %finish.3.rest_0_ = bf16[2,8,128,1024]{3,2,1,0:T(8,128)(2,1)} custom-call(f32[1024,1024]{1,0:T(8,128)} %get-tuple-element.27.own_ref, bf16[1024,1024]{1,0:T(8,128)(2,1)} %copy-done.2, f32[2,8,128,1024]{3,2,1,0:T(8,128)} %tok_ref.11), custom_call_target="tpu_custom_call" | custom-call | bytes 12582912 | tf_op jit(solution)/shard_map/finish/pallas_call | solution.py:462
  479.8 14.7 %collective-permute-done.4.got_ref = bf16[512,1024]{1,0:T(8,128)(2,1)S(1)} collective-permute-done((bf16[512,1024]{1,0:T(8,128)(2,1)}, bf16[512,1024]{1,0:T(8,128)(2,1)S(1)}, u32[]{:S(2)}, u32[]{:S(2)}) %collective-permute-start.4) | collective-permute-done | bytes 1048608 | tf_op jit(solution)/shard_map/ppermute | solution.py:521
  494.5 1.0 copy-done.5
  495.5 3.7 finish.4.rest_0_
  499.3 17.2 %collective-permute-done.3.got_ref = bf16[512,1024]{1,0:T(8,128)(2,1)} collective-permute-done((bf16[512,1024]{1,0:T(8,128)(2,1)}, bf16[512,1024]{1,0:T(8,128)(2,1)}, u32[]{:S(2)}, u32[]{:S(2)}) %collective-permute-start.3) | collective-permute-done | bytes 1048608 | tf_op jit(solution)/shard_map/ppermute | solution.py:521
  516.5 3.7 finish.5
  (8 shorter events, 0.0 us)
Async XLA Ops:
  0.0 5.9 %copy-start.8 = (bf16[2048,24]{0,1:T(8,128)(2,1)S(1)}, bf16[2048,24]{0,1:T(8,128)(2,1)}, u32[]{:S(2)}) copy-start(bf16[2048,24]{0,1:T(8,128)(2,1)} %param.14) | copy-start | bytes 294916
  0.0 6.2 %copy-start.11 = (f32[24]{0:T(128)S(1)}, f32[24]{0:T(128)}, u32[]{:S(2)}) copy-start(f32[24]{0:T(128)} %param.16) | copy-start | bytes 292
  0.0 6.2 %copy-start.12 = (f32[24]{0:T(128)S(1)}, f32[24]{0:T(128)}, u32[]{:S(2)}) copy-start(f32[24]{0:T(128)} %param.15) | copy-start | bytes 292
  0.0 6.7 %copy-start.4 = (bf16[2048,256]{1,0:T(8,128)(2,1)S(1)}, bf16[2048,256]{1,0:T(8,128)(2,1)}, u32[]{:S(2)}) copy-start(bf16[2048,256]{1,0:T(8,128)(2,1)} %param.13) | copy-start | bytes 3145732
  2.8 26.4 %collective-permute-start.2 = (bf16[512,1024]{1,0:T(8,128)(2,1)}, bf16[512,1024]{1,0:T(8,128)(2,1)S(1)}, u32[]{:S(2)}, u32[]{:S(2)}) collective-permute-start(bf16[512,1024]{1,0:T(8,128)(2,1)} %turn.5.own_ref), channel_id=1, source_target_pairs={{0,1},{1,0},{2,3},{3,2},{4,5},{5,4},{6,7},{7,6},{8,9},{9,8},{10,11... | collective-permute-start | bytes 3145736 | tf_op jit(solution)/shard_map/ppermute | solution.py:500
  29.2 1.0 copy-start.6
  40.5 45.8 %all-to-all-start = ((bf16[16,32,1920]{2,1,0:T(8,128)(2,1)}), bf16[16,32,1920]{2,1,0:T(8,128)(2,1)S(1)}, u32[]{:S(2)}, u32[]{:S(2)}) async-start(bf16[16,32,1920]{2,1,0:T(8,128)(2,1)} %get-tuple-element.19.refs_2_), calls=%async_computation | async-start | bytes 3932160 | tf_op jit(solution)/shard_map/all_to_all | solution.py:507
  49.3 25.7 %collective-permute-start = (bf16[512,1024]{1,0:T(8,128)(2,1)}, bf16[512,1024]{1,0:T(8,128)(2,1)S(1)}, u32[]{:S(2)}, u32[]{:S(2)}) collective-permute-start(bf16[512,1024]{1,0:T(8,128)(2,1)} %turn.3.own_ref), channel_id=1, source_target_pairs={{0,1},{1,0},{2,3},{3,2},{4,5},{5,4},{6,7},{7,6},{8,9},{9,8},{10,11... | collective-permute-start | bytes 3145736 | tf_op jit(solution)/shard_map/ppermute | solution.py:500
  75.0 1.0 copy-start.7
  86.3 14.6 %copy-start.3 = (bf16[16,32,1920]{2,1,0:T(8,128)(2,1)}, bf16[16,32,1920]{2,1,0:T(8,128)(2,1)S(1)}, u32[]{:S(2)}) copy-start(bf16[16,32,1920]{2,1,0:T(8,128)(2,1)S(1)} %all-to-all-done) | copy-start | bytes 5898244
  86.3 78.6 %all-to-all-start.2 = ((bf16[16,32,1920]{2,1,0:T(8,128)(2,1)}), bf16[16,32,1920]{2,1,0:T(8,128)(2,1)}, u32[]{:S(2)}, u32[]{:S(2)}) async-start(bf16[16,32,1920]{2,1,0:T(8,128)(2,1)} %get-tuple-element.17.refs_0_), calls=%async_computation.2 | async-start | bytes 3932160 | tf_op jit(solution)/shard_map/all_to_all | solution.py:507
  100.8 48.2 %collective-permute-start.1 = (bf16[1024,1024]{1,0:T(8,128)(2,1)}, bf16[1024,1024]{1,0:T(8,128)(2,1)}, u32[]{:S(2)}, u32[]{:S(2)}) collective-permute-start(bf16[1024,1024]{1,0:T(8,128)(2,1)} %turn.4.own_ref), channel_id=1, source_target_pairs={{0,1},{1,0},{2,3},{3,2},{4,5},{5,4},{6,7},{7,6},{8,9},{9,8},{10,11... | collective-permute-start | bytes 6291464 | tf_op jit(solution)/shard_map/ppermute | solution.py:500
  164.9 78.8 %all-to-all-start.4 = ((bf16[16,64,1920]{2,1,0:T(8,128)(2,1)}), bf16[16,64,1920]{2,1,0:T(8,128)(2,1)}, u32[]{:S(2)}, u32[]{:S(2)}) async-start(bf16[16,64,1920]{2,1,0:T(8,128)(2,1)} %get-tuple-element.18.refs_1_), calls=%async_computation.4 | async-start | bytes 7864320 | tf_op jit(solution)/shard_map/all_to_all | solution.py:507
  243.7 50.4 %all-to-all-start.3 = ((bf16[16,32,1536]{2,1,0:T(8,128)(2,1)}), bf16[16,32,1536]{2,1,0:T(8,128)(2,1)S(1)}, u32[]{:S(2)}, u32[]{:S(2)}) async-start(bf16[16,32,1536]{2,1,0:T(8,128)(2,1)} %bitcast.29), calls=%async_computation.3 | async-start | bytes 3145728 | tf_op jit(solution)/shard_map/all_to_all | solution.py:517
  294.1 1.1 copy-start.1
  295.2 68.3 %all-to-all-start.5 = ((bf16[16,64,1536]{2,1,0:T(8,128)(2,1)}), bf16[16,64,1536]{2,1,0:T(8,128)(2,1)S(1)}, u32[]{:S(2)}, u32[]{:S(2)}) async-start(bf16[16,64,1536]{2,1,0:T(8,128)(2,1)} %bitcast.26), calls=%async_computation.5 | async-start | bytes 6291456 | tf_op jit(solution)/shard_map/all_to_all | solution.py:517
  311.4 67.7 %copy-start.10 = (f32[24]{0:T(128)S(1)}, f32[24]{0:T(128)}, u32[]{:S(2)}) copy-start(f32[24]{0:T(128)} %param.17) | copy-start | bytes 292
  311.4 68.4 %copy-start.9 = (f32[1536]{0:T(1024)S(1)}, f32[1536]{0:T(1024)}, u32[]{:S(2)}) copy-start(f32[1536]{0:T(1024)} %param.18) | copy-start | bytes 18436
  363.6 46.4 %copy-start = (bf16[16,64,1536]{2,1,0:T(8,128)(2,1)}, bf16[16,64,1536]{2,1,0:T(8,128)(2,1)S(1)}, u32[]{:S(2)}) copy-start(bf16[16,64,1536]{2,1,0:T(8,128)(2,1)S(1)} %all-to-all-done.5.col_ref) | copy-start | bytes 9437188
  363.6 70.7 %all-to-all-start.1 = ((bf16[16,32,1536]{2,1,0:T(8,128)(2,1)}), bf16[16,32,1536]{2,1,0:T(8,128)(2,1)}, u32[]{:S(2)}, u32[]{:S(2)}) async-start(bf16[16,32,1536]{2,1,0:T(8,128)(2,1)} %bitcast.28), calls=%async_computation.1 | async-start | bytes 3145728 | tf_op jit(solution)/shard_map/all_to_all | solution.py:517
  423.3 48.7 %collective-permute-start.5 = (bf16[1024,1024]{1,0:T(8,128)(2,1)}, bf16[1024,1024]{1,0:T(8,128)(2,1)S(1)}, u32[]{:S(2)}, u32[]{:S(2)}) collective-permute-start(bf16[1024,1024]{1,0:T(8,128)(2,1)} %get-tuple-element.28), channel_id=1, source_target_pairs={{0,1},{1,0},{2,3},{3,2},{4,5},{5,4},{6,7},{7,6},{8,9},{9,8},{10,11... | collective-permute-start | bytes 6291464 | tf_op jit(solution)/shard_map/ppermute | solution.py:521
  433.7 60.8 %collective-permute-start.4 = (bf16[512,1024]{1,0:T(8,128)(2,1)}, bf16[512,1024]{1,0:T(8,128)(2,1)S(1)}, u32[]{:S(2)}, u32[]{:S(2)}) collective-permute-start(bf16[512,1024]{1,0:T(8,128)(2,1)} %get-tuple-element.25), channel_id=1, source_target_pairs={{0,1},{1,0},{2,3},{3,2},{4,5},{5,4},{6,7},{7,6},{8,9},{9,8},{10,11... | collective-permute-start | bytes 3145736 | tf_op jit(solution)/shard_map/ppermute | solution.py:521
  443.3 73.2 %collective-permute-start.3 = (bf16[512,1024]{1,0:T(8,128)(2,1)}, bf16[512,1024]{1,0:T(8,128)(2,1)}, u32[]{:S(2)}, u32[]{:S(2)}) collective-permute-start(bf16[512,1024]{1,0:T(8,128)(2,1)} %get-tuple-element.22), channel_id=1, source_target_pairs={{0,1},{1,0},{2,3},{3,2},{4,5},{5,4},{6,7},{7,6},{8,9},{9,8},{10,11... | collective-permute-start | bytes 3145736 | tf_op jit(solution)/shard_map/ppermute | solution.py:521
  472.0 1.4 copy-start.2
  494.5 1.0 copy-start.5

commit v3 on v2

--- a/solution.py
+++ b/solution.py
@@ -99,7 +99,7 @@
 LANES = 128
 SUBLANES = 8
 LOG2E = 1.4426950408889634
-HALVES = 2
+PARTS = 4
 VMEM_LIMIT = 60 * 1024 * 1024
 
 
@@ -122,17 +122,17 @@
 
 def turn(tokens, start, count):
     _, rows, columns, feats = tokens.shape
-    step = columns // HALVES // 2
+    step = columns // PARTS
     return pl.pallas_call(
         functools.partial(turn_kernel, rows),
-        grid=(2 * count,),
+        grid=(count,),
         in_specs=[grid_block(tokens, start)],
         out_specs=pl.BlockSpec((step * rows, feats), lambda k: (k, 0)),
-        out_shape=jax.ShapeDtypeStruct((2 * count * step * rows, feats), jnp.bfloat16),
+        out_shape=jax.ShapeDtypeStruct((count * step * rows, feats), jnp.bfloat16),
         scratch_shapes=[pltpu.VMEM((feats // LANES, step * rows, LANES), jnp.float32)],
         compiler_params=params(),
         cost_estimate=pl.CostEstimate(
-            flops=0, transcendentals=0, bytes_accessed=12 * count * step * rows * feats
+            flops=0, transcendentals=0, bytes_accessed=6 * count * step * rows * feats
         ),
         name="turn",
     )(tokens)
@@ -140,19 +140,19 @@
 
 def grid_block(tokens, start):
     _, rows, columns, feats = tokens.shape
-    per_image = 2 * HALVES
 
     def place(k):
-        at = 2 * start + k
-        return at // per_image, 0, at % per_image, 0
-
-    return pl.BlockSpec((1, rows, columns // per_image, feats), place)
+        at = start + k
+        return at // PARTS, 0, at % PARTS, 0
+
+    return pl.BlockSpec((1, rows, columns // PARTS, feats), place)
 
 
 def project_kernel(
     depth, heads, t_ref, own_ref, other_ref, g_own, g_other, w_own, w_other, m_own, m_other,
-    bias_ref, rate_ref, inner_ref, pack_ref,
+    bias_ref, rate_ref, *rest,
 ):
+    inner_ref, pack_ref = rest[-2:]
     own = own_ref[...].astype(jnp.float32)
     other = other_ref[...].astype(jnp.float32)
     squares = jnp.sum(own * own, axis=-1, keepdims=True) + jnp.sum(
@@ -190,12 +190,13 @@
         put(pair * LANES, inner[:, part].astype(jnp.float32) * spread)
 
 
-def project(own, other, in_gain, w_inner, w_small, bias, rate, place, heads, owners, count):
+def project(own, other, in_gain, w_inner, w_small, bias, rate, place, heads, owners, start, count, total, earlier):
     rows, feats = own.shape
     wide = w_inner.shape[1]
     small = w_small.shape[1]
-    tile = rows // (2 * count)
-    depth = 2 * tile // owners
+    tile = rows // count
+    depth = tile // owners
+    chained = [] if earlier is None else [earlier]
     gains = in_gain.reshape(2, 1, feats)
     w_inner = w_inner.reshape(2, feats, wide)
     w_small = w_small.reshape(2, feats, small)
@@ -217,22 +218,24 @@
             + pair((1, feats))
             + pair((feats, wide))
             + pair((feats, small))
-            + [resident((1, LANES), lambda i, t: (0, 0))] * 2,
+            + [resident((1, LANES), lambda i, t: (0, 0))] * 2
+            + [pl.BlockSpec(memory_space=pl.ANY)] * len(chained),
             out_specs=[
-                pl.BlockSpec((tile, wide), lambda i, t: (i, 0)),
-                pl.BlockSpec((owners // 2, depth, packed), lambda i, t: (i % 2, i // 2, 0)),
+                pl.BlockSpec((tile, wide), lambda i, t: (start + i, 0)),
+                pl.BlockSpec((owners, depth, packed), lambda i, t: (0, i, 0)),
             ],
         ),
         out_shape=[
-            jax.ShapeDtypeStruct((rows, wide), jnp.bfloat16),
+            jax.ShapeDtypeStruct((total * tile, wide), jnp.bfloat16),
             jax.ShapeDtypeStruct((owners, count * depth, packed), jnp.bfloat16),
         ],
+        input_output_aliases={11: 0} if chained else {},
         compiler_params=params(),
         cost_estimate=pl.CostEstimate(
             flops=4 * rows * feats * packed, transcendentals=0, bytes_accessed=20 * 2**20
         ),
         name="project",
-    )(place, own, other, gains, gains, w_inner, w_inner, w_small, w_small, bias, rate)
+    )(place, own, other, gains, gains, w_inner, w_inner, w_small, w_small, bias, rate, *chained)
 
 
 def scan_sequence(length, heads, in_map, out_map, decay, value_of, store):
@@ -276,7 +279,8 @@
         )
 
 
-def column_kernel(heads, pack_ref, out_ref):
+def column_kernel(heads, pack_ref, *rest):
+    out_ref = rest[-1]
     owners, _, rows, _ = pack_ref.shape
     length = owners * rows
     wide = out_ref.shape[3]
@@ -309,37 +313,40 @@
     )
 
 
-def column_scan(pack, heads):
-    owners, columns, rows, packed = pack.shape
+def column_scan(pack, heads, first, count, offset, total, earlier):
+    owners, _, rows, packed = pack.shape
     wide = heads * HEAD_DIM
+    chained = [] if earlier is None else [earlier]
     return pl.pallas_call(
         functools.partial(column_kernel, heads),
-        grid=(columns,),
-        in_specs=[pl.BlockSpec((owners, 1, rows, packed), lambda c: (0, c, 0, 0))],
-        out_specs=pl.BlockSpec((owners, 1, rows, wide), lambda c: (0, c, 0, 0)),
-        out_shape=jax.ShapeDtypeStruct((owners, columns, rows, wide), jnp.bfloat16),
+        grid=(count,),
+        in_specs=[pl.BlockSpec((owners, 1, rows, packed), lambda c: (0, first + c, 0, 0))]
+        + [pl.BlockSpec(memory_space=pl.ANY)] * len(chained),
+        out_specs=pl.BlockSpec((owners, 1, rows, wide), lambda c: (0, offset + c, 0, 0)),
+        out_shape=jax.ShapeDtypeStruct((owners, total, rows, wide), jnp.bfloat16),
+        input_output_aliases={1: 0} if chained else {},
         compiler_params=params(),
-        cost_estimate=scan_cost(columns, owners * rows, heads),
+        cost_estimate=scan_cost(count, owners * rows, heads),
         name="column_scan",
-    )(pack)
+    )(pack, *chained)
 
 
 def row_kernel(rows, heads, counts, *refs):
     packs, out_ref, held = refs[:-2], refs[-2], refs[-1]
     image, row = pl.program_id(0), pl.program_id(1)
     wide = heads * HEAD_DIM
-    tall = held.shape[1] // HALVES
+    tall = held.shape[1] // PARTS
     length = held.shape[1] // rows
     units = [(pack, k) for pack, count in zip(packs, counts) for k in range(count)]
 
     for u, (pack, k) in enumerate(units):
 
-        @pl.when((row == 0) & (image == u // HALVES))
-        def _(pack=pack, k=k, half=u % HALVES):
+        @pl.when((row == 0) & (image == u // PARTS))
+        def _(pack=pack, k=k, part=u % PARTS):
             depth = tall // pack.shape[0]
             for lane in range(pack.shape[2] // LANES):
                 block = pack[:, k * depth : (k + 1) * depth, lane * LANES : (lane + 1) * LANES]
-                held[lane, half * tall : (half + 1) * tall, :] = block.reshape(
+                held[lane, part * tall : (part + 1) * tall, :] = block.reshape(
                     tall, LANES
                 ).astype(jnp.float32)
 
@@ -406,22 +413,22 @@
 
 
 def output(row_out, start, count, col, inner, skip, gain, w_out, place):
-    rows, wide = inner.shape
+    wide = inner.shape[1]
     feats = w_out.shape[1] // 2
     depth = col.shape[1] // count
     owners = col.shape[0]
-    tile = owners * depth // 2
-    steps = rows // tile
-    row_spec = pl.BlockSpec((tile, wide), lambda i, t: (i, 0))
+    tile = owners * depth
+    rows = tile * count
+    row_spec = pl.BlockSpec((tile, wide), lambda i, t: (start + i, 0))
     out_spec = pl.BlockSpec((tile, feats), lambda i, t: (i, 0))
     return pl.pallas_call(
         output_kernel,
         grid_spec=pltpu.PrefetchScalarGridSpec(
             num_scalar_prefetch=1,
-            grid=(steps,),
+            grid=(count,),
             in_specs=[
-                pl.BlockSpec((wide // LANES, tile, LANES), lambda i, t: (0, 2 * start + i, 0)),
-                pl.BlockSpec((owners // 2, depth, wide), lambda i, t: (i % 2, i // 2, 0)),
+                pl.BlockSpec((wide // LANES, tile, LANES), lambda i, t: (0, start + i, 0)),
+                pl.BlockSpec((owners, depth, wide), lambda i, t: (0, i, 0)),
                 row_spec,
                 resident((1, wide), lambda i, t: (0, 0)),
                 resident((1, wide), lambda i, t: (0, 0)),
@@ -456,12 +463,12 @@
 
 def finish(own, got, tokens, start, count, earlier):
     _, rows, columns, feats = tokens.shape
-    step = columns // HALVES // 2
+    step = columns // PARTS
     flat = pl.BlockSpec((step * rows, feats), lambda k: (k, 0))
     chained = [] if earlier is None else [earlier]
     return pl.pallas_call(
         functools.partial(finish_kernel, rows),
-        grid=(2 * count,),
+        grid=(count,),
         in_specs=[flat, flat, grid_block(tokens, start)]
         + [pl.BlockSpec(memory_space=pl.ANY)] * len(chained),
         out_specs=grid_block(tokens, start),
@@ -470,7 +477,7 @@
         input_output_aliases={3: 0} if chained else {},
         compiler_params=params(),
         cost_estimate=pl.CostEstimate(
-            flops=0, transcendentals=0, bytes_accessed=24 * count * step * rows * feats
+            flops=0, transcendentals=0, bytes_accessed=12 * count * step * rows * feats
         ),
         name="finish",
     )(own, got, tokens, *chained)
@@ -490,49 +497,57 @@
     rate = jnp.pad(decay_rate, (0, pad)).reshape(1, LANES)
     skip_wide = jnp.repeat(skip, HEAD_DIM).reshape(1, wide)
     gain = norm_gain.reshape(1, wide)
-    counts = (1, images * HALVES - 2, 1)
-    starts = (0, 1, images * HALVES - 1)
-    groups = range(len(counts))
-    own, other, inner, packs, arrived, columns_out = [], [], [], [], [], []
-    for g in groups:
-        own.append(turn(tokens, starts[g], counts[g]))
-    for g in groups:
+    units = images * PARTS
+    per_unit = columns // PARTS // owners
+    there = groups_of((1, units // 2 - 1, units - units // 2))
+    back = groups_of((units // 2, units // 4, units - units // 2 - units // 4))
+    own, other, packs, arrived = [], [], [], []
+    for start, count in there:
+        own.append(turn(tokens, start, count))
+    for g in range(len(there)):
         other.append(lax.ppermute(own[g], "tensor", swap))
-    for g in groups:
-        a, b = project(
-            own[g], other[g], in_gain, w_inner, w_small, bias, rate, place, heads, owners, counts[g]
+    inner = None
+    for g, (start, count) in enumerate(there):
+        inner, pack = project(
+            own[g], other[g], in_gain, w_inner, w_small, bias, rate, place, heads, owners,
+            start, count, units, inner,
         )
-        inner.append(a)
-        packs.append(b)
-        arrived.append(lax.all_to_all(b, "space", split_axis=0, concat_axis=0, tiled=True))
-    for g in groups:
-        block = arrived[g]
-        shape = (owners, block.shape[1] // rows, rows, block.shape[2])
-        columns_out.append(
-            column_scan(block.reshape(shape), heads).reshape(owners, block.shape[1], wide)
-        )
+        packs.append(pack)
+        block = lax.all_to_all(pack, "space", split_axis=0, concat_axis=0, tiled=True)
+        arrived.append(block.reshape(owners, count * per_unit, rows, pack.shape[2]))
+    counts = tuple(count for _, count in there)
     row_out = row_scan(packs, counts, images, rows, columns, heads)
+    columns_out = [None] * len(back)
+    for g, (start, count) in enumerate(there):
+        for k, (low, size) in enumerate(back):
+            first, last = max(start, low), min(start + count, low + size)
+            if first < last:
+                columns_out[k] = column_scan(
+                    arrived[g], heads, (first - start) * per_unit, (last - first) * per_unit,
+                    (first - low) * per_unit, size * per_unit, columns_out[k],
+                )
     result = None
-    for g in ORDER:
-        back = lax.all_to_all(columns_out[g], "space", split_axis=0, concat_axis=0, tiled=True)
-        kept, send = output(
-            row_out, starts[g], counts[g], back, inner[g], skip_wide, gain, w_out, place
-        )
+    for k, (start, count) in enumerate(back):
+        block = columns_out[k].reshape(owners, count * per_unit * rows, wide)
+        block = lax.all_to_all(block, "space", split_axis=0, concat_axis=0, tiled=True)
+        kept, send = output(row_out, start, count, block, inner, skip_wide, gain, w_out, place)
         got = lax.ppermute(send, "tensor", swap)
-        result = finish(kept, got, tokens, starts[g], counts[g], result)
+        result = finish(kept, got, tokens, start, count, result)
     return result
 
 
-ORDER = (1, 0, 2)
+def groups_of(counts):
+    starts = [sum(counts[:k]) for k in range(len(counts))]
+    return list(zip(starts, counts))
 
 
 def fits(owners, tensor, tokens, heads):
     images, rows, columns, _ = tokens
     return (
         tensor == 2
-        and images * HALVES > 2
+        and images * PARTS == 8
         and rows == SUBLANES
-        and columns % (HALVES * owners) == 0
+        and columns % (PARTS * owners) == 0
         and owners * rows == columns == LANES
         and heads % NORM_HEADS == 0
         and heads % 2 == 0

time: 521 us -> 569 us (1.092)
  blocking collectives: 0 us -> 93.7 us
  waiting for transfers between devices: 289 us -> 256 us
  starting transfers between devices: 74.5 us -> 58.3 us
    all_to_all x0 -> x1, blocking collectives: none -> 93.7 us  [pipelined(): lax.all_to_all(pack, 'space', split_axis=0, concat_axis=0, tiled=True)]
    all_to_all x6 -> x5, waiting for transfers between devices: 138 us -> 119 us  [the longest x3 69.8 us: pipelined(): lax.all_to_all(block, 'space', split_axis=0, concat_axis=0, tiled=True)]
    all_to_all x6 -> x5, starting transfers between devices: 64.8 us -> 49.7 us  [the longest x3 39.3 us: pipelined(): lax.all_to_all(block, 'space', split_axis=0, concat_axis=0, tiled=True)]
    ppermute x3, waiting for transfers between devices: 92 us -> 78.1 us  [pipelined(): other.append(lax.ppermute(own[g], 'tensor', swap))]
    pallas_call x9 -> x10, Pallas kernels: 50.6 us -> 53.6 us  [the longest x4 28.3 us: column_scan(): pl.pallas_call(functools.partial(column_kernel, heads), grid=(count,), in...]
  transfers between devices with their start and end apart: 12 -> 11, of which waited for: 9 -> 7; matrix products, arithmetic and copies ran while one was open for 1% -> 1% of each run, Pallas kernels for 25% -> 25%
where the time goes in v3:
time: 569 us; the launch traced here: 568 us
  waiting for transfers between devices  256 us (45%)
  Pallas kernels  151 us (27%)
  blocking collectives  93.7 us (16%)
  starting transfers between devices  58.3 us (10%)
  local copies, waits for them, and re-layouts  6.52 us (1%)
    all_to_all x1, blocking collectives, pipelined(): lax.all_to_all(pack, 'space', split_axis=0, concat_axis=0, tiled=True)  93.7 us
    ppermute x3, waiting for transfers between devices, pipelined(): other.append(lax.ppermute(own[g], 'tensor', swap))  78.1 us
    all_to_all x3, waiting for transfers between devices, pipelined(): lax.all_to_all(block, 'space', split_axis=0, concat_axis=0, tiled=True)  69.8 us
    ppermute x3, waiting for transfers between devices, pipelined(): got = lax.ppermute(send, 'tensor', swap)  59.1 us
    all_to_all x2, waiting for transfers between devices, pipelined(): lax.all_to_all(pack, 'space', split_axis=0, concat_axis=0, tiled=True)  48.7 us
    all_to_all x3, starting transfers between devices, pipelined(): lax.all_to_all(block, 'space', split_axis=0, concat_axis=0, tiled=True)  39.3 us
    pallas_call x3, Pallas kernels, project(): pl.pallas_call(functools.partial(project_kernel, 2 * feats, heads), grid_...  36.4 us
    pallas_call x3, Pallas kernels, output(): pl.pallas_call(output_kernel, grid_spec=pltpu.PrefetchScalarGridSpec(num_...  31.3 us
  transfers between devices with their start and end apart: 11, of which 7 were waited for; matrix products, arithmetic and copies ran while one was open for 1% of the time, Pallas kernels for 25%

profile of v3, /device:TPU:0, one launch (start us, length us, event | category | flops | bytes accessed | tf_op | source)
XLA Modules:
  0.0 567.9 jit_solution(3334309636989705531)
XLA Ops:
  0.0 4.3 turn.4.own_ref
  4.3 3.0 collective-permute-start.1
  7.3 4.8 turn.5.own_ref
  12.0 0.0 copy-start.7
  12.1 0.0 copy-start.10
  12.1 0.1 collective-permute-start.2
  12.1 2.4 turn.3.own_ref
  14.5 2.0 collective-permute-start
  16.5 0.0 copy-done.7
  16.5 0.3 copy.17
  16.8 0.0 copy-done.10
  16.8 0.0 copy-done.11
  16.8 0.6 pad_bitcast_fusion
  17.4 2.6 fusion.1
  20.0 78.1 %collective-permute-done.other_ref = bf16[256,1024]{1,0:T(8,128)(2,1)S(1)} collective-permute-done((bf16[256,1024]{1,0:T(8,128)(2,1)}, bf16[256,1024]{1,0:T(8,128)(2,1)S(1)}, u32[]{:S(2)}, u32[]{:S(2)}) %collective-permute-start) | collective-permute-done | bytes 524320 | tf_op jit(solution)/shard_map/ppermute | solution.py:508
  98.1 0.8 copy-done.6
  98.9 7.5 %project.3 = (bf16[2048,1536]{1,0:T(8,128)(2,1)}, bf16[16,16,1920]{2,1,0:T(8,128)(2,1)}) custom-call(s32[1]{0:T(128)} %bitcast.t_ref, bf16[256,1024]{1,0:T(8,128)(2,1)} %turn.3.own_ref, bf16[256,1024]{1,0:T(8,128)(2,1)} %copy-done.6, f32[2,1,1024]{2,1,0:T(1,128)} %bitcast.33, f32[2,1,1024]{2,1,0:T(1,128)} %bitcast.34, bf16[2,1024,1536]{2,1,0:T(8,128)(2,1)} %bitcast.14, ...), custom_call_target="tpu_custom_call" | custom-call | flops 2013265920 | bytes 20971520 | tf_op jit(solution)/shard_map/project/pallas_call | solution.py:212
  106.4 6.1 %all-to-all-start.4 = ((bf16[16,16,1920]{2,1,0:T(8,128)(2,1)}), bf16[16,16,1920]{2,1,0:T(8,128)(2,1)S(1)}, u32[]{:S(2)}, u32[]{:S(2)}) async-start(bf16[16,16,1920]{2,1,0:T(8,128)(2,1)} %get-tuple-element.17.refs_0_), calls=%async_computation.4 | async-start | bytes 1966080 | tf_op jit(solution)/shard_map/all_to_all | solution.py:516
  112.5 0.0 collective-permute-done.1.other_ref
  112.5 0.0 copy-start.4
  112.6 1.1 copy-done.4
  113.7 13.0 %project.4 = (bf16[2048,1536]{1,0:T(8,128)(2,1)}, bf16[16,48,1920]{2,1,0:T(8,128)(2,1)}) custom-call(s32[1]{0:T(128)} %bitcast.t_ref, bf16[768,1024]{1,0:T(8,128)(2,1)} %turn.4.own_ref, bf16[768,1024]{1,0:T(8,128)(2,1)} %copy-done.4, f32[2,1,1024]{2,1,0:T(1,128)} %bitcast.35, f32[2,1,1024]{2,1,0:T(1,128)} %bitcast.36, ...), custom_call_target="tpu_custom_call", output_to_operand_aliasing={{0}: (11, {})} | custom-call | flops 6039797760 | bytes 20971520 | tf_op jit(solution)/shard_map/project/pallas_call | solution.py:212
  126.7 0.0 collective-permute-done.2.other_ref
  126.7 15.8 %project.5 = (bf16[2048,1536]{1,0:T(8,128)(2,1)}, bf16[16,64,1920]{2,1,0:T(8,128)(2,1)}) custom-call(s32[1]{0:T(128)} %bitcast.t_ref, bf16[1024,1024]{1,0:T(8,128)(2,1)} %turn.5.own_ref, bf16[1024,1024]{1,0:T(8,128)(2,1)} %collective-permute-done.2.other_ref, f32[2,1,1024]{2,1,0:T(1,128)} %bitcast.37, ...), custom_call_target="tpu_custom_call", output_to_operand_aliasing={{0}: (11, {})} | custom-call | flops 8053063680 | bytes 20971520 | tf_op jit(solution)/shard_map/project/pallas_call | solution.py:212
  142.6 0.0 all-to-all-done.4
  142.6 0.0 copy-start.2
  142.6 93.7 %all_to_all.30 = bf16[16,64,1920]{2,1,0:T(8,128)(2,1)} all-to-all(bf16[16,64,1920]{2,1,0:T(8,128)(2,1)} %get-tuple-element.21.refs_2_), channel_id=1, replica_groups=mesh['space'=16,'tensor'=2] {'space'}, dimensions={0} | all-to-all | bytes 7864320 | tf_op jit(solution)/shard_map/all_to_all | solution.py:516
  236.3 0.0 copy-done.2
  236.3 4.2 all-to-all-start.3
  240.5 7.1 %column_scan.5 = bf16[16,4,8,1536]{3,2,1,0:T(8,128)(2,1)} custom-call(bf16[16,8,8,1920]{3,2,1,0:T(8,128)(2,1)} %bitcast.28), custom_call_target="tpu_custom_call" | custom-call | flops 1610612736 | bytes 4718592 | tf_op jit(solution)/shard_map/column_scan/pallas_call | solution.py:320
  247.6 48.7 %all-to-all-done.3 = bf16[16,48,1920]{2,1,0:T(8,128)(2,1)S(1)} async-done(((bf16[16,48,1920]{2,1,0:T(8,128)(2,1)}), bf16[16,48,1920]{2,1,0:T(8,128)(2,1)S(1)}, u32[]{:S(2)}, u32[]{:S(2)}) %all-to-all-start.3) | async-done | bytes 2949152 | tf_op jit(solution)/shard_map/all_to_all | solution.py:516
  296.3 14.7 %all-to-all-start.2 = ((bf16[16,32,1536]{2,1,0:T(8,128)(2,1)}), bf16[16,32,1536]{2,1,0:T(8,128)(2,1)}, u32[]{:S(2)}, u32[]{:S(2)}) async-start(bf16[16,32,1536]{2,1,0:T(8,128)(2,1)} %bitcast.32), calls=%async_computation.2 | async-start | bytes 3145728 | tf_op jit(solution)/shard_map/all_to_all | solution.py:532
  311.0 4.4 column_scan.6.rest_0_
  315.4 0.0 copy-done.1
  315.4 9.7 %column_scan.7 = bf16[16,8,8,1536]{3,2,1,0:T(8,128)(2,1)} custom-call(bf16[16,6,8,1920]{3,2,1,0:T(8,128)(2,1)} %bitcast.27, bf16[16,8,8,1536]{3,2,1,0:T(8,128)(2,1)} %column_scan.6.rest_0_), custom_call_target="tpu_custom_call", output_to_operand_aliasing={{}: (1, {})} | custom-call | flops 2415919104 | bytes 7077888 | tf_op jit(solution)/shard_map/column_scan/pallas_call | solution.py:320
  325.2 17.7 %all-to-all-done.2.col_ref = bf16[16,32,1536]{2,1,0:T(8,128)(2,1)} async-done(((bf16[16,32,1536]{2,1,0:T(8,128)(2,1)}), bf16[16,32,1536]{2,1,0:T(8,128)(2,1)}, u32[]{:S(2)}, u32[]{:S(2)}) %all-to-all-start.2) | async-done | bytes 1572896 | tf_op jit(solution)/shard_map/all_to_all | solution.py:532
  342.9 9.1 %all-to-all-start.5 = ((bf16[16,64,1536]{2,1,0:T(8,128)(2,1)}), bf16[16,64,1536]{2,1,0:T(8,128)(2,1)S(1)}, u32[]{:S(2)}, u32[]{:S(2)}) async-start(bf16[16,64,1536]{2,1,0:T(8,128)(2,1)} %bitcast.26), calls=%async_computation.5 | async-start | bytes 6291456 | tf_op jit(solution)/shard_map/all_to_all | solution.py:532
  352.0 0.0 copy-start.9
  352.0 0.0 copy-start.8
  352.1 7.1 %column_scan.4 = bf16[16,4,8,1536]{3,2,1,0:T(8,128)(2,1)} custom-call(bf16[16,8,8,1920]{3,2,1,0:T(8,128)(2,1)} %bitcast.29), custom_call_target="tpu_custom_call" | custom-call | flops 1610612736 | bytes 4718592 | tf_op jit(solution)/shard_map/column_scan/pallas_call | solution.py:320
  359.2 52.1 %all-to-all-done.5.col_ref = bf16[16,64,1536]{2,1,0:T(8,128)(2,1)S(1)} async-done(((bf16[16,64,1536]{2,1,0:T(8,128)(2,1)}), bf16[16,64,1536]{2,1,0:T(8,128)(2,1)S(1)}, u32[]{:S(2)}, u32[]{:S(2)}) %all-to-all-start.5) | async-done | bytes 3145760 | tf_op jit(solution)/shard_map/all_to_all | solution.py:532
  411.3 15.5 %all-to-all-start.1 = ((bf16[16,32,1536]{2,1,0:T(8,128)(2,1)}), bf16[16,32,1536]{2,1,0:T(8,128)(2,1)}, u32[]{:S(2)}, u32[]{:S(2)}) async-start(bf16[16,32,1536]{2,1,0:T(8,128)(2,1)} %bitcast.31), calls=%async_computation.1 | async-start | bytes 3145728 | tf_op jit(solution)/shard_map/all_to_all | solution.py:532
  426.7 0.0 copy-done.9
  426.8 0.1 broadcast_in_dim.3
  426.8 0.7 reshape_reshape.3.skip_ref
  427.5 0.0 copy-done.8
  427.5 0.6 reshape.53.gain_ref
  428.1 29.6 %row_scan.1.row_ref = f32[12,2048,128]{2,1,0:T(8,128)} custom-call(bf16[16,16,1920]{2,1,0:T(8,128)(2,1)} %get-tuple-element.17.refs_0_, bf16[16,48,1920]{2,1,0:T(8,128)(2,1)} %get-tuple-element.19.refs_1_, bf16[16,64,1920]{2,1,0:T(8,128)(2,1)} %get-tuple-element.21.refs_2_), custom_call_target="tpu_custom_call" | custom-call | flops 6442450944 | bytes 18874368 | tf_op jit(solution)/shard_map/row_scan/pallas_call | solution.py:375
  457.7 0.0 copy-done
  457.7 13.4 %output.5 = (f32[1024,1024]{1,0:T(8,128)}, bf16[1024,1024]{1,0:T(8,128)(2,1)}) custom-call(s32[1]{0:T(128)} %bitcast.t_ref, f32[12,2048,128]{2,1,0:T(8,128)} %row_scan.1.row_ref, bf16[16,64,1536]{2,1,0:T(8,128)(2,1)} %copy-done, bf16[2048,1536]{1,0:T(8,128)(2,1)} %get-tuple-element.22.inner_ref, f32[1,1536]{1,0:T(1,128)} %reshape_reshape.3.skip_ref, ...), custom_call_target="tpu_custom_call" | custom-call | flops 6442450944 | bytes 16777216 | tf_op jit(solution)/shard_map/output/pallas_call | solution.py:424
  471.0 1.5 collective-permute-start.5
  472.6 9.0 %output.4 = (f32[512,1024]{1,0:T(8,128)}, bf16[512,1024]{1,0:T(8,128)(2,1)}) custom-call(s32[1]{0:T(128)} %bitcast.t_ref, f32[12,2048,128]{2,1,0:T(8,128)} %row_scan.1.row_ref, bf16[16,32,1536]{2,1,0:T(8,128)(2,1)} %all-to-all-done.2.col_ref, bf16[2048,1536]{1,0:T(8,128)(2,1)} %get-tuple-element.22.inner_ref, f32[1,1536]{1,0:T(1,128)} %reshape_reshape.3.skip_ref, ...), custom_call_target="tpu_custom_call" | custom-call | flops 3221225472 | bytes 16777216 | tf_op jit(solution)/shard_map/output/pallas_call | solution.py:424
  481.6 0.5 collective-permute-start.4
  482.1 0.0 all-to-all-done.1.col_ref
  482.1 9.0 %output.3 = (f32[512,1024]{1,0:T(8,128)}, bf16[512,1024]{1,0:T(8,128)(2,1)}) custom-call(s32[1]{0:T(128)} %bitcast.t_ref, f32[12,2048,128]{2,1,0:T(8,128)} %row_scan.1.row_ref, bf16[16,32,1536]{2,1,0:T(8,128)(2,1)} %all-to-all-done.1.col_ref, bf16[2048,1536]{1,0:T(8,128)(2,1)} %get-tuple-element.22.inner_ref, f32[1,1536]{1,0:T(1,128)} %reshape_reshape.3.skip_ref, ...), custom_call_target="tpu_custom_call" | custom-call | flops 3221225472 | bytes 16777216 | tf_op jit(solution)/shard_map/output/pallas_call | solution.py:424
  491.1 1.5 collective-permute-start.3
  492.6 27.2 %collective-permute-done.5.got_ref = bf16[1024,1024]{1,0:T(8,128)(2,1)S(1)} collective-permute-done((bf16[1024,1024]{1,0:T(8,128)(2,1)}, bf16[1024,1024]{1,0:T(8,128)(2,1)S(1)}, u32[]{:S(2)}, u32[]{:S(2)}) %collective-permute-start.5) | collective-permute-done | bytes 2097184 | tf_op jit(solution)/shard_map/ppermute | solution.py:534
  519.7 1.3 copy-done.3
  521.1 6.4 %finish.3.rest_0_ = bf16[2,8,128,1024]{3,2,1,0:T(8,128)(2,1)} custom-call(f32[1024,1024]{1,0:T(8,128)} %get-tuple-element.27.own_ref, bf16[1024,1024]{1,0:T(8,128)(2,1)} %copy-done.3, f32[2,8,128,1024]{3,2,1,0:T(8,128)} %tok_ref.11), custom_call_target="tpu_custom_call" | custom-call | bytes 12582912 | tf_op jit(solution)/shard_map/finish/pallas_call | solution.py:469
  527.5 14.7 %collective-permute-done.4.got_ref = bf16[512,1024]{1,0:T(8,128)(2,1)S(1)} collective-permute-done((bf16[512,1024]{1,0:T(8,128)(2,1)}, bf16[512,1024]{1,0:T(8,128)(2,1)S(1)}, u32[]{:S(2)}, u32[]{:S(2)}) %collective-permute-start.4) | collective-permute-done | bytes 1048608 | tf_op jit(solution)/shard_map/ppermute | solution.py:534
  542.2 1.0 copy-done.5
  543.2 3.7 finish.4.rest_0_
  546.9 17.2 %collective-permute-done.3.got_ref = bf16[512,1024]{1,0:T(8,128)(2,1)} collective-permute-done((bf16[512,1024]{1,0:T(8,128)(2,1)}, bf16[512,1024]{1,0:T(8,128)(2,1)}, u32[]{:S(2)}, u32[]{:S(2)}) %collective-permute-start.3) | collective-permute-done | bytes 1048608 | tf_op jit(solution)/shard_map/ppermute | solution.py:534
  564.2 3.7 finish.5
  (6 shorter events, 0.0 us)
Async XLA Ops:
  4.3 108.2 %collective-permute-start.1 = (bf16[768,1024]{1,0:T(8,128)(2,1)}, bf16[768,1024]{1,0:T(8,128)(2,1)S(1)}, u32[]{:S(2)}, u32[]{:S(2)}) collective-permute-start(bf16[768,1024]{1,0:T(8,128)(2,1)} %turn.4.own_ref), channel_id=1, source_target_pairs={{0,1},{1,0},{2,3},{3,2},{4,5},{5,4},{6,7},{7,6},{8,9},{9,8},{10,11... | collective-permute-start | bytes 4718600 | tf_op jit(solution)/shard_map/ppermute | solution.py:508
  12.0 4.5 copy-start.7
  12.1 4.7 copy-start.10
  12.1 4.7 copy-start.11
  12.1 114.7 %collective-permute-start.2 = (bf16[1024,1024]{1,0:T(8,128)(2,1)}, bf16[1024,1024]{1,0:T(8,128)(2,1)}, u32[]{:S(2)}, u32[]{:S(2)}) collective-permute-start(bf16[1024,1024]{1,0:T(8,128)(2,1)} %turn.5.own_ref), channel_id=1, source_target_pairs={{0,1},{1,0},{2,3},{3,2},{4,5},{5,4},{6,7},{7,6},{8,9},{9,8},{10,11... | collective-permute-start | bytes 6291464 | tf_op jit(solution)/shard_map/ppermute | solution.py:508
  14.5 83.6 %collective-permute-start = (bf16[256,1024]{1,0:T(8,128)(2,1)}, bf16[256,1024]{1,0:T(8,128)(2,1)S(1)}, u32[]{:S(2)}, u32[]{:S(2)}) collective-permute-start(bf16[256,1024]{1,0:T(8,128)(2,1)} %turn.3.own_ref), channel_id=1, source_target_pairs={{0,1},{1,0},{2,3},{3,2},{4,5},{5,4},{6,7},{7,6},{8,9},{9,8},{10,11... | collective-permute-start | bytes 1572872 | tf_op jit(solution)/shard_map/ppermute | solution.py:508
  98.1 0.8 copy-start.6
  106.4 36.2 %all-to-all-start.4 = ((bf16[16,16,1920]{2,1,0:T(8,128)(2,1)}), bf16[16,16,1920]{2,1,0:T(8,128)(2,1)S(1)}, u32[]{:S(2)}, u32[]{:S(2)}) async-start(bf16[16,16,1920]{2,1,0:T(8,128)(2,1)} %get-tuple-element.17.refs_0_), calls=%async_computation.4 | async-start | bytes 1966080 | tf_op jit(solution)/shard_map/all_to_all | solution.py:516
  112.5 1.1 copy-start.4
  142.6 93.7 %copy-start.2 = (bf16[16,16,1920]{2,1,0:T(8,128)(2,1)}, bf16[16,16,1920]{2,1,0:T(8,128)(2,1)S(1)}, u32[]{:S(2)}) copy-start(bf16[16,16,1920]{2,1,0:T(8,128)(2,1)S(1)} %all-to-all-done.4) | copy-start | bytes 2949124
  236.3 60.1 %all-to-all-start.3 = ((bf16[16,48,1920]{2,1,0:T(8,128)(2,1)}), bf16[16,48,1920]{2,1,0:T(8,128)(2,1)S(1)}, u32[]{:S(2)}, u32[]{:S(2)}) async-start(bf16[16,48,1920]{2,1,0:T(8,128)(2,1)} %get-tuple-element.19.refs_1_), calls=%async_computation.3 | async-start | bytes 5898240 | tf_op jit(solution)/shard_map/all_to_all | solution.py:516
  296.3 19.1 %copy-start.1 = (bf16[16,48,1920]{2,1,0:T(8,128)(2,1)}, bf16[16,48,1920]{2,1,0:T(8,128)(2,1)S(1)}, u32[]{:S(2)}) copy-start(bf16[16,48,1920]{2,1,0:T(8,128)(2,1)S(1)} %all-to-all-done.3) | copy-start | bytes 8847364
  296.3 46.6 %all-to-all-start.2 = ((bf16[16,32,1536]{2,1,0:T(8,128)(2,1)}), bf16[16,32,1536]{2,1,0:T(8,128)(2,1)}, u32[]{:S(2)}, u32[]{:S(2)}) async-start(bf16[16,32,1536]{2,1,0:T(8,128)(2,1)} %bitcast.32), calls=%async_computation.2 | async-start | bytes 3145728 | tf_op jit(solution)/shard_map/all_to_all | solution.py:532
  342.9 68.3 %all-to-all-start.5 = ((bf16[16,64,1536]{2,1,0:T(8,128)(2,1)}), bf16[16,64,1536]{2,1,0:T(8,128)(2,1)S(1)}, u32[]{:S(2)}, u32[]{:S(2)}) async-start(bf16[16,64,1536]{2,1,0:T(8,128)(2,1)} %bitcast.26), calls=%async_computation.5 | async-start | bytes 6291456 | tf_op jit(solution)/shard_map/all_to_all | solution.py:532
  352.0 74.7 %copy-start.9 = (f32[24]{0:T(128)S(1)}, f32[24]{0:T(128)}, u32[]{:S(2)}) copy-start(f32[24]{0:T(128)} %param.17) | copy-start | bytes 292
  352.0 75.5 %copy-start.8 = (f32[1536]{0:T(1024)S(1)}, f32[1536]{0:T(1024)}, u32[]{:S(2)}) copy-start(f32[1536]{0:T(1024)} %param.18) | copy-start | bytes 18436
  411.3 46.4 %copy-start = (bf16[16,64,1536]{2,1,0:T(8,128)(2,1)}, bf16[16,64,1536]{2,1,0:T(8,128)(2,1)S(1)}, u32[]{:S(2)}) copy-start(bf16[16,64,1536]{2,1,0:T(8,128)(2,1)S(1)} %all-to-all-done.5.col_ref) | copy-start | bytes 9437188
  411.3 70.8 %all-to-all-start.1 = ((bf16[16,32,1536]{2,1,0:T(8,128)(2,1)}), bf16[16,32,1536]{2,1,0:T(8,128)(2,1)}, u32[]{:S(2)}, u32[]{:S(2)}) async-start(bf16[16,32,1536]{2,1,0:T(8,128)(2,1)} %bitcast.31), calls=%async_computation.1 | async-start | bytes 3145728 | tf_op jit(solution)/shard_map/all_to_all | solution.py:532
  471.0 48.7 %collective-permute-start.5 = (bf16[1024,1024]{1,0:T(8,128)(2,1)}, bf16[1024,1024]{1,0:T(8,128)(2,1)S(1)}, u32[]{:S(2)}, u32[]{:S(2)}) collective-permute-start(bf16[1024,1024]{1,0:T(8,128)(2,1)} %get-tuple-element.28), channel_id=1, source_target_pairs={{0,1},{1,0},{2,3},{3,2},{4,5},{5,4},{6,7},{7,6},{8,9},{9,8},{10,11... | collective-permute-start | bytes 6291464 | tf_op jit(solution)/shard_map/ppermute | solution.py:534
  481.6 60.7 %collective-permute-start.4 = (bf16[512,1024]{1,0:T(8,128)(2,1)}, bf16[512,1024]{1,0:T(8,128)(2,1)S(1)}, u32[]{:S(2)}, u32[]{:S(2)}) collective-permute-start(bf16[512,1024]{1,0:T(8,128)(2,1)} %get-tuple-element.26), channel_id=1, source_target_pairs={{0,1},{1,0},{2,3},{3,2},{4,5},{5,4},{6,7},{7,6},{8,9},{9,8},{10,11... | collective-permute-start | bytes 3145736 | tf_op jit(solution)/shard_map/ppermute | solution.py:534
  491.1 73.1 %collective-permute-start.3 = (bf16[512,1024]{1,0:T(8,128)(2,1)}, bf16[512,1024]{1,0:T(8,128)(2,1)}, u32[]{:S(2)}, u32[]{:S(2)}) collective-permute-start(bf16[512,1024]{1,0:T(8,128)(2,1)} %get-tuple-element.24), channel_id=1, source_target_pairs={{0,1},{1,0},{2,3},{3,2},{4,5},{5,4},{6,7},{7,6},{8,9},{9,8},{10,11... | collective-permute-start | bytes 3145736 | tf_op jit(solution)/shard_map/ppermute | solution.py:534
  519.7 1.4 copy-start.3
  542.2 1.0 copy-start.5

commit v4 on v3

--- a/solution.py
+++ b/solution.py
@@ -152,7 +152,7 @@
     depth, heads, t_ref, own_ref, other_ref, g_own, g_other, w_own, w_other, m_own, m_other,
     bias_ref, rate_ref, *rest,
 ):
-    inner_ref, pack_ref = rest[-2:]
+    inner_ref, pack_ref, spare_ref = rest[-3:]
     own = own_ref[...].astype(jnp.float32)
     other = other_ref[...].astype(jnp.float32)
     squares = jnp.sum(own * own, axis=-1, keepdims=True) + jnp.sum(
@@ -176,8 +176,13 @@
         lanes = block.shape[1]
         pack_ref[:, :, start : start + lanes] = block.astype(jnp.bfloat16).reshape(blocks + (lanes,))
 
-    put(wide, small[:, : 2 * STATE])
-    put(wide + 2 * STATE, -rate_ref[...] * step)
+    first = t_ref[0] == 0
+    in_map, out_map = small[:, :STATE], small[:, STATE : 2 * STATE]
+    put(wide, jnp.where(first, in_map, out_map))
+    put(wide + STATE, -rate_ref[...] * step)
+    spare_ref[...] = (
+        jnp.where(first, out_map, in_map).astype(jnp.bfloat16).reshape(spare_ref.shape)
+    )
     inner = project(w_own[0], w_other[0]).astype(jnp.bfloat16)
     inner_ref[...] = inner
     rows = inner.shape[0]
@@ -208,7 +213,7 @@
             resident((1,) + shape, lambda i, t: (1 - t[0], 0, 0)),
         ]
 
-    packed = wide + small
+    packed = wide + small - STATE
     return pl.pallas_call(
         functools.partial(project_kernel, 2 * feats, heads),
         grid_spec=pltpu.PrefetchScalarGridSpec(
@@ -223,11 +228,13 @@
             out_specs=[
                 pl.BlockSpec((tile, wide), lambda i, t: (start + i, 0)),
                 pl.BlockSpec((owners, depth, packed), lambda i, t: (0, i, 0)),
+                pl.BlockSpec((owners, depth, STATE), lambda i, t: (0, i, 0)),
             ],
         ),
         out_shape=[
             jax.ShapeDtypeStruct((total * tile, wide), jnp.bfloat16),
             jax.ShapeDtypeStruct((owners, count * depth, packed), jnp.bfloat16),
+            jax.ShapeDtypeStruct((owners, count * depth, STATE), jnp.bfloat16),
         ],
         input_output_aliases={11: 0} if chained else {},
         compiler_params=params(),
@@ -279,7 +286,14 @@
         )
 
 
-def column_kernel(heads, pack_ref, *rest):
+def both_maps(mine, spare):
+    first = lax.axis_index("tensor") == 0
+    in_map = jnp.where(first, mine, spare).astype(jnp.bfloat16)
+    out_map = jnp.where(first, spare, mine).astype(jnp.bfloat16)
+    return in_map, out_map
+
+
+def column_kernel(heads, pack_ref, spare_ref, *rest):
     out_ref = rest[-1]
     owners, _, rows, _ = pack_ref.shape
     length = owners * rows
@@ -297,9 +311,8 @@
     scan_sequence(
         length,
         heads,
-        take(wide).astype(jnp.bfloat16),
+        *both_maps(take(wide), spare_ref[:, 0, :, :].astype(jnp.float32).reshape(length, STATE)),
         take(wide + STATE).astype(jnp.bfloat16),
-        take(wide + 2 * STATE).astype(jnp.bfloat16),
         lambda pair: take(pair * LANES),
         store,
     )
@@ -313,39 +326,50 @@
     )
 
 
-def column_scan(pack, heads, first, count, offset, total, earlier):
+def column_scan(pack, spare, heads, first, count, offset, total, earlier):
     owners, _, rows, packed = pack.shape
     wide = heads * HEAD_DIM
     chained = [] if earlier is None else [earlier]
     return pl.pallas_call(
         functools.partial(column_kernel, heads),
         grid=(count,),
-        in_specs=[pl.BlockSpec((owners, 1, rows, packed), lambda c: (0, first + c, 0, 0))]
+        in_specs=[
+            pl.BlockSpec((owners, 1, rows, packed), lambda c: (0, first + c, 0, 0)),
+            pl.BlockSpec((owners, 1, rows, STATE), lambda c: (0, first + c, 0, 0)),
+        ]
         + [pl.BlockSpec(memory_space=pl.ANY)] * len(chained),
         out_specs=pl.BlockSpec((owners, 1, rows, wide), lambda c: (0, offset + c, 0, 0)),
         out_shape=jax.ShapeDtypeStruct((owners, total, rows, wide), jnp.bfloat16),
-        input_output_aliases={1: 0} if chained else {},
+        input_output_aliases={2: 0} if chained else {},
         compiler_params=params(),
         cost_estimate=scan_cost(count, owners * rows, heads),
         name="column_scan",
-    )(pack, *chained)
+    )(pack, spare, *chained)
 
 
 def row_kernel(rows, heads, counts, *refs):
-    packs, out_ref, held = refs[:-2], refs[-2], refs[-1]
+    packs, spares = refs[: len(counts)], refs[len(counts) : -2]
+    out_ref, held = refs[-2:]
     image, row = pl.program_id(0), pl.program_id(1)
     wide = heads * HEAD_DIM
     tall = held.shape[1] // PARTS
     length = held.shape[1] // rows
-    units = [(pack, k) for pack, count in zip(packs, counts) for k in range(count)]
-
-    for u, (pack, k) in enumerate(units):
+    units = [
+        (pack, spare, k) for pack, spare, count in zip(packs, spares, counts) for k in range(count)
+    ]
+
+    for u, (pack, spare, k) in enumerate(units):
 
         @pl.when((row == 0) & (image == u // PARTS))
-        def _(pack=pack, k=k, part=u % PARTS):
+        def _(pack=pack, spare=spare, k=k, part=u % PARTS):
             depth = tall // pack.shape[0]
-            for lane in range(pack.shape[2] // LANES):
-                block = pack[:, k * depth : (k + 1) * depth, lane * LANES : (lane + 1) * LANES]
+            lanes = pack.shape[2] // LANES
+            here = slice(k * depth, (k + 1) * depth)
+            for lane in range(lanes + 1):
+                if lane < lanes:
+                    block = pack[:, here, lane * LANES : (lane + 1) * LANES]
+                else:
+                    block = spare[:, here, :]
                 held[lane, part * tall : (part + 1) * tall, :] = block.reshape(
                     tall, LANES
                 ).astype(jnp.float32)
@@ -360,29 +384,28 @@
     scan_sequence(
         length,
         heads,
-        take(first).astype(jnp.bfloat16),
+        *both_maps(take(first), take(first + 2)),
         take(first + 1).astype(jnp.bfloat16),
-        take(first + 2).astype(jnp.bfloat16),
         take,
         store,
     )
 
 
-def row_scan(packs, counts, images, rows, columns, heads):
+def row_scan(packs, spares, counts, images, rows, columns, heads):
     packed = packs[0].shape[2]
     total = rows * columns
     wide = heads * HEAD_DIM
     return pl.pallas_call(
         functools.partial(row_kernel, rows, heads, counts),
         grid=(images, rows),
-        in_specs=[resident(pack.shape, lambda i, r: (0, 0, 0)) for pack in packs],
+        in_specs=[resident(pack.shape, lambda i, r: (0, 0, 0)) for pack in packs + spares],
         out_specs=pl.BlockSpec((wide // LANES, total, LANES), lambda i, r: (0, i, 0)),
         out_shape=jax.ShapeDtypeStruct((wide // LANES, images * total, LANES), jnp.float32),
-        scratch_shapes=[pltpu.VMEM((packed // LANES, total, LANES), jnp.float32)],
+        scratch_shapes=[pltpu.VMEM((packed // LANES + 1, total, LANES), jnp.float32)],
         compiler_params=params(),
         cost_estimate=scan_cost(images * rows, columns, heads),
         name="row_scan",
-    )(*packs)
+    )(*packs, *spares)
 
 
 def output_kernel(t_ref, row_ref, col_ref, inner_ref, skip_ref, gain_ref, w_own, w_other, own_ref, send_ref):
@@ -501,29 +524,32 @@
     per_unit = columns // PARTS // owners
     there = groups_of((1, units // 2 - 1, units - units // 2))
     back = groups_of((units // 2, units // 4, units - units // 2 - units // 4))
-    own, other, packs, arrived = [], [], [], []
+    own, other, packs, spares, arrived, halves = [], [], [], [], [], []
     for start, count in there:
         own.append(turn(tokens, start, count))
     for g in range(len(there)):
         other.append(lax.ppermute(own[g], "tensor", swap))
     inner = None
     for g, (start, count) in enumerate(there):
-        inner, pack = project(
+        inner, pack, spare = project(
             own[g], other[g], in_gain, w_inner, w_small, bias, rate, place, heads, owners,
             start, count, units, inner,
         )
         packs.append(pack)
+        spares.append(spare)
         block = lax.all_to_all(pack, "space", split_axis=0, concat_axis=0, tiled=True)
         arrived.append(block.reshape(owners, count * per_unit, rows, pack.shape[2]))
+        half = lax.ppermute(block[:, :, wide : wide + STATE], "tensor", swap)
+        halves.append(half.reshape(owners, count * per_unit, rows, STATE))
     counts = tuple(count for _, count in there)
-    row_out = row_scan(packs, counts, images, rows, columns, heads)
+    row_out = row_scan(packs, spares, counts, images, rows, columns, heads)
     columns_out = [None] * len(back)
     for g, (start, count) in enumerate(there):
         for k, (low, size) in enumerate(back):
             first, last = max(start, low), min(start + count, low + size)
             if first < last:
                 columns_out[k] = column_scan(
-                    arrived[g], heads, (first - start) * per_unit, (last - first) * per_unit,
+                    arrived[g], halves[g], heads, (first - start) * per_unit, (last - first) * per_unit,
                     (first - low) * per_unit, size * per_unit, columns_out[k],
                 )
     result = None

time: 569 us -> 558 us (0.981)
  waiting for transfers between devices: 256 us -> 246 us
  blocking collectives: 93.7 us -> 87 us
    all_to_all x2, waiting for transfers between devices: 48.7 us -> 34.9 us  [pipelined(): lax.all_to_all(pack, 'space', split_axis=0, concat_axis=0, tiled=True)]
    ppermute x0 -> x3, waiting for transfers between devices: none -> 12.8 us  [pipelined(): half = lax.ppermute(block[:, :, wide:wide + STATE], 'tensor', swap)]
    all_to_all x3, waiting for transfers between devices: 69.8 us -> 59.8 us  [pipelined(): lax.all_to_all(block, 'space', split_axis=0, concat_axis=0, tiled=True)]
    all_to_all x1, blocking collectives: 93.7 us -> 87 us  [pipelined(): lax.all_to_all(pack, 'space', split_axis=0, concat_axis=0, tiled=True)]
  transfers between devices with their start and end apart: 11 -> 14, of which waited for: 7 -> 9; matrix products, arithmetic and copies ran while one was open for 1% -> 1% of each run, Pallas kernels for 25% -> 26%
where the time goes in v4:
time: 558 us; the launch traced here: 557 us
  waiting for transfers between devices  246 us (44%)
  Pallas kernels  151 us (27%)
  blocking collectives  87 us (16%)
  starting transfers between devices  62.1 us (11%)
  local copies, waits for them, and re-layouts  9.62 us (2%)
    all_to_all x1, blocking collectives, pipelined(): lax.all_to_all(pack, 'space', split_axis=0, concat_axis=0, tiled=True)  87 us
    ppermute x3, waiting for transfers between devices, pipelined(): other.append(lax.ppermute(own[g], 'tensor', swap))  79.4 us
    all_to_all x3, waiting for transfers between devices, pipelined(): lax.all_to_all(block, 'space', split_axis=0, concat_axis=0, tiled=True)  59.8 us
    ppermute x3, waiting for transfers between devices, pipelined(): got = lax.ppermute(send, 'tensor', swap)  59.1 us
    all_to_all x3, starting transfers between devices, pipelined(): lax.all_to_all(block, 'space', split_axis=0, concat_axis=0, tiled=True)  38.5 us
    pallas_call x3, Pallas kernels, project(): pl.pallas_call(functools.partial(project_kernel, 2 * feats, heads), grid_...  36.4 us
    all_to_all x2, waiting for transfers between devices, pipelined(): lax.all_to_all(pack, 'space', split_axis=0, concat_axis=0, tiled=True)  34.9 us
    pallas_call x3, Pallas kernels, output(): pl.pallas_call(output_kernel, grid_spec=pltpu.PrefetchScalarGridSpec(num_...  31.3 us
  transfers between devices with their start and end apart: 14, of which 9 were waited for; matrix products, arithmetic and copies ran while one was open for 1% of the time, Pallas kernels for 26%

profile of v4, /device:TPU:0, one launch (start us, length us, event | category | flops | bytes accessed | tf_op | source)
XLA Modules:
  0.0 557.2 jit_solution(9987145526090395978)
XLA Ops:
  0.0 4.3 turn.4.own_ref
  4.3 3.0 collective-permute-start.1
  7.3 4.8 turn.5.own_ref
  12.1 0.1 collective-permute-start.2
  12.2 2.5 turn.3.own_ref
  14.6 1.9 collective-permute-start
  16.5 0.3 copy.17
  16.8 0.6 pad_bitcast_fusion
  17.4 1.3 fusion.1
  18.8 79.4 %collective-permute-done.other_ref = bf16[256,1024]{1,0:T(8,128)(2,1)} collective-permute-done((bf16[256,1024]{1,0:T(8,128)(2,1)}, bf16[256,1024]{1,0:T(8,128)(2,1)}, u32[]{:S(2)}, u32[]{:S(2)}) %collective-permute-start) | collective-permute-done | bytes 524320 | tf_op jit(solution)/shard_map/ppermute | solution.py:531
  98.2 7.5 %project.3 = (bf16[2048,1536]{1,0:T(8,128)(2,1)}, bf16[16,16,1792]{2,1,0:T(8,128)(2,1)}, bf16[16,16,128]{2,1,0:T(8,128)(2,1)}) custom-call(s32[1]{0:T(128)} %bitcast.t_ref, bf16[256,1024]{1,0:T(8,128)(2,1)} %turn.3.own_ref, bf16[256,1024]{1,0:T(8,128)(2,1)} %collective-permute-done.other_ref, f32[2,1,1024]{2,1,0:T(1,128)} %bitcast.37, ...), custom_call_target="tpu_custom_call" | custom-call | flops 1879048192 | bytes 20971520 | tf_op jit(solution)/shard_map/project/pallas_call | solution.py:217
  105.7 6.1 %all-to-all-start.4 = ((bf16[16,16,1792]{2,1,0:T(8,128)(2,1)}), bf16[16,16,1792]{2,1,0:T(8,128)(2,1)S(1)}, u32[]{:S(2)}, u32[]{:S(2)}) async-start(bf16[16,16,1792]{2,1,0:T(8,128)(2,1)} %get-tuple-element.20.refs_0_), calls=%async_computation.4 | async-start | bytes 1835008 | tf_op jit(solution)/shard_map/all_to_all | solution.py:540
  111.9 0.0 collective-permute-done.1.other_ref
  111.9 0.0 copy-start.4
  111.9 1.1 copy-done.4
  113.0 13.0 %project.4 = (bf16[2048,1536]{1,0:T(8,128)(2,1)}, bf16[16,48,1792]{2,1,0:T(8,128)(2,1)}, bf16[16,48,128]{2,1,0:T(8,128)(2,1)}) custom-call(s32[1]{0:T(128)} %bitcast.t_ref, bf16[768,1024]{1,0:T(8,128)(2,1)} %turn.4.own_ref, bf16[768,1024]{1,0:T(8,128)(2,1)} %copy-done.4, f32[2,1,1024]{2,1,0:T(1,128)} %bitcast.39, ...), custom_call_target="tpu_custom_call", output_to_operand_aliasing={{0}: (11, {})} | custom-call | flops 5637144576 | bytes 20971520 | tf_op jit(solution)/shard_map/project/pallas_call | solution.py:217
  126.0 0.0 collective-permute-done.2.other_ref
  126.0 15.8 %project.5 = (bf16[2048,1536]{1,0:T(8,128)(2,1)}, bf16[16,64,1792]{2,1,0:T(8,128)(2,1)}, bf16[16,64,128]{2,1,0:T(8,128)(2,1)}) custom-call(s32[1]{0:T(128)} %bitcast.t_ref, bf16[1024,1024]{1,0:T(8,128)(2,1)} %turn.5.own_ref, bf16[1024,1024]{1,0:T(8,128)(2,1)} %collective-permute-done.2.other_ref, ...), custom_call_target="tpu_custom_call", output_to_operand_aliasing={{0}: (11, {})} | custom-call | flops 7516192768 | bytes 20971520 | tf_op jit(solution)/shard_map/project/pallas_call | solution.py:217
  141.9 0.0 all-to-all-done.4
  141.9 87.0 %all_to_all.30 = bf16[16,64,1792]{2,1,0:T(8,128)(2,1)} all-to-all(bf16[16,64,1792]{2,1,0:T(8,128)(2,1)} %get-tuple-element.24.refs_2_), channel_id=1, replica_groups=mesh['space'=16,'tensor'=2] {'space'}, dimensions={0} | all-to-all | bytes 7340032 | tf_op jit(solution)/shard_map/all_to_all | solution.py:540
  228.9 5.3 all-to-all-start.3
  234.1 1.0 slice.12
  235.1 1.6 collective-permute-start.3
  236.7 7.1 %collective-permute-done.3 = bf16[16,64,128]{2,1,0:T(8,128)(2,1)S(1)} collective-permute-done((bf16[16,64,128]{2,1,0:T(8,128)(2,1)S(1)}, bf16[16,64,128]{2,1,0:T(8,128)(2,1)S(1)}, u32[]{:S(2)}, u32[]{:S(2)}) %collective-permute-start.3) | collective-permute-done | bytes 262176 | tf_op jit(solution)/shard_map/ppermute | solution.py:542
  243.8 0.7 copy-done.14
  244.5 7.1 %column_scan.5 = bf16[16,4,8,1536]{3,2,1,0:T(8,128)(2,1)} custom-call(bf16[16,8,8,1792]{3,2,1,0:T(8,128)(2,1)} %bitcast.31, bf16[16,8,8,128]{3,2,1,0:T(8,128)(2,1)} %bitcast.44), custom_call_target="tpu_custom_call" | custom-call | flops 1610612736 | bytes 4718592 | tf_op jit(solution)/shard_map/column_scan/pallas_call | solution.py:333
  251.6 34.9 %all-to-all-done.3 = bf16[16,48,1792]{2,1,0:T(8,128)(2,1)S(1)} async-done(((bf16[16,48,1792]{2,1,0:T(8,128)(2,1)}), bf16[16,48,1792]{2,1,0:T(8,128)(2,1)S(1)}, u32[]{:S(2)}, u32[]{:S(2)}) %all-to-all-start.3) | async-done | bytes 2752544 | tf_op jit(solution)/shard_map/all_to_all | solution.py:540
  286.5 13.9 %all-to-all-start.2 = ((bf16[16,32,1536]{2,1,0:T(8,128)(2,1)}), bf16[16,32,1536]{2,1,0:T(8,128)(2,1)}, u32[]{:S(2)}, u32[]{:S(2)}) async-start(bf16[16,32,1536]{2,1,0:T(8,128)(2,1)} %bitcast.35), calls=%async_computation.2 | async-start | bytes 3145728 | tf_op jit(solution)/shard_map/all_to_all | solution.py:558
  300.5 1.6 collective-permute-start.6
  302.1 0.8 slice.14
  302.9 0.5 collective-permute-start.7
  303.4 5.7 %collective-permute-done.7 = bf16[16,16,128]{2,1,0:T(8,128)(2,1)S(1)} collective-permute-done((bf16[16,16,128]{2,1,0:T(8,128)(2,1)S(1)}, bf16[16,16,128]{2,1,0:T(8,128)(2,1)S(1)}, u32[]{:S(2)}, u32[]{:S(2)}) %collective-permute-start.7) | collective-permute-done | bytes 65568 | tf_op jit(solution)/shard_map/ppermute | solution.py:542
  309.1 0.6 copy-done.9
  309.7 4.4 column_scan.6.rest_0_
  314.1 0.0 collective-permute-done.6
  314.2 0.7 copy-done.7
  314.8 9.8 %column_scan.7 = bf16[16,8,8,1536]{3,2,1,0:T(8,128)(2,1)} custom-call(bf16[16,6,8,1792]{3,2,1,0:T(8,128)(2,1)} %bitcast.30, bf16[16,6,8,128]{3,2,1,0:T(8,128)(2,1)} %bitcast.36, bf16[16,8,8,1536]{3,2,1,0:T(8,128)(2,1)} %column_scan.6.rest_0_), custom_call_target="tpu_custom_call", output_to_operand_aliasing={{}: (2, {})} | custom-call | flops 2415919104 | bytes 7077888 | tf_op jit(solution)/shard_map/column_scan/pallas_call | solution.py:333
  324.6 7.7 %all-to-all-done.2.col_ref = bf16[16,32,1536]{2,1,0:T(8,128)(2,1)} async-done(((bf16[16,32,1536]{2,1,0:T(8,128)(2,1)}), bf16[16,32,1536]{2,1,0:T(8,128)(2,1)}, u32[]{:S(2)}, u32[]{:S(2)}) %all-to-all-start.2) | async-done | bytes 1572896 | tf_op jit(solution)/shard_map/all_to_all | solution.py:558
  332.3 9.1 %all-to-all-start.5 = ((bf16[16,64,1536]{2,1,0:T(8,128)(2,1)}), bf16[16,64,1536]{2,1,0:T(8,128)(2,1)S(1)}, u32[]{:S(2)}, u32[]{:S(2)}) async-start(bf16[16,64,1536]{2,1,0:T(8,128)(2,1)} %bitcast.29), calls=%async_computation.5 | async-start | bytes 6291456 | tf_op jit(solution)/shard_map/all_to_all | solution.py:558
  341.4 0.0 copy-start.11
  341.5 0.0 copy-start.10
  341.5 7.1 %column_scan.4 = bf16[16,4,8,1536]{3,2,1,0:T(8,128)(2,1)} custom-call(bf16[16,8,8,1792]{3,2,1,0:T(8,128)(2,1)} %bitcast.32, bf16[16,8,8,128]{3,2,1,0:T(8,128)(2,1)} %bitcast.45), custom_call_target="tpu_custom_call" | custom-call | flops 1610612736 | bytes 4718592 | tf_op jit(solution)/shard_map/column_scan/pallas_call | solution.py:333
  348.6 52.1 %all-to-all-done.5.col_ref = bf16[16,64,1536]{2,1,0:T(8,128)(2,1)S(1)} async-done(((bf16[16,64,1536]{2,1,0:T(8,128)(2,1)}), bf16[16,64,1536]{2,1,0:T(8,128)(2,1)S(1)}, u32[]{:S(2)}, u32[]{:S(2)}) %all-to-all-start.5) | async-done | bytes 3145760 | tf_op jit(solution)/shard_map/all_to_all | solution.py:558
  400.7 15.5 %all-to-all-start.1 = ((bf16[16,32,1536]{2,1,0:T(8,128)(2,1)}), bf16[16,32,1536]{2,1,0:T(8,128)(2,1)}, u32[]{:S(2)}, u32[]{:S(2)}) async-start(bf16[16,32,1536]{2,1,0:T(8,128)(2,1)} %bitcast.34), calls=%async_computation.1 | async-start | bytes 3145728 | tf_op jit(solution)/shard_map/all_to_all | solution.py:558
  416.2 0.0 copy-done.11
  416.2 0.1 broadcast_in_dim.3
  416.2 0.7 reshape_reshape.3.skip_ref
  416.9 0.6 reshape.63.gain_ref
  417.5 29.5 %row_scan.1.row_ref = f32[12,2048,128]{2,1,0:T(8,128)} custom-call(bf16[16,16,1792]{2,1,0:T(8,128)(2,1)} %get-tuple-element.20.refs_0_, bf16[16,48,1792]{2,1,0:T(8,128)(2,1)} %get-tuple-element.22.refs_1_, bf16[16,64,1792]{2,1,0:T(8,128)(2,1)} %get-tuple-element.24.refs_2_, bf16[16,16,128]{2,1,0:T(8,128)(2,1)} %get-tuple-element.25.refs_3_, ...), custom_call_target="tpu_custom_call" | custom-call | flops 6442450944 | bytes 18874368 | tf_op jit(solution)/shard_map/row_scan/pallas_call | solution.py:398
  447.0 13.4 %output.5 = (f32[1024,1024]{1,0:T(8,128)}, bf16[1024,1024]{1,0:T(8,128)(2,1)}) custom-call(s32[1]{0:T(128)} %bitcast.t_ref, f32[12,2048,128]{2,1,0:T(8,128)} %row_scan.1.row_ref, bf16[16,64,1536]{2,1,0:T(8,128)(2,1)} %copy-done, bf16[2048,1536]{1,0:T(8,128)(2,1)} %get-tuple-element.28.inner_ref, f32[1,1536]{1,0:T(1,128)} %reshape_reshape.3.skip_ref, ...), custom_call_target="tpu_custom_call" | custom-call | flops 6442450944 | bytes 16777216 | tf_op jit(solution)/shard_map/output/pallas_call | solution.py:447
  460.3 1.5 collective-permute-start.8
  461.9 9.0 %output.4 = (f32[512,1024]{1,0:T(8,128)}, bf16[512,1024]{1,0:T(8,128)(2,1)}) custom-call(s32[1]{0:T(128)} %bitcast.t_ref, f32[12,2048,128]{2,1,0:T(8,128)} %row_scan.1.row_ref, bf16[16,32,1536]{2,1,0:T(8,128)(2,1)} %all-to-all-done.2.col_ref, bf16[2048,1536]{1,0:T(8,128)(2,1)} %get-tuple-element.28.inner_ref, f32[1,1536]{1,0:T(1,128)} %reshape_reshape.3.skip_ref, ...), custom_call_target="tpu_custom_call" | custom-call | flops 3221225472 | bytes 16777216 | tf_op jit(solution)/shard_map/output/pallas_call | solution.py:447
  470.9 0.5 collective-permute-start.5
  471.4 0.0 all-to-all-done.1.col_ref
  471.4 9.0 %output.3 = (f32[512,1024]{1,0:T(8,128)}, bf16[512,1024]{1,0:T(8,128)(2,1)}) custom-call(s32[1]{0:T(128)} %bitcast.t_ref, f32[12,2048,128]{2,1,0:T(8,128)} %row_scan.1.row_ref, bf16[16,32,1536]{2,1,0:T(8,128)(2,1)} %all-to-all-done.1.col_ref, bf16[2048,1536]{1,0:T(8,128)(2,1)} %get-tuple-element.28.inner_ref, f32[1,1536]{1,0:T(1,128)} %reshape_reshape.3.skip_ref, ...), custom_call_target="tpu_custom_call" | custom-call | flops 3221225472 | bytes 16777216 | tf_op jit(solution)/shard_map/output/pallas_call | solution.py:447
  480.4 1.5 collective-permute-start.4
  481.9 27.2 %collective-permute-done.8.got_ref = bf16[1024,1024]{1,0:T(8,128)(2,1)S(1)} collective-permute-done((bf16[1024,1024]{1,0:T(8,128)(2,1)}, bf16[1024,1024]{1,0:T(8,128)(2,1)S(1)}, u32[]{:S(2)}, u32[]{:S(2)}) %collective-permute-start.8) | collective-permute-done | bytes 2097184 | tf_op jit(solution)/shard_map/ppermute | solution.py:560
  509.1 1.4 copy-done.3
  510.4 6.4 %finish.3.rest_0_ = bf16[2,8,128,1024]{3,2,1,0:T(8,128)(2,1)} custom-call(f32[1024,1024]{1,0:T(8,128)} %get-tuple-element.33.own_ref, bf16[1024,1024]{1,0:T(8,128)(2,1)} %copy-done.3, f32[2,8,128,1024]{3,2,1,0:T(8,128)} %tok_ref.11), custom_call_target="tpu_custom_call" | custom-call | bytes 12582912 | tf_op jit(solution)/shard_map/finish/pallas_call | solution.py:492
  516.8 14.7 %collective-permute-done.5.got_ref = bf16[512,1024]{1,0:T(8,128)(2,1)S(1)} collective-permute-done((bf16[512,1024]{1,0:T(8,128)(2,1)}, bf16[512,1024]{1,0:T(8,128)(2,1)S(1)}, u32[]{:S(2)}, u32[]{:S(2)}) %collective-permute-start.5) | collective-permute-done | bytes 1048608 | tf_op jit(solution)/shard_map/ppermute | solution.py:560
  531.5 1.0 copy-done.6
  532.6 3.7 finish.4.rest_0_
  536.3 17.2 %collective-permute-done.4.got_ref = bf16[512,1024]{1,0:T(8,128)(2,1)} collective-permute-done((bf16[512,1024]{1,0:T(8,128)(2,1)}, bf16[512,1024]{1,0:T(8,128)(2,1)}, u32[]{:S(2)}, u32[]{:S(2)}) %collective-permute-start.4) | collective-permute-done | bytes 1048608 | tf_op jit(solution)/shard_map/ppermute | solution.py:560
  553.5 3.7 finish.5
  (21 shorter events, 0.1 us)
Async XLA Ops:
  4.3 107.6 %collective-permute-start.1 = (bf16[768,1024]{1,0:T(8,128)(2,1)}, bf16[768,1024]{1,0:T(8,128)(2,1)S(1)}, u32[]{:S(2)}, u32[]{:S(2)}) collective-permute-start(bf16[768,1024]{1,0:T(8,128)(2,1)} %turn.4.own_ref), channel_id=1, source_target_pairs={{0,1},{1,0},{2,3},{3,2},{4,5},{5,4},{6,7},{7,6},{8,9},{9,8},{10,11... | collective-permute-start | bytes 4718600 | tf_op jit(solution)/shard_map/ppermute | solution.py:531
  12.1 4.5 copy-start.8
  12.1 4.7 copy-start.12
  12.1 4.7 copy-start.13
  12.1 5.4 copy-start.5
  12.1 113.9 %collective-permute-start.2 = (bf16[1024,1024]{1,0:T(8,128)(2,1)}, bf16[1024,1024]{1,0:T(8,128)(2,1)}, u32[]{:S(2)}, u32[]{:S(2)}) collective-permute-start(bf16[1024,1024]{1,0:T(8,128)(2,1)} %turn.5.own_ref), channel_id=1, source_target_pairs={{0,1},{1,0},{2,3},{3,2},{4,5},{5,4},{6,7},{7,6},{8,9},{9,8},{10,11... | collective-permute-start | bytes 6291464 | tf_op jit(solution)/shard_map/ppermute | solution.py:531
  14.6 83.5 %collective-permute-start = (bf16[256,1024]{1,0:T(8,128)(2,1)}, bf16[256,1024]{1,0:T(8,128)(2,1)}, u32[]{:S(2)}, u32[]{:S(2)}) collective-permute-start(bf16[256,1024]{1,0:T(8,128)(2,1)} %turn.3.own_ref), channel_id=1, source_target_pairs={{0,1},{1,0},{2,3},{3,2},{4,5},{5,4},{6,7},{7,6},{8,9},{9,8},{10,11... | collective-permute-start | bytes 1572872 | tf_op jit(solution)/shard_map/ppermute | solution.py:531
  105.7 36.2 %all-to-all-start.4 = ((bf16[16,16,1792]{2,1,0:T(8,128)(2,1)}), bf16[16,16,1792]{2,1,0:T(8,128)(2,1)S(1)}, u32[]{:S(2)}, u32[]{:S(2)}) async-start(bf16[16,16,1792]{2,1,0:T(8,128)(2,1)} %get-tuple-element.20.refs_0_), calls=%async_computation.4 | async-start | bytes 1835008 | tf_op jit(solution)/shard_map/all_to_all | solution.py:540
  111.9 1.1 copy-start.4
  141.9 87.0 %copy-start.2 = (bf16[16,16,1792]{2,1,0:T(8,128)(2,1)}, bf16[16,16,1792]{2,1,0:T(8,128)(2,1)S(1)}, u32[]{:S(2)}) copy-start(bf16[16,16,1792]{2,1,0:T(8,128)(2,1)S(1)} %all-to-all-done.4) | copy-start | bytes 2752516
  228.9 57.6 %all-to-all-start.3 = ((bf16[16,48,1792]{2,1,0:T(8,128)(2,1)}), bf16[16,48,1792]{2,1,0:T(8,128)(2,1)S(1)}, u32[]{:S(2)}, u32[]{:S(2)}) async-start(bf16[16,48,1792]{2,1,0:T(8,128)(2,1)} %get-tuple-element.22.refs_1_), calls=%async_computation.3 | async-start | bytes 5505024 | tf_op jit(solution)/shard_map/all_to_all | solution.py:540
  235.1 8.7 %collective-permute-start.3 = (bf16[16,64,128]{2,1,0:T(8,128)(2,1)S(1)}, bf16[16,64,128]{2,1,0:T(8,128)(2,1)S(1)}, u32[]{:S(2)}, u32[]{:S(2)}) collective-permute-start(bf16[16,64,128]{2,1,0:T(8,128)(2,1)S(1)} %slice.12), channel_id=1, source_target_pairs={{0,1},{1,0},{2,3},{3,2},{4,5},{5,4},{6,7},{7,6},{8,9},{9,8},{10,11... | collective-permute-start | bytes 786440 | tf_op jit(solution)/shard_map/ppermute | solution.py:542
  243.8 0.7 copy-start.14
  286.5 27.6 %copy-start.1 = (bf16[16,48,1792]{2,1,0:T(8,128)(2,1)}, bf16[16,48,1792]{2,1,0:T(8,128)(2,1)S(1)}, u32[]{:S(2)}) copy-start(bf16[16,48,1792]{2,1,0:T(8,128)(2,1)S(1)} %all-to-all-done.3) | copy-start | bytes 8257540
  286.5 45.8 %all-to-all-start.2 = ((bf16[16,32,1536]{2,1,0:T(8,128)(2,1)}), bf16[16,32,1536]{2,1,0:T(8,128)(2,1)}, u32[]{:S(2)}, u32[]{:S(2)}) async-start(bf16[16,32,1536]{2,1,0:T(8,128)(2,1)} %bitcast.35), calls=%async_computation.2 | async-start | bytes 3145728 | tf_op jit(solution)/shard_map/all_to_all | solution.py:558
  300.5 13.7 %collective-permute-start.6 = (bf16[16,48,128]{2,1,0:T(8,128)(2,1)S(1)}, bf16[16,48,128]{2,1,0:T(8,128)(2,1)S(1)}, u32[]{:S(2)}, u32[]{:S(2)}) collective-permute-start(bf16[16,48,128]{2,1,0:T(8,128)(2,1)S(1)} %slice.13), channel_id=1, source_target_pairs={{0,1},{1,0},{2,3},{3,2},{4,5},{5,4},{6,7},{7,6},{8,9},{9,8},{10,11... | collective-permute-start | bytes 589832 | tf_op jit(solution)/shard_map/ppermute | solution.py:542
  302.9 6.2 %collective-permute-start.7 = (bf16[16,16,128]{2,1,0:T(8,128)(2,1)S(1)}, bf16[16,16,128]{2,1,0:T(8,128)(2,1)S(1)}, u32[]{:S(2)}, u32[]{:S(2)}) collective-permute-start(bf16[16,16,128]{2,1,0:T(8,128)(2,1)S(1)} %slice.14), channel_id=1, source_target_pairs={{0,1},{1,0},{2,3},{3,2},{4,5},{5,4},{6,7},{7,6},{8,9},{9,8},{10,11... | collective-permute-start | bytes 196616 | tf_op jit(solution)/shard_map/ppermute | solution.py:542
  309.1 0.6 copy-start.9
  314.2 0.7 copy-start.7
  332.3 68.3 %all-to-all-start.5 = ((bf16[16,64,1536]{2,1,0:T(8,128)(2,1)}), bf16[16,64,1536]{2,1,0:T(8,128)(2,1)S(1)}, u32[]{:S(2)}, u32[]{:S(2)}) async-start(bf16[16,64,1536]{2,1,0:T(8,128)(2,1)} %bitcast.29), calls=%async_computation.5 | async-start | bytes 6291456 | tf_op jit(solution)/shard_map/all_to_all | solution.py:558
  341.4 74.7 %copy-start.11 = (f32[24]{0:T(128)S(1)}, f32[24]{0:T(128)}, u32[]{:S(2)}) copy-start(f32[24]{0:T(128)} %param.17) | copy-start | bytes 292
  341.5 75.5 %copy-start.10 = (f32[1536]{0:T(1024)S(1)}, f32[1536]{0:T(1024)}, u32[]{:S(2)}) copy-start(f32[1536]{0:T(1024)} %param.18) | copy-start | bytes 18436
  400.7 46.3 %copy-start = (bf16[16,64,1536]{2,1,0:T(8,128)(2,1)}, bf16[16,64,1536]{2,1,0:T(8,128)(2,1)S(1)}, u32[]{:S(2)}) copy-start(bf16[16,64,1536]{2,1,0:T(8,128)(2,1)S(1)} %all-to-all-done.5.col_ref) | copy-start | bytes 9437188
  400.7 70.7 %all-to-all-start.1 = ((bf16[16,32,1536]{2,1,0:T(8,128)(2,1)}), bf16[16,32,1536]{2,1,0:T(8,128)(2,1)}, u32[]{:S(2)}, u32[]{:S(2)}) async-start(bf16[16,32,1536]{2,1,0:T(8,128)(2,1)} %bitcast.34), calls=%async_computation.1 | async-start | bytes 3145728 | tf_op jit(solution)/shard_map/all_to_all | solution.py:558
  460.3 48.7 %collective-permute-start.8 = (bf16[1024,1024]{1,0:T(8,128)(2,1)}, bf16[1024,1024]{1,0:T(8,128)(2,1)S(1)}, u32[]{:S(2)}, u32[]{:S(2)}) collective-permute-start(bf16[1024,1024]{1,0:T(8,128)(2,1)} %get-tuple-element.34), channel_id=1, source_target_pairs={{0,1},{1,0},{2,3},{3,2},{4,5},{5,4},{6,7},{7,6},{8,9},{9,8},{10,11... | collective-permute-start | bytes 6291464 | tf_op jit(solution)/shard_map/ppermute | solution.py:560
  470.9 60.6 %collective-permute-start.5 = (bf16[512,1024]{1,0:T(8,128)(2,1)}, bf16[512,1024]{1,0:T(8,128)(2,1)S(1)}, u32[]{:S(2)}, u32[]{:S(2)}) collective-permute-start(bf16[512,1024]{1,0:T(8,128)(2,1)} %get-tuple-element.32), channel_id=1, source_target_pairs={{0,1},{1,0},{2,3},{3,2},{4,5},{5,4},{6,7},{7,6},{8,9},{9,8},{10,11... | collective-permute-start | bytes 3145736 | tf_op jit(solution)/shard_map/ppermute | solution.py:560
  480.4 73.1 %collective-permute-start.4 = (bf16[512,1024]{1,0:T(8,128)(2,1)}, bf16[512,1024]{1,0:T(8,128)(2,1)}, u32[]{:S(2)}, u32[]{:S(2)}) collective-permute-start(bf16[512,1024]{1,0:T(8,128)(2,1)} %get-tuple-element.30), channel_id=1, source_target_pairs={{0,1},{1,0},{2,3},{3,2},{4,5},{5,4},{6,7},{7,6},{8,9},{9,8},{10,11... | collective-permute-start | bytes 3145736 | tf_op jit(solution)/shard_map/ppermute | solution.py:560
  509.1 1.4 copy-start.3
  531.5 1.0 copy-start.6
